TPU v7x, 128 devices: a whole 4x4x4 slice. The times are simulated.
128 devices in a mesh: rows: 16 (over x, z), cols: 8 (over y, core).
Axes of the slice: x: 4, y: 4, z: 4, core: 2. Of those that a mesh axis runs over, the one named last changes fastest.
Arguments:
- band: float32 [16, 8, 1024, 1024], P('rows', 'cols'), may hold values from -6 to 6
- diag: float32 [8, 1024, 1024], P('cols', 'rows'), as said below
- row_factors: bfloat16 [16, 8, 2, 1024, 256], P('rows', 'cols'), as said below
- row_ranks: int32 [16, 8], P('rows', 'cols'), may hold values from 32 to 256
- col_factors: bfloat16 [8, 8, 2, 1024, 256], P(None, 'cols', None, 'rows'), as said below
- col_ranks: int32 [8, 8], replicated, may hold values from 32 to 256
Outputs:
- band_out: float32 [16, 8, 1024, 1024], P('rows', 'cols')
- diag_out: float32 [8, 1024, 1024], P('cols', 'rows')
Inputs may be any that keep to these rules, and one draw needn't show every extreme that they name: `diag`: every new_diag[c] is symmetric positive definite. `row_factors`: columns of a factor beyond its rank hold arbitrary values. `col_factors`: columns of a factor beyond its rank hold arbitrary values.
All inputs are finite; a program needn't handle non-finite values.
Results may differ from a plain program's by a relative error of at most 0.002.
Values may be sent and summed in bfloat16 or wider, within the bound.
No kernel may reach another device: no remote copies, remote signals or barrier semaphores. Data moves between devices by JAX's collectives and lax.ppermute only.
A program may use at most 128 MiB of HBM per device.

v0:
```python
import jax
import jax.numpy as jnp
from jax import lax
from jax.experimental import pallas as pl
from jax.experimental.pallas import tpu as pltpu
from jax.sharding import PartitionSpec as P


NB = 128
G = 8
SIDE = 4
AXES = ("rows", "cols")
COLUMN_GRANT = 46 << 20
TILE_GRANT = 60 << 20


def split2(x):
    hi = x.astype(jnp.bfloat16)
    lo = (x - hi.astype(jnp.float32)).astype(jnp.bfloat16)
    return hi, lo


def nt(a, b):
    return lax.dot_general(a, b, (((1,), (1,)), ((), ())), preferred_element_type=jnp.float32)


def nt3(ah, al, bh, bl):
    return nt(jnp.concatenate([ah, al, ah], axis=1), jnp.concatenate([bh, bh, bl], axis=1))


def lane_splat(x, lane):
    return jnp.broadcast_to(x[:, lane:lane + 1], x.shape)


def row_splat(x, s):
    return jnp.broadcast_to(x[s:s + 1, :], x.shape)


def factor_block(t_ref, up_ref, one_ref):
    one = one_ref[...]
    sub = lax.broadcasted_iota(jnp.int32, (G, NB), 0)
    lane = lax.broadcasted_iota(jnp.int32, (G, NB), 1)
    count = NB // G
    first = t_ref[0:G, :]
    diag = [lane_splat(first, c) * one for c in range(G)]
    for g in range(count):
        base = g * G
        v = t_ref[base:base + G, :]
        b = [[row_splat(diag[j], s) if s >= j else None for j in range(G)] for s in range(G)]
        more = g + 1 < count
        if more:
            below = t_ref[base + G:base + 2 * G, :]
            wn = [lane_splat(below, base + j) for j in range(G)]
            diag = [lane_splat(below, base + G + c) for c in range(G)]
        inside = (lane >= base) & (lane < base + G)
        vi = jnp.where(inside, jnp.where(lane - base == sub, 1.0, 0.0), v)
        low = [[None] * G for _ in range(G)]
        rinv = [None] * G
        ra = [row_splat(v, s) for s in range(G)]
        r = [row_splat(vi, s) for s in range(G)]
        for j in range(G):
            rinv[j] = lax.rsqrt(b[j][j])
            for s in range(j + 1, G):
                low[s][j] = b[s][j] * rinv[j]
            for t in range(j + 1, G):
                for s in range(t, G):
                    b[s][t] = b[s][t] - low[s][j] * low[t][j]
            if more:
                ln = wn[j] * rinv[j]
                for t in range(j + 1, G):
                    wn[t] = wn[t] - ln * low[t][j]
                for c in range(G):
                    diag[c] = diag[c] - ln * row_splat(ln, c)
            ra[j] = ra[j] * rinv[j]
            r[j] = r[j] * rinv[j]
            for s in range(j + 1, G):
                ra[s] = ra[s] - low[s][j] * ra[j]
                r[s] = r[s] - low[s][j] * r[j]
        out, outa = r[0], ra[0]
        for s in range(1, G):
            out = jnp.where(sub == s, r[s], out)
            outa = jnp.where(sub == s, ra[s], outa)
        up_ref[base:base + G, :] = outa
        t_ref[base:base + G, :] = out
        if more:
            m = [None] * G
            for s in reversed(range(G)):
                acc = r[s]
                for t in range(s + 1, G):
                    acc = acc - low[t][s] * m[t]
                m[s] = acc * rinv[s]
            for rb in range(g + 1, count):
                w = t_ref[rb * G:(rb + 1) * G, :]
                acc = jnp.where(inside, 0.0, w)
                for j in range(G):
                    acc = acc - lane_splat(w, base + j) * m[j]
                t_ref[rb * G:(rb + 1) * G, :] = acc


def chol_body(a_ref, inv_ref, t_ref, up_ref, one_ref, beside):
    n = a_ref.shape[0]
    nblk = n // NB
    ri = lax.broadcasted_iota(jnp.int32, (NB, NB), 0)
    ci = lax.broadcasted_iota(jnp.int32, (NB, NB), 1)

    def step(j, _):
        o = pl.multiple_of(j * NB, NB)
        t_ref[...] = a_ref[pl.ds(o, NB), pl.ds(o, NB)]
        factor_block(t_ref, up_ref, one_ref)
        beside(j)
        inv = jnp.where(ri >= ci, t_ref[...], 0.0)
        inv_ref[pl.ds(o, NB), :] = inv
        low = jnp.where(ri >= ci, up_ref[...].T, 0.0)
        ih, il = split2(inv)
        for v in range(nblk // 2):
            lo_row = 2 * NB * v

            @pl.when((j + 1) // 2 == v)
            def _():
                p = a_ref[lo_row:, pl.ds(o, NB)]
                ph, plo = split2(p)
                x = nt3(ph, plo, ih, il)
                rows = lax.broadcasted_iota(jnp.int32, x.shape, 0) + lo_row
                x = jnp.where(rows >= o + NB, x, 0.0)
                a_ref[lo_row:, pl.ds(o, NB)] = x
                xh, xl = split2(x)
                c = nt3(xh, xl, xh, xl)
                a_ref[lo_row:, lo_row:] = a_ref[lo_row:, lo_row:] - c
        a_ref[pl.ds(o, NB), pl.ds(o, NB)] = low
        return 0

    lax.fori_loop(0, nblk, step, 0)


def solve_body(b_ref, l_ref, inv_ref, x_ref, xh_ref, xl_ref, done):
    n = b_ref.shape[0]
    for j in range(n // (2 * NB)):
        o = 2 * NB * j
        s = slice(o, o + 2 * NB)
        i0, i1 = inv_ref[o:o + NB, :], inv_ref[o + NB:o + 2 * NB, :]
        i0h, i0l = split2(i0.T)
        i1h, i1l = split2(i1)
        mh, ml = split2(nt3(*split2(l_ref[o + NB:o + 2 * NB, o:o + NB]), i0h, i0l))
        off = -nt3(i1h, i1l, *split2(nt_same(mh, ml)))
        inv = jnp.concatenate([jnp.concatenate([i0, jnp.zeros_like(i0)], axis=1), jnp.concatenate([off, i1], axis=1)], axis=0)
        ih, il = split2(inv)
        acc = b_ref[:, s]
        if j:
            lh, ll = split2(l_ref[s, :o])
            acc = acc - nt(xh_ref[:, :o], lh) - nt(xl_ref[:, :o], lh) - nt(xh_ref[:, :o], ll)
        ah, al = split2(acc)
        x = nt3(ah, al, ih, il)
        x_ref[:, s] = x
        done(j, s)
        xh, xl = split2(x)
        xh_ref[:, s] = xh
        xl_ref[:, s] = xl


def nt_same(mh, ml):
    return (mh.astype(jnp.float32) + ml.astype(jnp.float32)).T


def tn(a, b):
    return lax.dot_general(a, b, (((0,), (0,)), ((), ())), preferred_element_type=jnp.float32)


def masked(core, rank_a, rank_b):
    kept = lax.broadcasted_iota(jnp.int32, core.shape, 1) < rank_b
    if rank_a is not None:
        kept = kept & (lax.broadcasted_iota(jnp.int32, core.shape, 0) < rank_a)
    return jnp.where(kept, core, 0.0).astype(jnp.bfloat16)


def started(pairs, sems, first=0):
    copies = [pltpu.make_async_copy(src, dst, sems.at[first + n]) for n, (src, dst) in enumerate(pairs)]
    for copy in copies:
        copy.start()
    return copies


def waited(copies):
    for copy in copies:
        copy.wait()


def slab_copies(meta, fs, gs, u_ref, v_ref, first, count, to=None):
    x, z = meta[1], meta[2]
    pairs = []
    for e in range(SIDE):
        for d in range(SIDE):
            slab = ((x + SIDE - d) % SIDE) * SIDE + (z + SIDE - e) % SIDE
            at = pl.ds(pl.multiple_of(slab * 64, 64), 64)
            pairs.append((fs[e].at[d, pl.ds(first, count)], v_ref.at[pl.ds(first if to is None else to, count), at, :]))
            pairs.append((gs[d].at[e, pl.ds(first, count)], u_ref.at[pl.ds(first if to is None else to, count), at, :]))
    return pairs


def row_copies(meta, rows, ru_ref, rv_ref):
    y, core_at = meta[0] // 2, meta[0] % 2
    pairs = []
    for e in range(SIDE):
        near = ((y + SIDE - e) % SIDE) * 2
        for src, k in ((rows[e], near + core_at), (rows[SIDE + e], near + 1 - core_at)):
            pairs.append((src.at[0], ru_ref.at[k]))
            pairs.append((src.at[1], rv_ref.at[k]))
    return pairs


def tile_panel(meta, k, tile_ref, u_ref, v_ref, ru_ref, rv_ref):
    n = tile_ref.shape[0]
    core = jnp.dot(rv_ref[k, 0:256], v_ref[k, 0:256], preferred_element_type=jnp.float32)
    for q in range(256, n, 256):
        core = core + jnp.dot(rv_ref[k, q:q + 256], v_ref[k, q:q + 256], preferred_element_type=jnp.float32)
    core = masked(core, None, meta[4 + k])
    left = jnp.dot(ru_ref[k], core, preferred_element_type=jnp.float32).astype(jnp.bfloat16)
    uk = u_ref[k]
    for s in range(0, n, 512):
        tile_ref[s:s + 512, :] = tile_ref[s:s + 512, :] - nt(left[s:s + 512], uk)


def column_kernel(meta, *refs):
    fs, gs, rows = refs[0:4], refs[4:8], refs[8:16]
    band_hbm, out_hbm, dout_hbm = refs[16:19]
    (u_ref, v_ref, hi_ref, lo_ref, ru_ref, rv_ref, tile_ref, acc_ref, l_ref, inv_ref, t_ref, up_ref, one_ref, xh_ref, xl_ref, sems) = refs[19:]
    n = l_ref.shape[0]

    @pl.when(meta[0] == 0)
    def _():
        one = started(slab_copies(meta, fs, gs, u_ref, v_ref, 0, 4), sems, 0)
        two = started(slab_copies(meta, fs, gs, u_ref, v_ref, 4, 4), sems, 32)
        three = started(slab_copies(meta, fs, gs, lo_ref, hi_ref, 8, 4, 0), sems, 64)
        acc_ref[...] = jnp.zeros_like(acc_ref)

        four = [pltpu.make_async_copy(src, dst, sems.at[96 + n])
                for n, (src, dst) in enumerate(row_copies(meta, rows, ru_ref, rv_ref) + [(band_hbm, tile_ref)])]

        def panel(k, _):
            @pl.when(k == 4)
            def _():
                waited(two)
                for copy in four:
                    copy.start()

            rank = meta[4 + k]
            vk, uk = v_ref[k], u_ref[k]
            core = masked(tn(vk, vk), rank, rank)
            left = jnp.dot(uk, core, preferred_element_type=jnp.float32).astype(jnp.bfloat16)
            for s in range(0, n, 512):
                acc_ref[s:s + 512, :] = acc_ref[s:s + 512, :] - nt(left[s:s + 512], uk)
            return 0

        waited(one)
        lax.fori_loop(0, 8, panel, 0)
        waited(three)

        def whole(rows, cols):
            q, at = cols.start // 256, slice(cols.start % 256, cols.start % 256 + NB)
            return acc_ref[rows, cols] + (hi_ref[q, rows, at].astype(jnp.float32) + lo_ref[q, rows, at].astype(jnp.float32))

        for i in range(n // NB):
            si = slice(i * NB, (i + 1) * NB)
            for j in range(i + 1):
                sj = slice(j * NB, (j + 1) * NB)
                l_ref[si, sj] = (whole(si, sj) + whole(sj, si).T) * 0.5
        waited(four)
        one_ref[...] = jnp.ones_like(one_ref)
        chol_body(l_ref, inv_ref, t_ref, up_ref, one_ref, lambda j: tile_panel(meta, j, tile_ref, u_ref, v_ref, ru_ref, rv_ref))
        for j in range(n // NB - 1):
            l_ref[j * NB:(j + 1) * NB, (j + 1) * NB:] = jnp.zeros((NB, n - (j + 1) * NB), jnp.float32)
        last = started([(l_ref.at[pl.ds(pl.multiple_of(meta[3] * 64, 64), 64), :], dout_hbm)], sems, 0)

        def done(j, s):
            last.extend(started([(tile_ref.at[:, s], out_hbm.at[:, s])], sems, 1 + j))

        solve_body(tile_ref, l_ref, inv_ref, tile_ref, xh_ref, xl_ref, done)
        waited(last)


def column_scratch(panels, order, rank):
    stack = pltpu.VMEM((panels, order, rank), jnp.bfloat16)
    quarter = pltpu.VMEM((4, order, rank), jnp.bfloat16)
    square = pltpu.VMEM((order, order), jnp.float32)
    block = pltpu.VMEM((NB, NB), jnp.float32)
    return [stack, stack, quarter, quarter, stack, stack, square, square, square,
            pltpu.VMEM((order, NB), jnp.float32), block, block, pltpu.VMEM((G, NB), jnp.float32),
            pltpu.VMEM((order, order), jnp.bfloat16), pltpu.VMEM((order, order), jnp.bfloat16),
            pltpu.SemaphoreType.DMA((128,))]


def tile_kernel(meta, *refs):
    even, odd, rows = refs[0:8], refs[8:16], refs[16:24]
    band_hbm, diag_hbm, _, _, out_hbm, dout_hbm = refs[24:30]
    u_ref, v_ref, ru_ref, rv_ref, tile_ref, slab_ref, sems, row_sems = refs[30:]
    panels = u_ref.shape[0]
    at = pl.ds(pl.multiple_of(meta[3] * 64, 64), 64)
    y, core_at = meta[0] // 2, meta[0] % 2

    @pl.when(meta[0] != 0)
    def _():
        four = started([(band_hbm, tile_ref), (diag_hbm, slab_ref)], sems, 128)

        def start_columns(group, _):
            first = ((y + SIDE - group) % SIDE) * 2

            @pl.when(core_at == 0)
            def _():
                started(slab_copies(meta, even[:4], even[4:], u_ref, v_ref, first, 2), sems, 16 * first)

            @pl.when(core_at != 0)
            def _():
                started(slab_copies(meta, odd[:4], odd[4:], u_ref, v_ref, first, 2), sems, 16 * first)

            return 0

        for e in range(SIDE):
            near = ((y + SIDE - e) % SIDE) * 2
            for src, k in ((rows[e], near + core_at), (rows[SIDE + e], near + 1 - core_at)):
                pltpu.make_async_copy(src.at[0], ru_ref.at[k], row_sems.at[k]).start()
                pltpu.make_async_copy(src.at[1], rv_ref.at[k], row_sems.at[panels + k]).start()
        lax.fori_loop(0, panels // 2, start_columns, 0)
        waited(four)

        def panel(step, _):
            k = ((y + SIDE - step // 2) % SIDE) * 2 + step % 2

            @pl.when(k % 2 == 0)
            def _():
                waits = slab_copies(meta, odd[:4], odd[4:], u_ref, v_ref, k, 2)
                waited([pltpu.make_async_copy(src, dst, sems.at[16 * k + i]) for i, (src, dst) in enumerate(waits)])

            pltpu.make_async_copy(rows[0].at[0], ru_ref.at[k], row_sems.at[k]).wait()
            pltpu.make_async_copy(rows[0].at[1], rv_ref.at[k], row_sems.at[panels + k]).wait()
            tile_panel(meta, k, tile_ref, u_ref, v_ref, ru_ref, rv_ref)
            rank = meta[4 + k]
            vk = v_ref[k]
            core = masked(tn(vk, vk), rank, rank)
            part = jnp.dot(u_ref[k, at, :], core, preferred_element_type=jnp.float32).astype(jnp.bfloat16)
            slab_ref[...] = slab_ref[...] - nt(part, u_ref[k])
            return 0

        lax.fori_loop(0, panels, panel, 0)
        waited(started([(tile_ref, out_hbm), (slab_ref, dout_hbm)], sems, 0))


def tile_scratch(panels, order, rank):
    stack = pltpu.VMEM((panels, order, rank), jnp.bfloat16)
    return [stack] * 4 + [pltpu.VMEM((order, order), jnp.float32), pltpu.VMEM((64, order), jnp.float32),
                          pltpu.SemaphoreType.DMA((130,)), pltpu.SemaphoreType.DMA((2 * panels,))]


def moved(value, pairs):
    return lax.ppermute(value, AXES, pairs)


def along(axis, step, parity):
    pairs = []
    for x in range(SIDE):
        for z in range(SIDE):
            for col in range(parity, 8, 2):
                to = ((x + step) % SIDE, z) if axis == "x" else (x, (z + step) % SIDE)
                pairs.append(((x * SIDE + z) * 8 + col, (to[0] * SIDE + to[1]) * 8 + col))
    return pairs


def across(change):
    return [(row * 8 + col, row * 8 + change(col)) for row in range(16) for col in range(8)]


def both_ways(a, b, one, two, parity):
    got_a, got_b = [a, None, None, None], [b, None, None, None]
    for d in (1, 3, 2):
        got_a[d] = moved(a, along(one, d, parity))
        got_b[d] = moved(b, along(two, d, parity))
    return got_a, got_b


def first_leg(first, second, parity):
    return both_ways(first, second, "x", "z", parity)


def second_leg(a, b, parity):
    a, b = lax.optimization_barrier((jnp.stack(a), jnp.stack(b)))
    return both_ways(a, b, "z", "x", parity)


def shards(band, diag, row_factors, row_ranks, col_factors, col_ranks):
    column = lax.axis_index("cols")
    slab = lax.axis_index("rows")
    panels, slab_rows = col_factors.shape[0], diag.shape[1]
    order, rank = row_factors.shape[3], row_factors.shape[4]
    own_ranks = lax.dynamic_index_in_dim(col_ranks, column, 0, keepdims=False)
    meta = jnp.concatenate([jnp.stack([column, slab // SIDE, slab % SIDE, slab]).astype(jnp.int32), own_ranks])

    turned = row_factors[0, 0, 1].reshape(order // rank, rank, rank).transpose(0, 2, 1)
    kept = (jnp.arange(rank, dtype=jnp.int32) < row_ranks[0, 0])[None, :, None]
    turned = jnp.where(kept, turned, jnp.zeros((), turned.dtype)).reshape(order, rank)
    mine = jnp.stack([row_factors[0, 0, 0], turned])

    own = lax.all_to_all(col_factors, "cols", split_axis=0, concat_axis=1, tiled=True)[0]
    pieces = diag[0].reshape(slab_rows, 4, rank).transpose(1, 0, 2)
    rounded = lax.reduce_precision(pieces, exponent_bits=8, mantissa_bits=7)
    high = rounded.astype(jnp.bfloat16)
    low = (pieces - rounded).astype(jnp.bfloat16)
    own, mine, meta, high, low = lax.optimization_barrier((own, mine, meta, high, low))
    near = [mine] + [moved(mine, across(lambda c, d=d: ((c // 2 + d) % SIDE) * 2 + c % 2)) for d in (1, 2, 3)]
    sides, bases = own[:, 1], own[:, 0]
    a, b = lax.optimization_barrier(first_leg(jnp.concatenate([sides, high]), jnp.concatenate([bases, low]), 0))
    fs, gs = second_leg(a, b, 0)
    far = [moved(p, across(lambda c: c ^ 1)) for p in near]
    odd_a, odd_b = lax.optimization_barrier(first_leg(sides, bases, 1))
    odd_fs, odd_gs = second_leg(odd_a, odd_b, 1)
    fs, gs, near, far, own_a, own_b = lax.optimization_barrier((fs, gs, near, far, odd_fs[0], odd_gs[0]))
    odd_fs, odd_gs = [own_a] + odd_fs[1:], [own_b] + odd_gs[1:]

    hbm = pl.BlockSpec(memory_space=pl.ANY)
    smem = pl.BlockSpec(memory_space=pltpu.SMEM)
    outs = (jax.ShapeDtypeStruct((order, order), jnp.float32), jax.ShapeDtypeStruct((slab_rows, order), jnp.float32))
    params = pltpu.CompilerParams(vmem_limit_bytes=COLUMN_GRANT)
    tile, slab_out = pl.pallas_call(
        column_kernel,
        out_shape=outs,
        in_specs=[smem] + [hbm] * 17,
        out_specs=(hbm, hbm),
        scratch_shapes=column_scratch(panels, order, rank),
        cost_estimate=pl.CostEstimate(flops=60_000_000_000, bytes_accessed=20_000_000, transcendentals=0),
        compiler_params=params, name="column")(meta, *fs, *gs, *near, *far, band[0, 0])

    tile, slab_out = pl.pallas_call(
        tile_kernel,
        out_shape=outs,
        in_specs=[smem] + [hbm] * 28,
        out_specs=(hbm, hbm),
        scratch_shapes=tile_scratch(panels, order, rank),
        input_output_aliases={27: 0, 28: 1},
        cost_estimate=pl.CostEstimate(flops=10_000_000_000, bytes_accessed=40_000_000, transcendentals=0),
        compiler_params=pltpu.CompilerParams(vmem_limit_bytes=TILE_GRANT), name="tile")(
            meta, *fs, *gs, *odd_fs, *odd_gs, *near, *far, band[0, 0], diag[0], tile, slab_out)
    return tile[None, None], slab_out[None]


def solution(mesh):
    placed = (
        P("rows", "cols", None, None),
        P("cols", "rows", None),
        P("rows", "cols", None, None, None),
        P("rows", "cols"),
        P(None, "cols", None, "rows", None),
        P(),
    )
    return jax.shard_map(
        shards,
        mesh=mesh,
        in_specs=placed,
        out_specs=(P("rows", "cols", None, None), P("cols", "rows", None)),
        check_vma=False,
    )
```

profile of v0, /device:TPU:4, one launch (start us, length us, event | category | flops | bytes accessed | tf_op | source)
XLA Modules:
  0.0 221.3 jit_solution(14349488049824836804)
XLA Ops:
  0.7 4.6 %all-to-all-start = ((bf16[8,1,2,64,256]{4,3,2,1,0:T(8,128)(2,1)}), bf16[8,1,2,64,256]{4,3,2,1,0:T(8,128)(2,1)S(1)}, u32[]{:S(2)}, u32[]{:S(2)}) async-start(bf16[8,1,2,64,256]{4,3,2,1,0:T(8,128)(2,1)} %param.10), calls=%async_computation | async-start | bytes 1048576 | tf_op jit(solution)/shard_map/all_to_all | solution.py:400
  5.9 1.1 reshape_squeeze.7
  7.1 0.2 copy.16
  7.3 0.1 broadcast_select_fusion
  7.5 0.1 concatenate.9.meta
  7.6 0.1 pad_maximum_fusion.2.refs_8_.refs_16_
  7.7 7.9 %all-to-all-done = bf16[8,1,2,64,256]{4,3,2,1,0:T(8,128)(2,1)S(1)} async-done(((bf16[8,1,2,64,256]{4,3,2,1,0:T(8,128)(2,1)}), bf16[8,1,2,64,256]{4,3,2,1,0:T(8,128)(2,1)S(1)}, u32[]{:S(2)}, u32[]{:S(2)}) %all-to-all-start) | async-done | bytes 524320 | tf_op jit(solution)/shard_map/all_to_all | solution.py:400
  15.7 0.7 collective-permute-start.24
  16.4 0.7 collective-permute-start.23
  17.1 2.4 %collective-permute-start.2 = (bf16[12,64,256]{2,1,0:T(8,128)(2,1)S(1)}, bf16[12,64,256]{2,1,0:T(8,128)(2,1)S(1)}, u32[]{:S(2)}, u32[]{:S(2)}) collective-permute-start(bf16[12,64,256]{2,1,0:T(8,128)(2,1)S(1)} %pad_maximum_fusion.5), channel_id=1, source_target_pairs={{0,96},{2,98},{4,100},{6,102},{8,104},{10,106},{12,108},{14,110},{... | collective-permute-start | bytes 1179656 | tf_op jit(solution)/shard_map/ppermute | solution.py:353
  19.6 0.7 collective-permute-start.22
  20.2 0.7 collective-permute-start.21
  20.9 4.6 %collective-permute-start.1 = (bf16[12,64,256]{2,1,0:T(8,128)(2,1)S(1)}, bf16[12,64,256]{2,1,0:T(8,128)(2,1)S(1)}, u32[]{:S(2)}, u32[]{:S(2)}) collective-permute-start(bf16[12,64,256]{2,1,0:T(8,128)(2,1)S(1)} %pad_maximum_fusion.5), channel_id=1, source_target_pairs={{0,64},{2,66},{4,68},{6,70},{8,72},{10,74},{12,76},{14,78},{16,80}... | collective-permute-start | bytes 1179656 | tf_op jit(solution)/shard_map/ppermute | solution.py:353
  25.6 1.9 collective-permute-start
  27.6 5.9 %collective-permute-start.5 = (bf16[12,64,256]{2,1,0:T(8,128)(2,1)S(1)}, bf16[12,64,256]{2,1,0:T(8,128)(2,1)S(1)}, u32[]{:S(2)}, u32[]{:S(2)}) collective-permute-start(bf16[12,64,256]{2,1,0:T(8,128)(2,1)S(1)} %pad_maximum_fusion.6), channel_id=1, source_target_pairs={{0,24},{2,26},{4,28},{6,30},{8,0},{10,2},{12,4},{14,6},{16,8},{18,... | collective-permute-start | bytes 1179656 | tf_op jit(solution)/shard_map/ppermute | solution.py:353
  33.5 1.9 collective-permute-start.4
  35.5 3.2 %collective-permute-start.3 = (bf16[12,64,256]{2,1,0:T(8,128)(2,1)S(1)}, bf16[12,64,256]{2,1,0:T(8,128)(2,1)S(1)}, u32[]{:S(2)}, u32[]{:S(2)}) collective-permute-start(bf16[12,64,256]{2,1,0:T(8,128)(2,1)S(1)} %pad_maximum_fusion.6), channel_id=1, source_target_pairs={{0,8},{2,10},{4,12},{6,14},{8,16},{10,18},{12,20},{14,22},{16,24},... | collective-permute-start | bytes 1179656 | tf_op jit(solution)/shard_map/ppermute | solution.py:353
  38.8 1.2 collective-permute-start.14
  40.0 3.0 %collective-permute-done.5 = bf16[12,64,256]{2,1,0:T(8,128)(2,1)S(1)} collective-permute-done((bf16[12,64,256]{2,1,0:T(8,128)(2,1)S(1)}, bf16[12,64,256]{2,1,0:T(8,128)(2,1)S(1)}, u32[]{:S(2)}, u32[]{:S(2)}) %collective-permute-start.5) | collective-permute-done | bytes 393248 | tf_op jit(solution)/shard_map/ppermute | solution.py:353
  43.0 0.7 collective-permute-start.20
  43.7 1.1 collective-permute-done.4
  44.8 0.4 collective-permute-start.13
  45.2 3.7 %collective-permute-done.3 = bf16[12,64,256]{2,1,0:T(8,128)(2,1)S(1)} collective-permute-done((bf16[12,64,256]{2,1,0:T(8,128)(2,1)S(1)}, bf16[12,64,256]{2,1,0:T(8,128)(2,1)S(1)}, u32[]{:S(2)}, u32[]{:S(2)}) %collective-permute-start.3) | collective-permute-done | bytes 393248 | tf_op jit(solution)/shard_map/ppermute | solution.py:353
  48.9 0.6 collective-permute-start.12
  49.5 0.7 collective-permute-start.19
  50.2 0.4 pad_maximum_fusion
  50.7 2.5 %collective-permute-start.8 = (bf16[4,12,64,256]{3,2,1,0:T(8,128)(2,1)S(1)}, bf16[4,12,64,256]{3,2,1,0:T(8,128)(2,1)S(1)}, u32[]{:S(2)}, u32[]{:S(2)}) collective-permute-start(bf16[4,12,64,256]{3,2,1,0:T(8,128)(2,1)S(1)} %get-tuple-element.74.refs_0_), channel_id=1, source_target_pairs={{0,24},{2,26},{4,28},{6,30},{8,0},{10,2},{12,4},{14,6},{16,8},{18,... | collective-permute-start | bytes 4718600 | tf_op jit(solution)/shard_map/ppermute | solution.py:353
  53.2 1.9 collective-permute-start.7
  55.1 9.7 %collective-permute-done.14.refs_11_.refs_19_ = bf16[2,1024,256]{2,1,0:T(8,128)(2,1)S(1)} collective-permute-done((bf16[2,1024,256]{2,1,0:T(8,128)(2,1)S(1)}, bf16[2,1024,256]{2,1,0:T(8,128)(2,1)S(1)}, u32[]{:S(2)}, u32[]{:S(2)}) %collective-permute-start.14) | collective-permute-done | bytes 1048608 | tf_op jit(solution)/shard_map/ppermute | solution.py:353
  64.9 4.1 %collective-permute-start.6 = (bf16[4,12,64,256]{3,2,1,0:T(8,128)(2,1)S(1)}, bf16[4,12,64,256]{3,2,1,0:T(8,128)(2,1)S(1)}, u32[]{:S(2)}, u32[]{:S(2)}) collective-permute-start(bf16[4,12,64,256]{3,2,1,0:T(8,128)(2,1)S(1)} %get-tuple-element.74.refs_0_), channel_id=1, source_target_pairs={{0,8},{2,10},{4,12},{6,14},{8,16},{10,18},{12,20},{14,22},{16,24},... | collective-permute-start | bytes 4718600 | tf_op jit(solution)/shard_map/ppermute | solution.py:353
  69.0 3.4 %collective-permute-done.13.refs_10_.refs_18_ = bf16[2,1024,256]{2,1,0:T(8,128)(2,1)S(1)} collective-permute-done((bf16[2,1024,256]{2,1,0:T(8,128)(2,1)S(1)}, bf16[2,1024,256]{2,1,0:T(8,128)(2,1)S(1)}, u32[]{:S(2)}, u32[]{:S(2)}) %collective-permute-start.13) | collective-permute-done | bytes 1048608 | tf_op jit(solution)/shard_map/ppermute | solution.py:353
  72.4 3.9 %collective-permute-start.11 = (bf16[4,12,64,256]{3,2,1,0:T(8,128)(2,1)S(1)}, bf16[4,12,64,256]{3,2,1,0:T(8,128)(2,1)S(1)}, u32[]{:S(2)}, u32[]{:S(2)}) collective-permute-start(bf16[4,12,64,256]{3,2,1,0:T(8,128)(2,1)S(1)} %get-tuple-element.78.refs_4_), channel_id=1, source_target_pairs={{0,96},{2,98},{4,100},{6,102},{8,104},{10,106},{12,108},{14,110},{... | collective-permute-start | bytes 4718600 | tf_op jit(solution)/shard_map/ppermute | solution.py:353
  76.3 16.3 %collective-permute-done.12.refs_9_.refs_17_ = bf16[2,1024,256]{2,1,0:T(8,128)(2,1)S(1)} collective-permute-done((bf16[2,1024,256]{2,1,0:T(8,128)(2,1)S(1)}, bf16[2,1024,256]{2,1,0:T(8,128)(2,1)S(1)}, u32[]{:S(2)}, u32[]{:S(2)}) %collective-permute-start.12) | collective-permute-done | bytes 1048608 | tf_op jit(solution)/shard_map/ppermute | solution.py:353
  92.6 3.8 %collective-permute-start.10 = (bf16[4,12,64,256]{3,2,1,0:T(8,128)(2,1)S(1)}, bf16[4,12,64,256]{3,2,1,0:T(8,128)(2,1)S(1)}, u32[]{:S(2)}, u32[]{:S(2)}) collective-permute-start(bf16[4,12,64,256]{3,2,1,0:T(8,128)(2,1)S(1)} %get-tuple-element.78.refs_4_), channel_id=1, source_target_pairs={{0,64},{2,66},{4,68},{6,70},{8,72},{10,74},{12,76},{14,78},{16,80}... | collective-permute-start | bytes 4718600 | tf_op jit(solution)/shard_map/ppermute | solution.py:353
  96.3 3.9 %collective-permute-start.9 = (bf16[4,12,64,256]{3,2,1,0:T(8,128)(2,1)S(1)}, bf16[4,12,64,256]{3,2,1,0:T(8,128)(2,1)S(1)}, u32[]{:S(2)}, u32[]{:S(2)}) collective-permute-start(bf16[4,12,64,256]{3,2,1,0:T(8,128)(2,1)S(1)} %get-tuple-element.78.refs_4_), channel_id=1, source_target_pairs={{0,32},{2,34},{4,36},{6,38},{8,40},{10,42},{12,44},{14,46},{16,48}... | collective-permute-start | bytes 4718600 | tf_op jit(solution)/shard_map/ppermute | solution.py:353
  100.4 0.5 collective-permute-start.17
  100.8 0.3 pad_maximum_fusion.3
  101.1 0.2 collective-permute-start.16
  101.3 15.1 %collective-permute-done.10.refs_6_ = bf16[4,12,64,256]{3,2,1,0:T(8,128)(2,1)S(1)} collective-permute-done((bf16[4,12,64,256]{3,2,1,0:T(8,128)(2,1)S(1)}, bf16[4,12,64,256]{3,2,1,0:T(8,128)(2,1)S(1)}, u32[]{:S(2)}, u32[]{:S(2)}) %collective-permute-start.10) | collective-permute-done | bytes 1572896 | tf_op jit(solution)/shard_map/ppermute | solution.py:353
  116.5 0.7 collective-permute-start.27
  117.2 38.5 %collective-permute-done.9.refs_5_ = bf16[4,12,64,256]{3,2,1,0:T(8,128)(2,1)S(1)} collective-permute-done((bf16[4,12,64,256]{3,2,1,0:T(8,128)(2,1)S(1)}, bf16[4,12,64,256]{3,2,1,0:T(8,128)(2,1)S(1)}, u32[]{:S(2)}, u32[]{:S(2)}) %collective-permute-start.9) | collective-permute-done | bytes 1572896 | tf_op jit(solution)/shard_map/ppermute | solution.py:353
  155.7 1.7 collective-permute-start.26
  157.4 1.6 collective-permute-start.25
  159.0 1.6 collective-permute-start.30
  160.6 1.6 collective-permute-start.29
  162.3 1.7 collective-permute-start.28
  164.1 54.9 %column.1 = (f32[1024,1024]{1,0:T(8,128)}, f32[64,1024]{1,0:T(8,128)}) custom-call(s32[12]{0:T(128)S(1)} %concatenate.9.meta, bf16[4,12,64,256]{3,2,1,0:T(8,128)(2,1)} %copy-done.9, bf16[4,12,64,256]{3,2,1,0:T(8,128)(2,1)} %copy-done.15, bf16[4,12,64,256]{3,2,1,0:T(8,128)(2,1)} %copy-done.14, bf16[4,12,64,256]{3,2,1,0:T(8,128)(2,1)} %copy-done.13, ...), custom_call_target="tpu_custom_call" | custom-call | flops 60000002048 | bytes 20000000 | tf_op jit(solution)/shard_map/column/pallas_call | solution.py:420
  219.0 2.0 tile.1
  (77 shorter events, 0.6 us)
Async XLA Ops:
  0.7 14.9 %all-to-all-start = ((bf16[8,1,2,64,256]{4,3,2,1,0:T(8,128)(2,1)}), bf16[8,1,2,64,256]{4,3,2,1,0:T(8,128)(2,1)S(1)}, u32[]{:S(2)}, u32[]{:S(2)}) async-start(bf16[8,1,2,64,256]{4,3,2,1,0:T(8,128)(2,1)} %param.10), calls=%async_computation | async-start | bytes 1048576 | tf_op jit(solution)/shard_map/all_to_all | solution.py:400
  7.5 156.4 %copy-start.8 = (s32[12]{0:T(128)}, s32[12]{0:T(128)S(1)}, u32[]{:S(2)}) copy-start(s32[12]{0:T(128)S(1)} %concatenate.9.meta) | copy-start | bytes 148
  7.7 156.3 %copy-start.1 = (bf16[2,1024,256]{2,1,0:T(8,128)(2,1)}, bf16[2,1024,256]{2,1,0:T(8,128)(2,1)S(1)}, u32[]{:S(2)}) copy-start(bf16[2,1024,256]{2,1,0:T(8,128)(2,1)S(1)} %pad_maximum_fusion.2.refs_8_.refs_16_) | copy-start | bytes 3145732
  15.7 5.2 %collective-permute-start.24 = (bf16[8,64,256]{2,1,0:T(8,128)(2,1)S(1)}, bf16[8,64,256]{2,1,0:T(8,128)(2,1)S(1)}, u32[]{:S(2)}, u32[]{:S(2)}) collective-permute-start(bf16[8,64,256]{2,1,0:T(8,128)(2,1)S(1)} %get-tuple-element.68), channel_id=1, source_target_pairs={{1,25},{3,27},{5,29},{7,31},{9,1},{11,3},{13,5},{15,7},{17,9},{19,... | collective-permute-start | bytes 786440 | tf_op jit(solution)/shard_map/ppermute | solution.py:353
  16.4 9.2 %collective-permute-start.23 = (bf16[8,64,256]{2,1,0:T(8,128)(2,1)S(1)}, bf16[8,64,256]{2,1,0:T(8,128)(2,1)S(1)}, u32[]{:S(2)}, u32[]{:S(2)}) collective-permute-start(bf16[8,64,256]{2,1,0:T(8,128)(2,1)S(1)} %get-tuple-element.68), channel_id=1, source_target_pairs={{1,17},{3,19},{5,21},{7,23},{9,25},{11,27},{13,29},{15,31},{17,1},... | collective-permute-start | bytes 786440 | tf_op jit(solution)/shard_map/ppermute | solution.py:353
  17.1 18.4 %collective-permute-start.2 = (bf16[12,64,256]{2,1,0:T(8,128)(2,1)S(1)}, bf16[12,64,256]{2,1,0:T(8,128)(2,1)S(1)}, u32[]{:S(2)}, u32[]{:S(2)}) collective-permute-start(bf16[12,64,256]{2,1,0:T(8,128)(2,1)S(1)} %pad_maximum_fusion.5), channel_id=1, source_target_pairs={{0,96},{2,98},{4,100},{6,102},{8,104},{10,106},{12,108},{14,110},{... | collective-permute-start | bytes 1179656 | tf_op jit(solution)/shard_map/ppermute | solution.py:353
  19.6 8.0 %collective-permute-start.22 = (bf16[8,64,256]{2,1,0:T(8,128)(2,1)S(1)}, bf16[8,64,256]{2,1,0:T(8,128)(2,1)S(1)}, u32[]{:S(2)}, u32[]{:S(2)}) collective-permute-start(bf16[8,64,256]{2,1,0:T(8,128)(2,1)S(1)} %get-tuple-element.68), channel_id=1, source_target_pairs={{1,9},{3,11},{5,13},{7,15},{9,17},{11,19},{13,21},{15,23},{17,25},... | collective-permute-start | bytes 786440 | tf_op jit(solution)/shard_map/ppermute | solution.py:353
  20.2 13.3 %collective-permute-start.21 = (bf16[8,64,256]{2,1,0:T(8,128)(2,1)S(1)}, bf16[8,64,256]{2,1,0:T(8,128)(2,1)S(1)}, u32[]{:S(2)}, u32[]{:S(2)}) collective-permute-start(bf16[8,64,256]{2,1,0:T(8,128)(2,1)S(1)} %get-tuple-element.64), channel_id=1, source_target_pairs={{1,97},{3,99},{5,101},{7,103},{9,105},{11,107},{13,109},{15,111},{... | collective-permute-start | bytes 786440 | tf_op jit(solution)/shard_map/ppermute | solution.py:353
  20.9 17.7 %collective-permute-start.1 = (bf16[12,64,256]{2,1,0:T(8,128)(2,1)S(1)}, bf16[12,64,256]{2,1,0:T(8,128)(2,1)S(1)}, u32[]{:S(2)}, u32[]{:S(2)}) collective-permute-start(bf16[12,64,256]{2,1,0:T(8,128)(2,1)S(1)} %pad_maximum_fusion.5), channel_id=1, source_target_pairs={{0,64},{2,66},{4,68},{6,70},{8,72},{10,74},{12,76},{14,78},{16,80}... | collective-permute-start | bytes 1179656 | tf_op jit(solution)/shard_map/ppermute | solution.py:353
  25.6 13.2 %collective-permute-start = (bf16[12,64,256]{2,1,0:T(8,128)(2,1)S(1)}, bf16[12,64,256]{2,1,0:T(8,128)(2,1)S(1)}, u32[]{:S(2)}, u32[]{:S(2)}) collective-permute-start(bf16[12,64,256]{2,1,0:T(8,128)(2,1)S(1)} %pad_maximum_fusion.5), channel_id=1, source_target_pairs={{0,32},{2,34},{4,36},{6,38},{8,40},{10,42},{12,44},{14,46},{16,48}... | collective-permute-start | bytes 1179656 | tf_op jit(solution)/shard_map/ppermute | solution.py:353
  27.6 15.4 %collective-permute-start.5 = (bf16[12,64,256]{2,1,0:T(8,128)(2,1)S(1)}, bf16[12,64,256]{2,1,0:T(8,128)(2,1)S(1)}, u32[]{:S(2)}, u32[]{:S(2)}) collective-permute-start(bf16[12,64,256]{2,1,0:T(8,128)(2,1)S(1)} %pad_maximum_fusion.6), channel_id=1, source_target_pairs={{0,24},{2,26},{4,28},{6,30},{8,0},{10,2},{12,4},{14,6},{16,8},{18,... | collective-permute-start | bytes 1179656 | tf_op jit(solution)/shard_map/ppermute | solution.py:353
  33.5 11.3 %collective-permute-start.4 = (bf16[12,64,256]{2,1,0:T(8,128)(2,1)S(1)}, bf16[12,64,256]{2,1,0:T(8,128)(2,1)S(1)}, u32[]{:S(2)}, u32[]{:S(2)}) collective-permute-start(bf16[12,64,256]{2,1,0:T(8,128)(2,1)S(1)} %pad_maximum_fusion.6), channel_id=1, source_target_pairs={{0,16},{2,18},{4,20},{6,22},{8,24},{10,26},{12,28},{14,30},{16,0},... | collective-permute-start | bytes 1179656 | tf_op jit(solution)/shard_map/ppermute | solution.py:353
  35.5 13.4 %collective-permute-start.3 = (bf16[12,64,256]{2,1,0:T(8,128)(2,1)S(1)}, bf16[12,64,256]{2,1,0:T(8,128)(2,1)S(1)}, u32[]{:S(2)}, u32[]{:S(2)}) collective-permute-start(bf16[12,64,256]{2,1,0:T(8,128)(2,1)S(1)} %pad_maximum_fusion.6), channel_id=1, source_target_pairs={{0,8},{2,10},{4,12},{6,14},{8,16},{10,18},{12,20},{14,22},{16,24},... | collective-permute-start | bytes 1179656 | tf_op jit(solution)/shard_map/ppermute | solution.py:353
  38.6 14.5 %collective-permute-start.15 = (bf16[2,1024,256]{2,1,0:T(8,128)(2,1)S(1)}, bf16[2,1024,256]{2,1,0:T(8,128)(2,1)S(1)}, u32[]{:S(2)}, u32[]{:S(2)}) collective-permute-start(bf16[2,1024,256]{2,1,0:T(8,128)(2,1)S(1)} %pad_maximum_fusion.2.refs_8_.refs_16_), channel_id=1, source_target_pairs={{0,1},{1,0},{2,3},{3,2},{4,5},{5,4},{6,7},{7,6},{8,9},{9,8},{10,11... | collective-permute-start | bytes 3145736 | tf_op jit(solution)/shard_map/ppermute | solution.py:353
  38.8 26.1 %collective-permute-start.14 = (bf16[2,1024,256]{2,1,0:T(8,128)(2,1)S(1)}, bf16[2,1024,256]{2,1,0:T(8,128)(2,1)S(1)}, u32[]{:S(2)}, u32[]{:S(2)}) collective-permute-start(bf16[2,1024,256]{2,1,0:T(8,128)(2,1)S(1)} %pad_maximum_fusion.2.refs_8_.refs_16_), channel_id=1, source_target_pairs={{0,6},{1,7},{2,0},{3,1},{4,2},{5,3},{6,4},{7,5},{8,14},{9,15},{10,... | collective-permute-start | bytes 3145736 | tf_op jit(solution)/shard_map/ppermute | solution.py:353
  43.0 6.5 %collective-permute-start.20 = (bf16[8,64,256]{2,1,0:T(8,128)(2,1)S(1)}, bf16[8,64,256]{2,1,0:T(8,128)(2,1)S(1)}, u32[]{:S(2)}, u32[]{:S(2)}) collective-permute-start(bf16[8,64,256]{2,1,0:T(8,128)(2,1)S(1)} %get-tuple-element.64), channel_id=1, source_target_pairs={{1,65},{3,67},{5,69},{7,71},{9,73},{11,75},{13,77},{15,79},{17,81}... | collective-permute-start | bytes 786440 | tf_op jit(solution)/shard_map/ppermute | solution.py:353
  44.8 27.6 %collective-permute-start.13 = (bf16[2,1024,256]{2,1,0:T(8,128)(2,1)S(1)}, bf16[2,1024,256]{2,1,0:T(8,128)(2,1)S(1)}, u32[]{:S(2)}, u32[]{:S(2)}) collective-permute-start(bf16[2,1024,256]{2,1,0:T(8,128)(2,1)S(1)} %pad_maximum_fusion.2.refs_8_.refs_16_), channel_id=1, source_target_pairs={{0,4},{1,5},{2,6},{3,7},{4,0},{5,1},{6,2},{7,3},{8,12},{9,13},{10,... | collective-permute-start | bytes 3145736 | tf_op jit(solution)/shard_map/ppermute | solution.py:353
  48.9 43.6 %collective-permute-start.12 = (bf16[2,1024,256]{2,1,0:T(8,128)(2,1)S(1)}, bf16[2,1024,256]{2,1,0:T(8,128)(2,1)S(1)}, u32[]{:S(2)}, u32[]{:S(2)}) collective-permute-start(bf16[2,1024,256]{2,1,0:T(8,128)(2,1)S(1)} %pad_maximum_fusion.2.refs_8_.refs_16_), channel_id=1, source_target_pairs={{0,2},{1,3},{2,4},{3,5},{4,6},{5,7},{6,0},{7,1},{8,10},{9,11},{10,... | collective-permute-start | bytes 3145736 | tf_op jit(solution)/shard_map/ppermute | solution.py:353
  49.5 1.1 collective-permute-start.19
  50.6 113.3 %copy-start.9 = (bf16[4,12,64,256]{3,2,1,0:T(8,128)(2,1)}, bf16[4,12,64,256]{3,2,1,0:T(8,128)(2,1)S(1)}, u32[]{:S(2)}) copy-start(bf16[4,12,64,256]{3,2,1,0:T(8,128)(2,1)S(1)} %get-tuple-element.74.refs_0_) | copy-start | bytes 4718596
  50.6 113.3 %copy-start.10 = (bf16[4,12,64,256]{3,2,1,0:T(8,128)(2,1)}, bf16[4,12,64,256]{3,2,1,0:T(8,128)(2,1)S(1)}, u32[]{:S(2)}) copy-start(bf16[4,12,64,256]{3,2,1,0:T(8,128)(2,1)S(1)} %get-tuple-element.78.refs_4_) | copy-start | bytes 4718596
  50.7 45.7 %collective-permute-start.8 = (bf16[4,12,64,256]{3,2,1,0:T(8,128)(2,1)S(1)}, bf16[4,12,64,256]{3,2,1,0:T(8,128)(2,1)S(1)}, u32[]{:S(2)}, u32[]{:S(2)}) collective-permute-start(bf16[4,12,64,256]{3,2,1,0:T(8,128)(2,1)S(1)} %get-tuple-element.74.refs_0_), channel_id=1, source_target_pairs={{0,24},{2,26},{4,28},{6,30},{8,0},{10,2},{12,4},{14,6},{16,8},{18,... | collective-permute-start | bytes 4718600 | tf_op jit(solution)/shard_map/ppermute | solution.py:353
  53.2 110.8 %copy-start.2 = (bf16[2,1024,256]{2,1,0:T(8,128)(2,1)}, bf16[2,1024,256]{2,1,0:T(8,128)(2,1)S(1)}, u32[]{:S(2)}) copy-start(bf16[2,1024,256]{2,1,0:T(8,128)(2,1)S(1)} %collective-permute-done.15.refs_12_.refs_20_) | copy-start | bytes 3145732
  53.2 47.0 %collective-permute-start.7 = (bf16[4,12,64,256]{3,2,1,0:T(8,128)(2,1)S(1)}, bf16[4,12,64,256]{3,2,1,0:T(8,128)(2,1)S(1)}, u32[]{:S(2)}, u32[]{:S(2)}) collective-permute-start(bf16[4,12,64,256]{3,2,1,0:T(8,128)(2,1)S(1)} %get-tuple-element.74.refs_0_), channel_id=1, source_target_pairs={{0,16},{2,18},{4,20},{6,22},{8,24},{10,26},{12,28},{14,30},{16,0},... | collective-permute-start | bytes 4718600 | tf_op jit(solution)/shard_map/ppermute | solution.py:353
  64.9 99.1 %copy-start.3 = (bf16[2,1024,256]{2,1,0:T(8,128)(2,1)}, bf16[2,1024,256]{2,1,0:T(8,128)(2,1)S(1)}, u32[]{:S(2)}) copy-start(bf16[2,1024,256]{2,1,0:T(8,128)(2,1)S(1)} %collective-permute-done.14.refs_11_.refs_19_) | copy-start | bytes 3145732
  64.9 35.5 %collective-permute-start.6 = (bf16[4,12,64,256]{3,2,1,0:T(8,128)(2,1)S(1)}, bf16[4,12,64,256]{3,2,1,0:T(8,128)(2,1)S(1)}, u32[]{:S(2)}, u32[]{:S(2)}) collective-permute-start(bf16[4,12,64,256]{3,2,1,0:T(8,128)(2,1)S(1)} %get-tuple-element.74.refs_0_), channel_id=1, source_target_pairs={{0,8},{2,10},{4,12},{6,14},{8,16},{10,18},{12,20},{14,22},{16,24},... | collective-permute-start | bytes 4718600 | tf_op jit(solution)/shard_map/ppermute | solution.py:353
  72.4 91.6 %copy-start.4 = (bf16[2,1024,256]{2,1,0:T(8,128)(2,1)}, bf16[2,1024,256]{2,1,0:T(8,128)(2,1)S(1)}, u32[]{:S(2)}) copy-start(bf16[2,1024,256]{2,1,0:T(8,128)(2,1)S(1)} %collective-permute-done.13.refs_10_.refs_18_) | copy-start | bytes 3145732
  72.4 28.7 %collective-permute-start.11 = (bf16[4,12,64,256]{3,2,1,0:T(8,128)(2,1)S(1)}, bf16[4,12,64,256]{3,2,1,0:T(8,128)(2,1)S(1)}, u32[]{:S(2)}, u32[]{:S(2)}) collective-permute-start(bf16[4,12,64,256]{3,2,1,0:T(8,128)(2,1)S(1)} %get-tuple-element.78.refs_4_), channel_id=1, source_target_pairs={{0,96},{2,98},{4,100},{6,102},{8,104},{10,106},{12,108},{14,110},{... | collective-permute-start | bytes 4718600 | tf_op jit(solution)/shard_map/ppermute | solution.py:353
  92.6 71.5 %copy-start.5 = (bf16[2,1024,256]{2,1,0:T(8,128)(2,1)}, bf16[2,1024,256]{2,1,0:T(8,128)(2,1)S(1)}, u32[]{:S(2)}) copy-start(bf16[2,1024,256]{2,1,0:T(8,128)(2,1)S(1)} %collective-permute-done.12.refs_9_.refs_17_) | copy-start | bytes 3145732
  92.6 23.9 %collective-permute-start.10 = (bf16[4,12,64,256]{3,2,1,0:T(8,128)(2,1)S(1)}, bf16[4,12,64,256]{3,2,1,0:T(8,128)(2,1)S(1)}, u32[]{:S(2)}, u32[]{:S(2)}) collective-permute-start(bf16[4,12,64,256]{3,2,1,0:T(8,128)(2,1)S(1)} %get-tuple-element.78.refs_4_), channel_id=1, source_target_pairs={{0,64},{2,66},{4,68},{6,70},{8,72},{10,74},{12,76},{14,78},{16,80}... | collective-permute-start | bytes 4718600 | tf_op jit(solution)/shard_map/ppermute | solution.py:353
  96.3 67.7 %copy-start.13 = (bf16[4,12,64,256]{3,2,1,0:T(8,128)(2,1)}, bf16[4,12,64,256]{3,2,1,0:T(8,128)(2,1)S(1)}, u32[]{:S(2)}) copy-start(bf16[4,12,64,256]{3,2,1,0:T(8,128)(2,1)S(1)} %collective-permute-done.8.refs_3_) | copy-start | bytes 4718596
  96.3 59.3 %collective-permute-start.9 = (bf16[4,12,64,256]{3,2,1,0:T(8,128)(2,1)S(1)}, bf16[4,12,64,256]{3,2,1,0:T(8,128)(2,1)S(1)}, u32[]{:S(2)}, u32[]{:S(2)}) collective-permute-start(bf16[4,12,64,256]{3,2,1,0:T(8,128)(2,1)S(1)} %get-tuple-element.78.refs_4_), channel_id=1, source_target_pairs={{0,32},{2,34},{4,36},{6,38},{8,40},{10,42},{12,44},{14,46},{16,48}... | collective-permute-start | bytes 4718600 | tf_op jit(solution)/shard_map/ppermute | solution.py:353
  100.2 63.8 %copy-start.14 = (bf16[4,12,64,256]{3,2,1,0:T(8,128)(2,1)}, bf16[4,12,64,256]{3,2,1,0:T(8,128)(2,1)S(1)}, u32[]{:S(2)}) copy-start(bf16[4,12,64,256]{3,2,1,0:T(8,128)(2,1)S(1)} %collective-permute-done.7.refs_2_) | copy-start | bytes 4718596
  100.2 57.1 %collective-permute-start.18 = (bf16[2,1024,256]{2,1,0:T(8,128)(2,1)S(1)}, bf16[2,1024,256]{2,1,0:T(8,128)(2,1)S(1)}, u32[]{:S(2)}, u32[]{:S(2)}) collective-permute-start(bf16[2,1024,256]{2,1,0:T(8,128)(2,1)S(1)} %collective-permute-done.14.refs_11_.refs_19_), channel_id=1, source_target_pairs={{0,1},{1,0},{2,3},{3,2},{4,5},{5,4},{6,7},{7,6},{8,9},{9,8},{10,11... | collective-permute-start | bytes 3145736 | tf_op jit(solution)/shard_map/ppermute | solution.py:353
  100.3 63.7 %copy-start.15 = (bf16[4,12,64,256]{3,2,1,0:T(8,128)(2,1)}, bf16[4,12,64,256]{3,2,1,0:T(8,128)(2,1)S(1)}, u32[]{:S(2)}) copy-start(bf16[4,12,64,256]{3,2,1,0:T(8,128)(2,1)S(1)} %collective-permute-done.6.refs_1_) | copy-start | bytes 4718596
  100.4 58.7 %collective-permute-start.17 = (bf16[2,1024,256]{2,1,0:T(8,128)(2,1)S(1)}, bf16[2,1024,256]{2,1,0:T(8,128)(2,1)S(1)}, u32[]{:S(2)}, u32[]{:S(2)}) collective-permute-start(bf16[2,1024,256]{2,1,0:T(8,128)(2,1)S(1)} %collective-permute-done.13.refs_10_.refs_18_), channel_id=1, source_target_pairs={{0,1},{1,0},{2,3},{3,2},{4,5},{5,4},{6,7},{7,6},{8,9},{9,8},{10,11... | collective-permute-start | bytes 3145736 | tf_op jit(solution)/shard_map/ppermute | solution.py:353
  101.1 117.8 %copy-start.11 = (bf16[4,8,64,256]{3,2,1,0:T(8,128)(2,1)}, bf16[4,8,64,256]{3,2,1,0:T(8,128)(2,1)S(1)}, u32[]{:S(2)}) copy-start(bf16[4,8,64,256]{3,2,1,0:T(8,128)(2,1)S(1)} %get-tuple-element.82.refs_8_) | copy-start | bytes 3145732
  101.1 117.8 %copy-start.12 = (bf16[4,8,64,256]{3,2,1,0:T(8,128)(2,1)}, bf16[4,8,64,256]{3,2,1,0:T(8,128)(2,1)S(1)}, u32[]{:S(2)}) copy-start(bf16[4,8,64,256]{3,2,1,0:T(8,128)(2,1)S(1)} %get-tuple-element.83.refs_12_) | copy-start | bytes 3145732
  101.1 61.2 %copy-start.16 = (bf16[4,12,64,256]{3,2,1,0:T(8,128)(2,1)}, bf16[4,12,64,256]{3,2,1,0:T(8,128)(2,1)S(1)}, u32[]{:S(2)}) copy-start(bf16[4,12,64,256]{3,2,1,0:T(8,128)(2,1)S(1)} %collective-permute-done.11.refs_7_) | copy-start | bytes 4718596
  101.1 59.5 %collective-permute-start.16 = (bf16[2,1024,256]{2,1,0:T(8,128)(2,1)S(1)}, bf16[2,1024,256]{2,1,0:T(8,128)(2,1)S(1)}, u32[]{:S(2)}, u32[]{:S(2)}) collective-permute-start(bf16[2,1024,256]{2,1,0:T(8,128)(2,1)S(1)} %collective-permute-done.12.refs_9_.refs_17_), channel_id=1, source_target_pairs={{0,1},{1,0},{2,3},{3,2},{4,5},{5,4},{6,7},{7,6},{8,9},{9,8},{10,11... | collective-permute-start | bytes 3145736 | tf_op jit(solution)/shard_map/ppermute | solution.py:353
  116.5 45.8 %collective-permute-start.27 = (bf16[4,8,64,256]{3,2,1,0:T(8,128)(2,1)S(1)}, bf16[4,8,64,256]{3,2,1,0:T(8,128)(2,1)S(1)}, u32[]{:S(2)}, u32[]{:S(2)}) collective-permute-start(bf16[4,8,64,256]{3,2,1,0:T(8,128)(2,1)S(1)} %get-tuple-element.82.refs_8_), channel_id=1, source_target_pairs={{1,25},{3,27},{5,29},{7,31},{9,1},{11,3},{13,5},{15,7},{17,9},{19,... | collective-permute-start | bytes 3145736 | tf_op jit(solution)/shard_map/ppermute | solution.py:353
  155.7 63.3 %collective-permute-start.26 = (bf16[4,8,64,256]{3,2,1,0:T(8,128)(2,1)S(1)}, bf16[4,8,64,256]{3,2,1,0:T(8,128)(2,1)}, u32[]{:S(2)}, u32[]{:S(2)}) collective-permute-start(bf16[4,8,64,256]{3,2,1,0:T(8,128)(2,1)S(1)} %get-tuple-element.82.refs_8_), channel_id=1, source_target_pairs={{1,17},{3,19},{5,21},{7,23},{9,25},{11,27},{13,29},{15,31},{17,1},... | collective-permute-start | bytes 3145736 | tf_op jit(solution)/shard_map/ppermute | solution.py:353
  157.4 61.6 %collective-permute-start.25 = (bf16[4,8,64,256]{3,2,1,0:T(8,128)(2,1)S(1)}, bf16[4,8,64,256]{3,2,1,0:T(8,128)(2,1)}, u32[]{:S(2)}, u32[]{:S(2)}) collective-permute-start(bf16[4,8,64,256]{3,2,1,0:T(8,128)(2,1)S(1)} %get-tuple-element.82.refs_8_), channel_id=1, source_target_pairs={{1,9},{3,11},{5,13},{7,15},{9,17},{11,19},{13,21},{15,23},{17,25},... | collective-permute-start | bytes 3145736 | tf_op jit(solution)/shard_map/ppermute | solution.py:353
  159.0 60.0 %copy-start.6 = (bf16[2,1024,256]{2,1,0:T(8,128)(2,1)}, bf16[2,1024,256]{2,1,0:T(8,128)(2,1)S(1)}, u32[]{:S(2)}) copy-start(bf16[2,1024,256]{2,1,0:T(8,128)(2,1)S(1)} %collective-permute-done.17.refs_14_.refs_22_) | copy-start | bytes 3145732
  159.0 60.0 %collective-permute-start.30 = (bf16[4,8,64,256]{3,2,1,0:T(8,128)(2,1)S(1)}, bf16[4,8,64,256]{3,2,1,0:T(8,128)(2,1)}, u32[]{:S(2)}, u32[]{:S(2)}) collective-permute-start(bf16[4,8,64,256]{3,2,1,0:T(8,128)(2,1)S(1)} %get-tuple-element.83.refs_12_), channel_id=1, source_target_pairs={{1,97},{3,99},{5,101},{7,103},{9,105},{11,107},{13,109},{15,111},{... | collective-permute-start | bytes 3145736 | tf_op jit(solution)/shard_map/ppermute | solution.py:353
  160.6 58.3 %copy-start.7 = (bf16[2,1024,256]{2,1,0:T(8,128)(2,1)}, bf16[2,1024,256]{2,1,0:T(8,128)(2,1)S(1)}, u32[]{:S(2)}) copy-start(bf16[2,1024,256]{2,1,0:T(8,128)(2,1)S(1)} %collective-permute-done.16.refs_13_.refs_21_) | copy-start | bytes 3145732
  160.6 58.4 %collective-permute-start.29 = (bf16[4,8,64,256]{3,2,1,0:T(8,128)(2,1)S(1)}, bf16[4,8,64,256]{3,2,1,0:T(8,128)(2,1)}, u32[]{:S(2)}, u32[]{:S(2)}) collective-permute-start(bf16[4,8,64,256]{3,2,1,0:T(8,128)(2,1)S(1)} %get-tuple-element.83.refs_12_), channel_id=1, source_target_pairs={{1,65},{3,67},{5,69},{7,71},{9,73},{11,75},{13,77},{15,79},{17,81}... | collective-permute-start | bytes 3145736 | tf_op jit(solution)/shard_map/ppermute | solution.py:353
  162.3 56.7 %collective-permute-start.28 = (bf16[4,8,64,256]{3,2,1,0:T(8,128)(2,1)S(1)}, bf16[4,8,64,256]{3,2,1,0:T(8,128)(2,1)}, u32[]{:S(2)}, u32[]{:S(2)}) collective-permute-start(bf16[4,8,64,256]{3,2,1,0:T(8,128)(2,1)S(1)} %get-tuple-element.83.refs_12_), channel_id=1, source_target_pairs={{1,33},{3,35},{5,37},{7,39},{9,41},{11,43},{13,45},{15,47},{17,49}... | collective-permute-start | bytes 3145736 | tf_op jit(solution)/shard_map/ppermute | solution.py:353
  (6 other events, 77.3 us)
where the time goes:
time: 222 us; the launch traced here: 221 us
  waiting for transfers between devices  98.8 us (45%)
  starting transfers between devices  60.7 us (27%)
  Pallas kernels  56.9 us (26%)
    ppermute x31, waiting for transfers between devices, moved(): return lax.ppermute(value, AXES, pairs)  91 us
    ppermute x31, starting transfers between devices, moved(): return lax.ppermute(value, AXES, pairs)  56.1 us
    pallas_call x1, Pallas kernels, shards(): pl.pallas_call(column_kernel, out_shape=outs, in_specs=[smem] + [hbm] * 1...  54.9 us
    all_to_all x1, waiting for transfers between devices, shards(): lax.all_to_all(col_factors, 'cols', split_axis=0, concat_axis=1, tiled=True)  7.86 us
    all_to_all x1, starting transfers between devices, shards(): lax.all_to_all(col_factors, 'cols', split_axis=0, concat_axis=1, tiled=True)  4.61 us
  transfers between devices with their start and end apart: 32, of which 9 were waited for; matrix products, arithmetic and copies ran while one was open for 1% of the time, Pallas kernels for 25%

commit v1 on v0

--- a/solution.py
+++ b/solution.py
@@ -10,6 +10,7 @@
 G = 8
 SIDE = 4
 AXES = ("rows", "cols")
+NEAR = (0, 1, 3, 2)
 COLUMN_GRANT = 46 << 20
 TILE_GRANT = 60 << 20
 
@@ -189,10 +190,12 @@
     pairs = []
     for e in range(SIDE):
         for d in range(SIDE):
-            slab = ((x + SIDE - d) % SIDE) * SIDE + (z + SIDE - e) % SIDE
-            at = pl.ds(pl.multiple_of(slab * 64, 64), 64)
-            pairs.append((fs[e].at[d, pl.ds(first, count)], v_ref.at[pl.ds(first if to is None else to, count), at, :]))
-            pairs.append((gs[d].at[e, pl.ds(first, count)], u_ref.at[pl.ds(first if to is None else to, count), at, :]))
+            for far, near, at_x, at_z, dst in (
+                (e, d, x ^ NEAR[d], (z + SIDE - e) % SIDE, v_ref), (d, e, (x + SIDE - d) % SIDE, z ^ NEAR[e], u_ref)
+            ):
+                at = pl.ds(pl.multiple_of((at_x * SIDE + at_z) * 64, 64), 64)
+                src = fs[far] if dst is v_ref else gs[far]
+                pairs.append((src.at[near, pl.ds(first, count)], dst.at[pl.ds(first if to is None else to, count), at, :]))
     return pairs
 
 
@@ -353,12 +356,12 @@
     return lax.ppermute(value, AXES, pairs)
 
 
-def along(axis, step, parity):
+def along(axis, change, parity):
     pairs = []
     for x in range(SIDE):
         for z in range(SIDE):
             for col in range(parity, 8, 2):
-                to = ((x + step) % SIDE, z) if axis == "x" else (x, (z + step) % SIDE)
+                to = (change(x), z) if axis == "x" else (x, change(z))
                 pairs.append(((x * SIDE + z) * 8 + col, (to[0] * SIDE + to[1]) * 8 + col))
     return pairs
 
@@ -367,21 +370,21 @@
     return [(row * 8 + col, row * 8 + change(col)) for row in range(16) for col in range(8)]
 
 
-def both_ways(a, b, one, two, parity):
+def first_leg(a, b, parity):
+    a, b = a[None], b[None]
+    for change in (lambda p: p ^ 1, lambda p: p ^ 3):
+        got_a = moved(a, along("x", change, parity))
+        got_b = moved(b, along("z", change, parity))
+        a, b = jnp.concatenate([a, got_a]), jnp.concatenate([b, got_b])
+    return a, b
+
+
+def second_leg(a, b, parity):
     got_a, got_b = [a, None, None, None], [b, None, None, None]
-    for d in (1, 3, 2):
-        got_a[d] = moved(a, along(one, d, parity))
-        got_b[d] = moved(b, along(two, d, parity))
+    for d in (1, 2, 3):
+        got_a[d] = moved(a, along("z", lambda p: (p + d) % SIDE, parity))
+        got_b[d] = moved(b, along("x", lambda p: (p + d) % SIDE, parity))
     return got_a, got_b
-
-
-def first_leg(first, second, parity):
-    return both_ways(first, second, "x", "z", parity)
-
-
-def second_leg(a, b, parity):
-    a, b = lax.optimization_barrier((jnp.stack(a), jnp.stack(b)))
-    return both_ways(a, b, "z", "x", parity)
 
 
 def shards(band, diag, row_factors, row_ranks, col_factors, col_ranks):
@@ -403,7 +406,9 @@
     high = rounded.astype(jnp.bfloat16)
     low = (pieces - rounded).astype(jnp.bfloat16)
     own, mine, meta, high, low = lax.optimization_barrier((own, mine, meta, high, low))
-    near = [mine] + [moved(mine, across(lambda c, d=d: ((c // 2 + d) % SIDE) * 2 + c % 2)) for d in (1, 2, 3)]
+    near = [mine]
+    for d in (1, 2, 3):
+        near.append(moved(mine, across(lambda c: ((c // 2 + d) % SIDE) * 2 + c % 2)))
     sides, bases = own[:, 1], own[:, 0]
     a, b = lax.optimization_barrier(first_leg(jnp.concatenate([sides, high]), jnp.concatenate([bases, low]), 0))
     fs, gs = second_leg(a, b, 0)

time: 222 us -> 224 us (level)
  the two profiles are of different devices: /device:TPU:4 before, /device:TPU:32 now
where the time goes in v1:
time: 224 us; the launch traced here: 223 us
  waiting for transfers between devices  105 us (47%)
  Pallas kernels  56.7 us (25%)
  starting transfers between devices  53.7 us (24%)
  local copies, waits for them, and re-layouts  4.51 us (2%)
    ppermute x27, waiting for transfers between devices, moved(): return lax.ppermute(value, AXES, pairs)  96.9 us
    pallas_call x1, Pallas kernels, shards(): pl.pallas_call(column_kernel, out_shape=outs, in_specs=[smem] + [hbm] * 1...  54.7 us
    ppermute x27, starting transfers between devices, moved(): return lax.ppermute(value, AXES, pairs)  49.1 us
    all_to_all x1, waiting for transfers between devices, shards(): lax.all_to_all(col_factors, 'cols', split_axis=0, concat_axis=1, tiled=True)  7.86 us
    all_to_all x1, starting transfers between devices, shards(): lax.all_to_all(col_factors, 'cols', split_axis=0, concat_axis=1, tiled=True)  4.61 us
  transfers between devices with their start and end apart: 28, of which 11 were waited for; matrix products, arithmetic and copies ran while one was open for 1% of the time, Pallas kernels for 25%

profile of v1, /device:TPU:32, one launch (start us, length us, event | category | flops | bytes accessed | tf_op | source)
XLA Modules:
  0.0 222.9 jit_solution(778455674289736108)
XLA Ops:
  0.7 4.6 %all-to-all-start = ((bf16[8,1,2,64,256]{4,3,2,1,0:T(8,128)(2,1)}), bf16[8,1,2,64,256]{4,3,2,1,0:T(8,128)(2,1)S(1)}, u32[]{:S(2)}, u32[]{:S(2)}) async-start(bf16[8,1,2,64,256]{4,3,2,1,0:T(8,128)(2,1)} %param.10), calls=%async_computation | async-start | bytes 1048576 | tf_op jit(solution)/shard_map/all_to_all | solution.py:403
  5.9 1.1 reshape_squeeze.7
  7.1 0.2 copy.16
  7.3 0.1 broadcast_select_fusion
  7.5 0.1 concatenate.37.meta
  7.6 0.1 pad_maximum_fusion.2.refs_8_.refs_16_
  7.7 7.9 %all-to-all-done = bf16[8,1,2,64,256]{4,3,2,1,0:T(8,128)(2,1)S(1)} async-done(((bf16[8,1,2,64,256]{4,3,2,1,0:T(8,128)(2,1)}), bf16[8,1,2,64,256]{4,3,2,1,0:T(8,128)(2,1)S(1)}, u32[]{:S(2)}, u32[]{:S(2)}) %all-to-all-start) | async-done | bytes 524320 | tf_op jit(solution)/shard_map/all_to_all | solution.py:403
  15.8 3.4 %collective-permute-start = (bf16[1,12,64,256]{3,2,1,0:T(8,128)(2,1)S(1)}, bf16[1,12,64,256]{3,2,1,0:T(8,128)(2,1)S(1)}, u32[]{:S(2)}, u32[]{:S(2)}) collective-permute-start(bf16[1,12,64,256]{3,2,1,0:T(8,128)(2,1)S(1)} %maximum_bitcast_fusion), channel_id=1, source_target_pairs={{0,32},{2,34},{4,36},{6,38},{8,40},{10,42},{12,44},{14,46},{16,48}... | collective-permute-start | bytes 1179656 | tf_op jit(solution)/shard_map/ppermute | solution.py:356
  19.2 2.0 collective-permute-start.2
  21.2 0.7 collective-permute-start.19
  21.9 3.5 %collective-permute-done = bf16[1,12,64,256]{3,2,1,0:T(8,128)(2,1)S(1)} collective-permute-done((bf16[1,12,64,256]{3,2,1,0:T(8,128)(2,1)S(1)}, bf16[1,12,64,256]{3,2,1,0:T(8,128)(2,1)S(1)}, u32[]{:S(2)}, u32[]{:S(2)}) %collective-permute-start) | collective-permute-done | bytes 393248 | tf_op jit(solution)/shard_map/ppermute | solution.py:356
  25.5 4.7 %collective-permute-start.1 = (bf16[2,12,64,256]{3,2,1,0:T(8,128)(2,1)S(1)}, bf16[2,12,64,256]{3,2,1,0:T(8,128)(2,1)S(1)}, u32[]{:S(2)}, u32[]{:S(2)}) collective-permute-start(bf16[2,12,64,256]{3,2,1,0:T(8,128)(2,1)S(1)} %pad_maximum_fusion.5), channel_id=1, source_target_pairs={{0,96},{2,98},{4,100},{6,102},{8,104},{10,106},{12,108},{14,110},{... | collective-permute-start | bytes 2359304 | tf_op jit(solution)/shard_map/ppermute | solution.py:356
  30.3 3.8 %collective-permute-start.3 = (bf16[2,12,64,256]{3,2,1,0:T(8,128)(2,1)S(1)}, bf16[2,12,64,256]{3,2,1,0:T(8,128)(2,1)S(1)}, u32[]{:S(2)}, u32[]{:S(2)}) collective-permute-start(bf16[2,12,64,256]{3,2,1,0:T(8,128)(2,1)S(1)} %pad_maximum_fusion.6), channel_id=1, source_target_pairs={{0,24},{2,26},{4,28},{6,30},{8,16},{10,18},{12,20},{14,22},{16,8},... | collective-permute-start | bytes 2359304 | tf_op jit(solution)/shard_map/ppermute | solution.py:356
  34.2 0.7 collective-permute-start.20
  34.9 0.7 collective-permute-start.17
  35.6 1.2 collective-permute-start.12
  36.8 1.5 collective-permute-start.11
  38.4 2.2 collective-permute-done.1
  40.6 0.7 collective-permute-start.18
  41.3 2.9 %collective-permute-done.3 = bf16[2,12,64,256]{3,2,1,0:T(8,128)(2,1)S(1)} collective-permute-done((bf16[2,12,64,256]{3,2,1,0:T(8,128)(2,1)S(1)}, bf16[2,12,64,256]{3,2,1,0:T(8,128)(2,1)S(1)}, u32[]{:S(2)}, u32[]{:S(2)}) %collective-permute-start.3) | collective-permute-done | bytes 786464 | tf_op jit(solution)/shard_map/ppermute | solution.py:356
  44.2 0.2 pad_maximum_fusion.refs_0_
  44.3 0.2 pad_maximum_fusion.1.refs_4_
  44.5 4.0 %collective-permute-start.6 = (bf16[4,12,64,256]{3,2,1,0:T(8,128)(2,1)S(1)}, bf16[4,12,64,256]{3,2,1,0:T(8,128)(2,1)S(1)}, u32[]{:S(2)}, u32[]{:S(2)}) collective-permute-start(bf16[4,12,64,256]{3,2,1,0:T(8,128)(2,1)S(1)} %pad_maximum_fusion.refs_0_), channel_id=1, source_target_pairs={{0,24},{2,26},{4,28},{6,30},{8,0},{10,2},{12,4},{14,6},{16,8},{18,... | collective-permute-start | bytes 4718600 | tf_op jit(solution)/shard_map/ppermute | solution.py:356
  48.6 13.1 %collective-permute-done.12.refs_11_.refs_19_ = bf16[2,1024,256]{2,1,0:T(8,128)(2,1)S(1)} collective-permute-done((bf16[2,1024,256]{2,1,0:T(8,128)(2,1)S(1)}, bf16[2,1024,256]{2,1,0:T(8,128)(2,1)S(1)}, u32[]{:S(2)}, u32[]{:S(2)}) %collective-permute-start.12) | collective-permute-done | bytes 1048608 | tf_op jit(solution)/shard_map/ppermute | solution.py:356
  61.7 2.7 %collective-permute-done.11.refs_10_.refs_18_ = bf16[2,1024,256]{2,1,0:T(8,128)(2,1)S(1)} collective-permute-done((bf16[2,1024,256]{2,1,0:T(8,128)(2,1)S(1)}, bf16[2,1024,256]{2,1,0:T(8,128)(2,1)S(1)}, u32[]{:S(2)}, u32[]{:S(2)}) %collective-permute-start.11) | collective-permute-done | bytes 1048608 | tf_op jit(solution)/shard_map/ppermute | solution.py:356
  64.4 19.9 %collective-permute-done.10.refs_9_.refs_17_ = bf16[2,1024,256]{2,1,0:T(8,128)(2,1)S(1)} collective-permute-done((bf16[2,1024,256]{2,1,0:T(8,128)(2,1)S(1)}, bf16[2,1024,256]{2,1,0:T(8,128)(2,1)S(1)}, u32[]{:S(2)}, u32[]{:S(2)}) %collective-permute-start.10) | collective-permute-done | bytes 1048608 | tf_op jit(solution)/shard_map/ppermute | solution.py:356
  84.3 3.3 %collective-permute-start.5 = (bf16[4,12,64,256]{3,2,1,0:T(8,128)(2,1)S(1)}, bf16[4,12,64,256]{3,2,1,0:T(8,128)(2,1)S(1)}, u32[]{:S(2)}, u32[]{:S(2)}) collective-permute-start(bf16[4,12,64,256]{3,2,1,0:T(8,128)(2,1)S(1)} %pad_maximum_fusion.refs_0_), channel_id=1, source_target_pairs={{0,16},{2,18},{4,20},{6,22},{8,24},{10,26},{12,28},{14,30},{16,0},... | collective-permute-start | bytes 4718600 | tf_op jit(solution)/shard_map/ppermute | solution.py:356
  87.6 4.2 %collective-permute-start.4 = (bf16[4,12,64,256]{3,2,1,0:T(8,128)(2,1)S(1)}, bf16[4,12,64,256]{3,2,1,0:T(8,128)(2,1)S(1)}, u32[]{:S(2)}, u32[]{:S(2)}) collective-permute-start(bf16[4,12,64,256]{3,2,1,0:T(8,128)(2,1)S(1)} %pad_maximum_fusion.refs_0_), channel_id=1, source_target_pairs={{0,8},{2,10},{4,12},{6,14},{8,16},{10,18},{12,20},{14,22},{16,24},... | collective-permute-start | bytes 4718600 | tf_op jit(solution)/shard_map/ppermute | solution.py:356
  91.8 4.6 %collective-permute-start.9 = (bf16[4,12,64,256]{3,2,1,0:T(8,128)(2,1)S(1)}, bf16[4,12,64,256]{3,2,1,0:T(8,128)(2,1)S(1)}, u32[]{:S(2)}, u32[]{:S(2)}) collective-permute-start(bf16[4,12,64,256]{3,2,1,0:T(8,128)(2,1)S(1)} %pad_maximum_fusion.1.refs_4_), channel_id=1, source_target_pairs={{0,96},{2,98},{4,100},{6,102},{8,104},{10,106},{12,108},{14,110},{... | collective-permute-start | bytes 4718600 | tf_op jit(solution)/shard_map/ppermute | solution.py:356
  96.5 3.0 %collective-permute-start.8 = (bf16[4,12,64,256]{3,2,1,0:T(8,128)(2,1)S(1)}, bf16[4,12,64,256]{3,2,1,0:T(8,128)(2,1)S(1)}, u32[]{:S(2)}, u32[]{:S(2)}) collective-permute-start(bf16[4,12,64,256]{3,2,1,0:T(8,128)(2,1)S(1)} %pad_maximum_fusion.1.refs_4_), channel_id=1, source_target_pairs={{0,64},{2,66},{4,68},{6,70},{8,72},{10,74},{12,76},{14,78},{16,80}... | collective-permute-start | bytes 4718600 | tf_op jit(solution)/shard_map/ppermute | solution.py:356
  99.5 2.5 %collective-permute-start.7 = (bf16[4,12,64,256]{3,2,1,0:T(8,128)(2,1)S(1)}, bf16[4,12,64,256]{3,2,1,0:T(8,128)(2,1)S(1)}, u32[]{:S(2)}, u32[]{:S(2)}) collective-permute-start(bf16[4,12,64,256]{3,2,1,0:T(8,128)(2,1)S(1)} %pad_maximum_fusion.1.refs_4_), channel_id=1, source_target_pairs={{0,32},{2,34},{4,36},{6,38},{8,40},{10,42},{12,44},{14,46},{16,48}... | collective-permute-start | bytes 4718600 | tf_op jit(solution)/shard_map/ppermute | solution.py:356
  102.0 0.1 pad_maximum_fusion.4.refs_12_
  102.1 0.1 pad_maximum_fusion.3.refs_8_
  102.3 20.9 %collective-permute-done.5.refs_2_ = bf16[4,12,64,256]{3,2,1,0:T(8,128)(2,1)S(1)} collective-permute-done((bf16[4,12,64,256]{3,2,1,0:T(8,128)(2,1)S(1)}, bf16[4,12,64,256]{3,2,1,0:T(8,128)(2,1)S(1)}, u32[]{:S(2)}, u32[]{:S(2)}) %collective-permute-start.5) | collective-permute-done | bytes 1572896 | tf_op jit(solution)/shard_map/ppermute | solution.py:356
  123.1 0.7 collective-permute-start.23
  123.8 22.5 %collective-permute-done.4.refs_1_ = bf16[4,12,64,256]{3,2,1,0:T(8,128)(2,1)S(1)} collective-permute-done((bf16[4,12,64,256]{3,2,1,0:T(8,128)(2,1)S(1)}, bf16[4,12,64,256]{3,2,1,0:T(8,128)(2,1)S(1)}, u32[]{:S(2)}, u32[]{:S(2)}) %collective-permute-start.4) | collective-permute-done | bytes 1572896 | tf_op jit(solution)/shard_map/ppermute | solution.py:356
  146.3 0.7 collective-permute-start.22
  147.0 6.7 %collective-permute-done.9.refs_7_ = bf16[4,12,64,256]{3,2,1,0:T(8,128)(2,1)S(1)} collective-permute-done((bf16[4,12,64,256]{3,2,1,0:T(8,128)(2,1)S(1)}, bf16[4,12,64,256]{3,2,1,0:T(8,128)(2,1)S(1)}, u32[]{:S(2)}, u32[]{:S(2)}) %collective-permute-start.9) | collective-permute-done | bytes 1572896 | tf_op jit(solution)/shard_map/ppermute | solution.py:356
  153.7 1.6 collective-permute-start.21
  155.4 1.6 collective-permute-start.26
  157.0 2.6 %collective-permute-done.7.refs_5_ = bf16[4,12,64,256]{3,2,1,0:T(8,128)(2,1)S(1)} collective-permute-done((bf16[4,12,64,256]{3,2,1,0:T(8,128)(2,1)S(1)}, bf16[4,12,64,256]{3,2,1,0:T(8,128)(2,1)S(1)}, u32[]{:S(2)}, u32[]{:S(2)}) %collective-permute-start.7) | collective-permute-done | bytes 1572896 | tf_op jit(solution)/shard_map/ppermute | solution.py:356
  159.6 1.6 collective-permute-start.25
  161.3 1.6 collective-permute-start.24
  163.0 54.7 %column.1 = (f32[1024,1024]{1,0:T(8,128)}, f32[64,1024]{1,0:T(8,128)}) custom-call(s32[12]{0:T(128)S(1)} %concatenate.37.meta, bf16[4,12,64,256]{3,2,1,0:T(8,128)(2,1)} %copy-done.9, bf16[4,12,64,256]{3,2,1,0:T(8,128)(2,1)} %copy-done.15, bf16[4,12,64,256]{3,2,1,0:T(8,128)(2,1)} %copy-done.14, bf16[4,12,64,256]{3,2,1,0:T(8,128)(2,1)} %copy-done.13, ...), custom_call_target="tpu_custom_call" | custom-call | flops 60000002048 | bytes 20000000 | tf_op jit(solution)/shard_map/column/pallas_call | solution.py:425
  217.8 1.0 copy-done.6
  218.7 1.0 copy-done.7
  219.7 1.0 copy-done.21
  220.7 2.0 tile.1
  (77 shorter events, 0.8 us)
Async XLA Ops:
  0.6 6.8 %copy-start = (s32[8,8]{1,0:T(8,128)S(1)}, s32[8,8]{1,0:T(8,128)}, u32[]{:S(2)}) copy-start(s32[8,8]{1,0:T(8,128)} %param.11) | copy-start | bytes 772
  0.6 6.4 %copy-start.22 = (bf16[1,1,2,1024,256]{4,3,2,1,0:T(8,128)(2,1)S(1)}, bf16[1,1,2,1024,256]{4,3,2,1,0:T(8,128)(2,1)}, u32[]{:S(2)}) copy-start(bf16[1,1,2,1024,256]{4,3,2,1,0:T(8,128)(2,1)} %param.8) | copy-start | bytes 3145732
  0.7 14.9 %all-to-all-start = ((bf16[8,1,2,64,256]{4,3,2,1,0:T(8,128)(2,1)}), bf16[8,1,2,64,256]{4,3,2,1,0:T(8,128)(2,1)S(1)}, u32[]{:S(2)}, u32[]{:S(2)}) async-start(bf16[8,1,2,64,256]{4,3,2,1,0:T(8,128)(2,1)} %param.10), calls=%async_computation | async-start | bytes 1048576 | tf_op jit(solution)/shard_map/all_to_all | solution.py:403
  7.5 155.4 %copy-start.8 = (s32[12]{0:T(128)}, s32[12]{0:T(128)S(1)}, u32[]{:S(2)}) copy-start(s32[12]{0:T(128)S(1)} %concatenate.37.meta) | copy-start | bytes 148
  7.7 155.3 %copy-start.1 = (bf16[2,1024,256]{2,1,0:T(8,128)(2,1)}, bf16[2,1024,256]{2,1,0:T(8,128)(2,1)S(1)}, u32[]{:S(2)}) copy-start(bf16[2,1024,256]{2,1,0:T(8,128)(2,1)S(1)} %pad_maximum_fusion.2.refs_8_.refs_16_) | copy-start | bytes 3145732
  15.8 9.7 %collective-permute-start = (bf16[1,12,64,256]{3,2,1,0:T(8,128)(2,1)S(1)}, bf16[1,12,64,256]{3,2,1,0:T(8,128)(2,1)S(1)}, u32[]{:S(2)}, u32[]{:S(2)}) collective-permute-start(bf16[1,12,64,256]{3,2,1,0:T(8,128)(2,1)S(1)} %maximum_bitcast_fusion), channel_id=1, source_target_pairs={{0,32},{2,34},{4,36},{6,38},{8,40},{10,42},{12,44},{14,46},{16,48}... | collective-permute-start | bytes 1179656 | tf_op jit(solution)/shard_map/ppermute | solution.py:356
  19.2 11.0 %collective-permute-start.2 = (bf16[1,12,64,256]{3,2,1,0:T(8,128)(2,1)S(1)}, bf16[1,12,64,256]{3,2,1,0:T(8,128)(2,1)S(1)}, u32[]{:S(2)}, u32[]{:S(2)}) collective-permute-start(bf16[1,12,64,256]{3,2,1,0:T(8,128)(2,1)S(1)} %maximum_bitcast_fusion.1), channel_id=1, source_target_pairs={{0,8},{2,10},{4,12},{6,14},{8,0},{10,2},{12,4},{14,6},{16,24},{18,... | collective-permute-start | bytes 1179656 | tf_op jit(solution)/shard_map/ppermute | solution.py:356
  21.2 12.9 %collective-permute-start.19 = (bf16[1,8,64,256]{3,2,1,0:T(8,128)(2,1)S(1)}, bf16[1,8,64,256]{3,2,1,0:T(8,128)(2,1)S(1)}, u32[]{:S(2)}, u32[]{:S(2)}) collective-permute-start(bf16[1,8,64,256]{3,2,1,0:T(8,128)(2,1)S(1)} %get-tuple-element.66), channel_id=1, source_target_pairs={{1,9},{3,11},{5,13},{7,15},{9,1},{11,3},{13,5},{15,7},{17,25},{19,... | collective-permute-start | bytes 786440 | tf_op jit(solution)/shard_map/ppermute | solution.py:356
  25.5 15.1 %collective-permute-start.1 = (bf16[2,12,64,256]{3,2,1,0:T(8,128)(2,1)S(1)}, bf16[2,12,64,256]{3,2,1,0:T(8,128)(2,1)S(1)}, u32[]{:S(2)}, u32[]{:S(2)}) collective-permute-start(bf16[2,12,64,256]{3,2,1,0:T(8,128)(2,1)S(1)} %pad_maximum_fusion.5), channel_id=1, source_target_pairs={{0,96},{2,98},{4,100},{6,102},{8,104},{10,106},{12,108},{14,110},{... | collective-permute-start | bytes 2359304 | tf_op jit(solution)/shard_map/ppermute | solution.py:356
  30.3 13.9 %collective-permute-start.3 = (bf16[2,12,64,256]{3,2,1,0:T(8,128)(2,1)S(1)}, bf16[2,12,64,256]{3,2,1,0:T(8,128)(2,1)S(1)}, u32[]{:S(2)}, u32[]{:S(2)}) collective-permute-start(bf16[2,12,64,256]{3,2,1,0:T(8,128)(2,1)S(1)} %pad_maximum_fusion.6), channel_id=1, source_target_pairs={{0,24},{2,26},{4,28},{6,30},{8,16},{10,18},{12,20},{14,22},{16,8},... | collective-permute-start | bytes 2359304 | tf_op jit(solution)/shard_map/ppermute | solution.py:356
  34.2 4.1 %collective-permute-start.20 = (bf16[2,8,64,256]{3,2,1,0:T(8,128)(2,1)S(1)}, bf16[2,8,64,256]{3,2,1,0:T(8,128)(2,1)S(1)}, u32[]{:S(2)}, u32[]{:S(2)}) collective-permute-start(bf16[2,8,64,256]{3,2,1,0:T(8,128)(2,1)S(1)} %pad_maximum_fusion.8), channel_id=1, source_target_pairs={{1,25},{3,27},{5,29},{7,31},{9,17},{11,19},{13,21},{15,23},{17,9},... | collective-permute-start | bytes 1572872 | tf_op jit(solution)/shard_map/ppermute | solution.py:356
  34.9 1.9 collective-permute-start.17
  35.6 26.1 %collective-permute-start.12 = (bf16[2,1024,256]{2,1,0:T(8,128)(2,1)S(1)}, bf16[2,1024,256]{2,1,0:T(8,128)(2,1)S(1)}, u32[]{:S(2)}, u32[]{:S(2)}) collective-permute-start(bf16[2,1024,256]{2,1,0:T(8,128)(2,1)S(1)} %pad_maximum_fusion.2.refs_8_.refs_16_), channel_id=1, source_target_pairs={{0,6},{1,7},{2,0},{3,1},{4,2},{5,3},{6,4},{7,5},{8,14},{9,15},{10,... | collective-permute-start | bytes 3145736 | tf_op jit(solution)/shard_map/ppermute | solution.py:356
  36.8 27.6 %collective-permute-start.11 = (bf16[2,1024,256]{2,1,0:T(8,128)(2,1)S(1)}, bf16[2,1024,256]{2,1,0:T(8,128)(2,1)S(1)}, u32[]{:S(2)}, u32[]{:S(2)}) collective-permute-start(bf16[2,1024,256]{2,1,0:T(8,128)(2,1)S(1)} %pad_maximum_fusion.2.refs_8_.refs_16_), channel_id=1, source_target_pairs={{0,4},{1,5},{2,6},{3,7},{4,0},{5,1},{6,2},{7,3},{8,12},{9,13},{10,... | collective-permute-start | bytes 3145736 | tf_op jit(solution)/shard_map/ppermute | solution.py:356
  38.3 45.9 %collective-permute-start.10 = (bf16[2,1024,256]{2,1,0:T(8,128)(2,1)S(1)}, bf16[2,1024,256]{2,1,0:T(8,128)(2,1)S(1)}, u32[]{:S(2)}, u32[]{:S(2)}) collective-permute-start(bf16[2,1024,256]{2,1,0:T(8,128)(2,1)S(1)} %pad_maximum_fusion.2.refs_8_.refs_16_), channel_id=1, source_target_pairs={{0,2},{1,3},{2,4},{3,5},{4,6},{5,7},{6,0},{7,1},{8,10},{9,11},{10,... | collective-permute-start | bytes 3145736 | tf_op jit(solution)/shard_map/ppermute | solution.py:356
  40.6 3.9 %collective-permute-start.18 = (bf16[2,8,64,256]{3,2,1,0:T(8,128)(2,1)S(1)}, bf16[2,8,64,256]{3,2,1,0:T(8,128)(2,1)S(1)}, u32[]{:S(2)}, u32[]{:S(2)}) collective-permute-start(bf16[2,8,64,256]{3,2,1,0:T(8,128)(2,1)S(1)} %pad_maximum_fusion.7), channel_id=1, source_target_pairs={{1,97},{3,99},{5,101},{7,103},{9,105},{11,107},{13,109},{15,111},{... | collective-permute-start | bytes 1572872 | tf_op jit(solution)/shard_map/ppermute | solution.py:356
  44.2 40.1 %collective-permute-start.13 = (bf16[2,1024,256]{2,1,0:T(8,128)(2,1)S(1)}, bf16[2,1024,256]{2,1,0:T(8,128)(2,1)S(1)}, u32[]{:S(2)}, u32[]{:S(2)}) collective-permute-start(bf16[2,1024,256]{2,1,0:T(8,128)(2,1)S(1)} %pad_maximum_fusion.2.refs_8_.refs_16_), channel_id=1, source_target_pairs={{0,1},{1,0},{2,3},{3,2},{4,5},{5,4},{6,7},{7,6},{8,9},{9,8},{10,11... | collective-permute-start | bytes 3145736 | tf_op jit(solution)/shard_map/ppermute | solution.py:356
  44.3 43.3 %copy-start.9 = (bf16[4,12,64,256]{3,2,1,0:T(8,128)(2,1)}, bf16[4,12,64,256]{3,2,1,0:T(8,128)(2,1)S(1)}, u32[]{:S(2)}) copy-start(bf16[4,12,64,256]{3,2,1,0:T(8,128)(2,1)S(1)} %pad_maximum_fusion.refs_0_) | copy-start | bytes 4718596
  44.5 118.5 %copy-start.10 = (bf16[4,12,64,256]{3,2,1,0:T(8,128)(2,1)}, bf16[4,12,64,256]{3,2,1,0:T(8,128)(2,1)S(1)}, u32[]{:S(2)}) copy-start(bf16[4,12,64,256]{3,2,1,0:T(8,128)(2,1)S(1)} %pad_maximum_fusion.1.refs_4_) | copy-start | bytes 4718596
  44.5 55.0 %collective-permute-start.6 = (bf16[4,12,64,256]{3,2,1,0:T(8,128)(2,1)S(1)}, bf16[4,12,64,256]{3,2,1,0:T(8,128)(2,1)S(1)}, u32[]{:S(2)}, u32[]{:S(2)}) collective-permute-start(bf16[4,12,64,256]{3,2,1,0:T(8,128)(2,1)S(1)} %pad_maximum_fusion.refs_0_), channel_id=1, source_target_pairs={{0,24},{2,26},{4,28},{6,30},{8,0},{10,2},{12,4},{14,6},{16,8},{18,... | collective-permute-start | bytes 4718600 | tf_op jit(solution)/shard_map/ppermute | solution.py:356
  61.7 101.3 %copy-start.2 = (bf16[2,1024,256]{2,1,0:T(8,128)(2,1)}, bf16[2,1024,256]{2,1,0:T(8,128)(2,1)S(1)}, u32[]{:S(2)}) copy-start(bf16[2,1024,256]{2,1,0:T(8,128)(2,1)S(1)} %collective-permute-done.12.refs_11_.refs_19_) | copy-start | bytes 3145732
  61.7 25.9 %collective-permute-start.16 = (bf16[2,1024,256]{2,1,0:T(8,128)(2,1)S(1)}, bf16[2,1024,256]{2,1,0:T(8,128)(2,1)S(1)}, u32[]{:S(2)}, u32[]{:S(2)}) collective-permute-start(bf16[2,1024,256]{2,1,0:T(8,128)(2,1)S(1)} %collective-permute-done.12.refs_11_.refs_19_), channel_id=1, source_target_pairs={{0,1},{1,0},{2,3},{3,2},{4,5},{5,4},{6,7},{7,6},{8,9},{9,8},{10,11... | collective-permute-start | bytes 3145736 | tf_op jit(solution)/shard_map/ppermute | solution.py:356
  64.3 98.6 %copy-start.3 = (bf16[2,1024,256]{2,1,0:T(8,128)(2,1)}, bf16[2,1024,256]{2,1,0:T(8,128)(2,1)S(1)}, u32[]{:S(2)}) copy-start(bf16[2,1024,256]{2,1,0:T(8,128)(2,1)S(1)} %collective-permute-done.11.refs_10_.refs_18_) | copy-start | bytes 3145732
  64.4 27.5 %collective-permute-start.15 = (bf16[2,1024,256]{2,1,0:T(8,128)(2,1)S(1)}, bf16[2,1024,256]{2,1,0:T(8,128)(2,1)S(1)}, u32[]{:S(2)}, u32[]{:S(2)}) collective-permute-start(bf16[2,1024,256]{2,1,0:T(8,128)(2,1)S(1)} %collective-permute-done.11.refs_10_.refs_18_), channel_id=1, source_target_pairs={{0,1},{1,0},{2,3},{3,2},{4,5},{5,4},{6,7},{7,6},{8,9},{9,8},{10,11... | collective-permute-start | bytes 3145736 | tf_op jit(solution)/shard_map/ppermute | solution.py:356
  84.3 78.7 %copy-start.4 = (bf16[2,1024,256]{2,1,0:T(8,128)(2,1)}, bf16[2,1024,256]{2,1,0:T(8,128)(2,1)S(1)}, u32[]{:S(2)}) copy-start(bf16[2,1024,256]{2,1,0:T(8,128)(2,1)S(1)} %collective-permute-done.10.refs_9_.refs_17_) | copy-start | bytes 3145732
  84.3 12.2 %collective-permute-start.14 = (bf16[2,1024,256]{2,1,0:T(8,128)(2,1)S(1)}, bf16[2,1024,256]{2,1,0:T(8,128)(2,1)S(1)}, u32[]{:S(2)}, u32[]{:S(2)}) collective-permute-start(bf16[2,1024,256]{2,1,0:T(8,128)(2,1)S(1)} %collective-permute-done.10.refs_9_.refs_17_), channel_id=1, source_target_pairs={{0,1},{1,0},{2,3},{3,2},{4,5},{5,4},{6,7},{7,6},{8,9},{9,8},{10,11... | collective-permute-start | bytes 3145736 | tf_op jit(solution)/shard_map/ppermute | solution.py:356
  84.3 78.7 %copy-start.5 = (bf16[2,1024,256]{2,1,0:T(8,128)(2,1)}, bf16[2,1024,256]{2,1,0:T(8,128)(2,1)S(1)}, u32[]{:S(2)}) copy-start(bf16[2,1024,256]{2,1,0:T(8,128)(2,1)S(1)} %collective-permute-done.13.refs_12_.refs_20_) | copy-start | bytes 3145732
  84.3 38.8 %collective-permute-start.5 = (bf16[4,12,64,256]{3,2,1,0:T(8,128)(2,1)S(1)}, bf16[4,12,64,256]{3,2,1,0:T(8,128)(2,1)S(1)}, u32[]{:S(2)}, u32[]{:S(2)}) collective-permute-start(bf16[4,12,64,256]{3,2,1,0:T(8,128)(2,1)S(1)} %pad_maximum_fusion.refs_0_), channel_id=1, source_target_pairs={{0,16},{2,18},{4,20},{6,22},{8,24},{10,26},{12,28},{14,30},{16,0},... | collective-permute-start | bytes 4718600 | tf_op jit(solution)/shard_map/ppermute | solution.py:356
  87.6 11.9 %copy-start.19 = (bf16[2,1024,256]{2,1,0:T(8,128)(2,1)}, bf16[2,1024,256]{2,1,0:T(8,128)(2,1)S(1)}, u32[]{:S(2)}) copy-start(bf16[2,1024,256]{2,1,0:T(8,128)(2,1)S(1)} %collective-permute-done.16.refs_15_.refs_23_) | copy-start | bytes 3145732
  87.6 58.7 %collective-permute-start.4 = (bf16[4,12,64,256]{3,2,1,0:T(8,128)(2,1)S(1)}, bf16[4,12,64,256]{3,2,1,0:T(8,128)(2,1)S(1)}, u32[]{:S(2)}, u32[]{:S(2)}) collective-permute-start(bf16[4,12,64,256]{3,2,1,0:T(8,128)(2,1)S(1)} %pad_maximum_fusion.refs_0_), channel_id=1, source_target_pairs={{0,8},{2,10},{4,12},{6,14},{8,16},{10,18},{12,20},{14,22},{16,24},... | collective-permute-start | bytes 4718600 | tf_op jit(solution)/shard_map/ppermute | solution.py:356
  91.8 61.9 %collective-permute-start.9 = (bf16[4,12,64,256]{3,2,1,0:T(8,128)(2,1)S(1)}, bf16[4,12,64,256]{3,2,1,0:T(8,128)(2,1)S(1)}, u32[]{:S(2)}, u32[]{:S(2)}) collective-permute-start(bf16[4,12,64,256]{3,2,1,0:T(8,128)(2,1)S(1)} %pad_maximum_fusion.1.refs_4_), channel_id=1, source_target_pairs={{0,96},{2,98},{4,100},{6,102},{8,104},{10,106},{12,108},{14,110},{... | collective-permute-start | bytes 4718600 | tf_op jit(solution)/shard_map/ppermute | solution.py:356
  96.5 58.9 %collective-permute-start.8 = (bf16[4,12,64,256]{3,2,1,0:T(8,128)(2,1)S(1)}, bf16[4,12,64,256]{3,2,1,0:T(8,128)(2,1)S(1)}, u32[]{:S(2)}, u32[]{:S(2)}) collective-permute-start(bf16[4,12,64,256]{3,2,1,0:T(8,128)(2,1)S(1)} %pad_maximum_fusion.1.refs_4_), channel_id=1, source_target_pairs={{0,64},{2,66},{4,68},{6,70},{8,72},{10,74},{12,76},{14,78},{16,80}... | collective-permute-start | bytes 4718600 | tf_op jit(solution)/shard_map/ppermute | solution.py:356
  99.5 63.5 %copy-start.13 = (bf16[4,12,64,256]{3,2,1,0:T(8,128)(2,1)}, bf16[4,12,64,256]{3,2,1,0:T(8,128)(2,1)S(1)}, u32[]{:S(2)}) copy-start(bf16[4,12,64,256]{3,2,1,0:T(8,128)(2,1)S(1)} %collective-permute-done.6.refs_3_) | copy-start | bytes 4718596
  99.5 60.1 %collective-permute-start.7 = (bf16[4,12,64,256]{3,2,1,0:T(8,128)(2,1)S(1)}, bf16[4,12,64,256]{3,2,1,0:T(8,128)(2,1)S(1)}, u32[]{:S(2)}, u32[]{:S(2)}) collective-permute-start(bf16[4,12,64,256]{3,2,1,0:T(8,128)(2,1)S(1)} %pad_maximum_fusion.1.refs_4_), channel_id=1, source_target_pairs={{0,32},{2,34},{4,36},{6,38},{8,40},{10,42},{12,44},{14,46},{16,48}... | collective-permute-start | bytes 4718600 | tf_op jit(solution)/shard_map/ppermute | solution.py:356
  102.1 115.6 %copy-start.11 = (bf16[4,8,64,256]{3,2,1,0:T(8,128)(2,1)}, bf16[4,8,64,256]{3,2,1,0:T(8,128)(2,1)S(1)}, u32[]{:S(2)}) copy-start(bf16[4,8,64,256]{3,2,1,0:T(8,128)(2,1)S(1)} %pad_maximum_fusion.4.refs_12_) | copy-start | bytes 3145732
  102.2 115.5 %copy-start.12 = (bf16[4,8,64,256]{3,2,1,0:T(8,128)(2,1)}, bf16[4,8,64,256]{3,2,1,0:T(8,128)(2,1)S(1)}, u32[]{:S(2)}) copy-start(bf16[4,8,64,256]{3,2,1,0:T(8,128)(2,1)S(1)} %pad_maximum_fusion.3.refs_8_) | copy-start | bytes 3145732
  123.1 39.9 %copy-start.14 = (bf16[4,12,64,256]{3,2,1,0:T(8,128)(2,1)}, bf16[4,12,64,256]{3,2,1,0:T(8,128)(2,1)S(1)}, u32[]{:S(2)}) copy-start(bf16[4,12,64,256]{3,2,1,0:T(8,128)(2,1)S(1)} %collective-permute-done.5.refs_2_) | copy-start | bytes 4718596
  123.1 38.2 %collective-permute-start.23 = (bf16[4,8,64,256]{3,2,1,0:T(8,128)(2,1)S(1)}, bf16[4,8,64,256]{3,2,1,0:T(8,128)(2,1)S(1)}, u32[]{:S(2)}, u32[]{:S(2)}) collective-permute-start(bf16[4,8,64,256]{3,2,1,0:T(8,128)(2,1)S(1)} %pad_maximum_fusion.3.refs_8_), channel_id=1, source_target_pairs={{1,25},{3,27},{5,29},{7,31},{9,1},{11,3},{13,5},{15,7},{17,9},{19,... | collective-permute-start | bytes 3145736 | tf_op jit(solution)/shard_map/ppermute | solution.py:356
  146.3 16.7 %copy-start.15 = (bf16[4,12,64,256]{3,2,1,0:T(8,128)(2,1)}, bf16[4,12,64,256]{3,2,1,0:T(8,128)(2,1)S(1)}, u32[]{:S(2)}) copy-start(bf16[4,12,64,256]{3,2,1,0:T(8,128)(2,1)S(1)} %collective-permute-done.4.refs_1_) | copy-start | bytes 4718596
  146.3 73.4 %collective-permute-start.22 = (bf16[4,8,64,256]{3,2,1,0:T(8,128)(2,1)S(1)}, bf16[4,8,64,256]{3,2,1,0:T(8,128)(2,1)S(1)}, u32[]{:S(2)}, u32[]{:S(2)}) collective-permute-start(bf16[4,8,64,256]{3,2,1,0:T(8,128)(2,1)S(1)} %pad_maximum_fusion.3.refs_8_), channel_id=1, source_target_pairs={{1,17},{3,19},{5,21},{7,23},{9,25},{11,27},{13,29},{15,31},{17,1},... | collective-permute-start | bytes 3145736 | tf_op jit(solution)/shard_map/ppermute | solution.py:356
  153.7 7.5 %copy-start.16 = (bf16[4,12,64,256]{3,2,1,0:T(8,128)(2,1)}, bf16[4,12,64,256]{3,2,1,0:T(8,128)(2,1)S(1)}, u32[]{:S(2)}) copy-start(bf16[4,12,64,256]{3,2,1,0:T(8,128)(2,1)S(1)} %collective-permute-done.9.refs_7_) | copy-start | bytes 4718596
  153.7 65.9 %collective-permute-start.21 = (bf16[4,8,64,256]{3,2,1,0:T(8,128)(2,1)S(1)}, bf16[4,8,64,256]{3,2,1,0:T(8,128)(2,1)}, u32[]{:S(2)}, u32[]{:S(2)}) collective-permute-start(bf16[4,8,64,256]{3,2,1,0:T(8,128)(2,1)S(1)} %pad_maximum_fusion.3.refs_8_), channel_id=1, source_target_pairs={{1,9},{3,11},{5,13},{7,15},{9,17},{11,19},{13,21},{15,23},{17,25},... | collective-permute-start | bytes 3145736 | tf_op jit(solution)/shard_map/ppermute | solution.py:356
  155.4 7.6 %copy-start.17 = (bf16[4,12,64,256]{3,2,1,0:T(8,128)(2,1)}, bf16[4,12,64,256]{3,2,1,0:T(8,128)(2,1)S(1)}, u32[]{:S(2)}) copy-start(bf16[4,12,64,256]{3,2,1,0:T(8,128)(2,1)S(1)} %collective-permute-done.8.refs_6_) | copy-start | bytes 4718596
  155.4 64.3 %collective-permute-start.26 = (bf16[4,8,64,256]{3,2,1,0:T(8,128)(2,1)S(1)}, bf16[4,8,64,256]{3,2,1,0:T(8,128)(2,1)}, u32[]{:S(2)}, u32[]{:S(2)}) collective-permute-start(bf16[4,8,64,256]{3,2,1,0:T(8,128)(2,1)S(1)} %pad_maximum_fusion.4.refs_12_), channel_id=1, source_target_pairs={{1,97},{3,99},{5,101},{7,103},{9,105},{11,107},{13,109},{15,111},{... | collective-permute-start | bytes 3145736 | tf_op jit(solution)/shard_map/ppermute | solution.py:356
  159.6 3.3 %copy-start.18 = (bf16[4,12,64,256]{3,2,1,0:T(8,128)(2,1)}, bf16[4,12,64,256]{3,2,1,0:T(8,128)(2,1)S(1)}, u32[]{:S(2)}) copy-start(bf16[4,12,64,256]{3,2,1,0:T(8,128)(2,1)S(1)} %collective-permute-done.7.refs_5_) | copy-start | bytes 4718596
  159.6 60.1 %collective-permute-start.25 = (bf16[4,8,64,256]{3,2,1,0:T(8,128)(2,1)S(1)}, bf16[4,8,64,256]{3,2,1,0:T(8,128)(2,1)}, u32[]{:S(2)}, u32[]{:S(2)}) collective-permute-start(bf16[4,8,64,256]{3,2,1,0:T(8,128)(2,1)S(1)} %pad_maximum_fusion.4.refs_12_), channel_id=1, source_target_pairs={{1,65},{3,67},{5,69},{7,71},{9,73},{11,75},{13,77},{15,79},{17,81}... | collective-permute-start | bytes 3145736 | tf_op jit(solution)/shard_map/ppermute | solution.py:356
  161.3 1.7 copy-start.20
  161.3 58.4 %collective-permute-start.24 = (bf16[4,8,64,256]{3,2,1,0:T(8,128)(2,1)S(1)}, bf16[4,8,64,256]{3,2,1,0:T(8,128)(2,1)}, u32[]{:S(2)}, u32[]{:S(2)}) collective-permute-start(bf16[4,8,64,256]{3,2,1,0:T(8,128)(2,1)S(1)} %pad_maximum_fusion.4.refs_12_), channel_id=1, source_target_pairs={{1,33},{3,35},{5,37},{7,39},{9,41},{11,43},{13,45},{15,47},{17,49}... | collective-permute-start | bytes 3145736 | tf_op jit(solution)/shard_map/ppermute | solution.py:356
  (3 other events, 2.9 us)

commit v2 on v1

--- a/solution.py
+++ b/solution.py
@@ -194,7 +194,13 @@
                 (e, d, x ^ NEAR[d], (z + SIDE - e) % SIDE, v_ref), (d, e, (x + SIDE - d) % SIDE, z ^ NEAR[e], u_ref)
             ):
                 at = pl.ds(pl.multiple_of((at_x * SIDE + at_z) * 64, 64), 64)
-                src = fs[far] if dst is v_ref else gs[far]
+                stacks = fs if dst is v_ref else gs
+                if len(stacks) == SIDE:
+                    src, near = stacks[far], near
+                elif far == 2:
+                    src, near = stacks[2 + near // 2], near % 2
+                else:
+                    src = stacks[(0, 1, None, 4)[far]]
                 pairs.append((src.at[near, pl.ds(first, count)], dst.at[pl.ds(first if to is None else to, count), at, :]))
     return pairs
 
@@ -223,9 +229,9 @@
 
 
 def column_kernel(meta, *refs):
-    fs, gs, rows = refs[0:4], refs[4:8], refs[8:16]
-    band_hbm, out_hbm, dout_hbm = refs[16:19]
-    (u_ref, v_ref, hi_ref, lo_ref, ru_ref, rv_ref, tile_ref, acc_ref, l_ref, inv_ref, t_ref, up_ref, one_ref, xh_ref, xl_ref, sems) = refs[19:]
+    fs, gs, rows = refs[0:5], refs[5:10], refs[10:18]
+    band_hbm, out_hbm, dout_hbm = refs[18:21]
+    (u_ref, v_ref, hi_ref, lo_ref, ru_ref, rv_ref, tile_ref, acc_ref, l_ref, inv_ref, t_ref, up_ref, one_ref, xh_ref, xl_ref, sems) = refs[21:]
     n = l_ref.shape[0]
 
     @pl.when(meta[0] == 0)
@@ -292,9 +298,9 @@
 
 
 def tile_kernel(meta, *refs):
-    even, odd, rows = refs[0:8], refs[8:16], refs[16:24]
-    band_hbm, diag_hbm, _, _, out_hbm, dout_hbm = refs[24:30]
-    u_ref, v_ref, ru_ref, rv_ref, tile_ref, slab_ref, sems, row_sems = refs[30:]
+    even, odd, rows = refs[0:10], refs[10:18], refs[18:26]
+    band_hbm, diag_hbm, _, _, out_hbm, dout_hbm = refs[26:32]
+    u_ref, v_ref, ru_ref, rv_ref, tile_ref, slab_ref, sems, row_sems = refs[32:]
     panels = u_ref.shape[0]
     at = pl.ds(pl.multiple_of(meta[3] * 64, 64), 64)
     y, core_at = meta[0] // 2, meta[0] % 2
@@ -308,7 +314,7 @@
 
             @pl.when(core_at == 0)
             def _():
-                started(slab_copies(meta, even[:4], even[4:], u_ref, v_ref, first, 2), sems, 16 * first)
+                started(slab_copies(meta, even[:5], even[5:], u_ref, v_ref, first, 2), sems, 16 * first)
 
             @pl.when(core_at != 0)
             def _():
@@ -385,6 +391,19 @@
         got_a[d] = moved(a, along("z", lambda p: (p + d) % SIDE, parity))
         got_b[d] = moved(b, along("x", lambda p: (p + d) % SIDE, parity))
     return got_a, got_b
+
+
+def ring_leg(a, b):
+    ahead, back = (lambda p: (p + 1) % SIDE), (lambda p: (p + 3) % SIDE)
+    got = {}
+    for step, change in ((1, ahead), (3, back)):
+        for side, value, axis in (("a", a, "z"), ("b", b, "x")):
+            got[side, step] = moved(value, along(axis, change, 0))
+    half = a.shape[0] // 2
+    for step, change, part in ((1, ahead, slice(0, half)), (3, back, slice(half, 2 * half))):
+        for side, axis in (("a", "z"), ("b", "x")):
+            got[side, 2, step] = moved(got[side, step][part], along(axis, change, 0))
+    return [[own, got[side, 1], got[side, 2, 1], got[side, 2, 3], got[side, 3]] for side, own in (("a", a), ("b", b))]
 
 
 def shards(band, diag, row_factors, row_ranks, col_factors, col_ranks):
@@ -411,7 +430,7 @@
         near.append(moved(mine, across(lambda c: ((c // 2 + d) % SIDE) * 2 + c % 2)))
     sides, bases = own[:, 1], own[:, 0]
     a, b = lax.optimization_barrier(first_leg(jnp.concatenate([sides, high]), jnp.concatenate([bases, low]), 0))
-    fs, gs = second_leg(a, b, 0)
+    fs, gs = ring_leg(a, b)
     far = [moved(p, across(lambda c: c ^ 1)) for p in near]
     odd_a, odd_b = lax.optimization_barrier(first_leg(sides, bases, 1))
     odd_fs, odd_gs = second_leg(odd_a, odd_b, 1)
@@ -425,7 +444,7 @@
     tile, slab_out = pl.pallas_call(
         column_kernel,
         out_shape=outs,
-        in_specs=[smem] + [hbm] * 17,
+        in_specs=[smem] + [hbm] * 19,
         out_specs=(hbm, hbm),
         scratch_shapes=column_scratch(panels, order, rank),
         cost_estimate=pl.CostEstimate(flops=60_000_000_000, bytes_accessed=20_000_000, transcendentals=0),
@@ -434,10 +453,10 @@
     tile, slab_out = pl.pallas_call(
         tile_kernel,
         out_shape=outs,
-        in_specs=[smem] + [hbm] * 28,
+        in_specs=[smem] + [hbm] * 30,
         out_specs=(hbm, hbm),
         scratch_shapes=tile_scratch(panels, order, rank),
-        input_output_aliases={27: 0, 28: 1},
+        input_output_aliases={29: 0, 30: 1},
         cost_estimate=pl.CostEstimate(flops=10_000_000_000, bytes_accessed=40_000_000, transcendentals=0),
         compiler_params=pltpu.CompilerParams(vmem_limit_bytes=TILE_GRANT), name="tile")(
             meta, *fs, *gs, *odd_fs, *odd_gs, *near, *far, band[0, 0], diag[0], tile, slab_out)

time: 224 us -> 206 us (0.920)
  the two profiles are of different devices: /device:TPU:32 before, /device:TPU:0 now
where the time goes in v2:
time: 206 us; the launch traced here: 205 us
  waiting for transfers between devices  79.1 us (38%)
  starting transfers between devices  61.4 us (30%)
  Pallas kernels  56.4 us (27%)
  local copies, waits for them, and re-layouts  4.44 us (2%)
  between operations  2.31 us (1%)
    ppermute x29, waiting for transfers between devices, moved(): return lax.ppermute(value, AXES, pairs)  71.2 us
    ppermute x29, starting transfers between devices, moved(): return lax.ppermute(value, AXES, pairs)  56.7 us
    pallas_call x1, Pallas kernels, shards(): pl.pallas_call(column_kernel, out_shape=outs, in_specs=[smem] + [hbm] * 1...  54.4 us
    all_to_all x1, waiting for transfers between devices, shards(): lax.all_to_all(col_factors, 'cols', split_axis=0, concat_axis=1, tiled=True)  7.86 us
    all_to_all x1, starting transfers between devices, shards(): lax.all_to_all(col_factors, 'cols', split_axis=0, concat_axis=1, tiled=True)  4.73 us
  transfers between devices with their start and end apart: 30, of which 10 were waited for; matrix products, arithmetic and copies ran while one was open for 1% of the time, Pallas kernels for 27%

profile of v2, /device:TPU:0, one launch (start us, length us, event | category | flops | bytes accessed | tf_op | source)
XLA Modules:
  0.0 204.8 jit_solution(8127782039400563578)
XLA Ops:
  0.7 4.7 %all-to-all-start = ((bf16[8,1,2,64,256]{4,3,2,1,0:T(8,128)(2,1)}), bf16[8,1,2,64,256]{4,3,2,1,0:T(8,128)(2,1)S(1)}, u32[]{:S(2)}, u32[]{:S(2)}) async-start(bf16[8,1,2,64,256]{4,3,2,1,0:T(8,128)(2,1)} %param.10), calls=%async_computation | async-start | bytes 1048576 | tf_op jit(solution)/shard_map/all_to_all | solution.py:422
  6.0 1.1 reshape_squeeze.7
  7.2 0.2 copy.16
  7.8 7.9 %all-to-all-done = bf16[8,1,2,64,256]{4,3,2,1,0:T(8,128)(2,1)S(1)} async-done(((bf16[8,1,2,64,256]{4,3,2,1,0:T(8,128)(2,1)}), bf16[8,1,2,64,256]{4,3,2,1,0:T(8,128)(2,1)S(1)}, u32[]{:S(2)}, u32[]{:S(2)}) %all-to-all-start) | async-done | bytes 524320 | tf_op jit(solution)/shard_map/all_to_all | solution.py:422
  15.9 3.4 %collective-permute-start = (bf16[1,12,64,256]{3,2,1,0:T(8,128)(2,1)S(1)}, bf16[1,12,64,256]{3,2,1,0:T(8,128)(2,1)S(1)}, u32[]{:S(2)}, u32[]{:S(2)}) collective-permute-start(bf16[1,12,64,256]{3,2,1,0:T(8,128)(2,1)S(1)} %maximum_bitcast_fusion), channel_id=1, source_target_pairs={{0,32},{2,34},{4,36},{6,38},{8,40},{10,42},{12,44},{14,46},{16,48}... | collective-permute-start | bytes 1179656 | tf_op jit(solution)/shard_map/ppermute | solution.py:362
  19.4 3.8 %collective-permute-start.2 = (bf16[1,12,64,256]{3,2,1,0:T(8,128)(2,1)S(1)}, bf16[1,12,64,256]{3,2,1,0:T(8,128)(2,1)S(1)}, u32[]{:S(2)}, u32[]{:S(2)}) collective-permute-start(bf16[1,12,64,256]{3,2,1,0:T(8,128)(2,1)S(1)} %maximum_bitcast_fusion.1), channel_id=1, source_target_pairs={{0,8},{2,10},{4,12},{6,14},{8,0},{10,2},{12,4},{14,6},{16,24},{18,... | collective-permute-start | bytes 1179656 | tf_op jit(solution)/shard_map/ppermute | solution.py:362
  23.2 2.4 %collective-permute-done = bf16[1,12,64,256]{3,2,1,0:T(8,128)(2,1)S(1)} collective-permute-done((bf16[1,12,64,256]{3,2,1,0:T(8,128)(2,1)S(1)}, bf16[1,12,64,256]{3,2,1,0:T(8,128)(2,1)S(1)}, u32[]{:S(2)}, u32[]{:S(2)}) %collective-permute-start) | collective-permute-done | bytes 393248 | tf_op jit(solution)/shard_map/ppermute | solution.py:362
  25.7 4.7 %collective-permute-start.1 = (bf16[2,12,64,256]{3,2,1,0:T(8,128)(2,1)S(1)}, bf16[2,12,64,256]{3,2,1,0:T(8,128)(2,1)S(1)}, u32[]{:S(2)}, u32[]{:S(2)}) collective-permute-start(bf16[2,12,64,256]{3,2,1,0:T(8,128)(2,1)S(1)} %pad_maximum_fusion.5), channel_id=1, source_target_pairs={{0,96},{2,98},{4,100},{6,102},{8,104},{10,106},{12,108},{14,110},{... | collective-permute-start | bytes 2359304 | tf_op jit(solution)/shard_map/ppermute | solution.py:362
  30.3 0.7 collective-permute-start.21
  31.1 6.5 %collective-permute-start.3 = (bf16[2,12,64,256]{3,2,1,0:T(8,128)(2,1)S(1)}, bf16[2,12,64,256]{3,2,1,0:T(8,128)(2,1)S(1)}, u32[]{:S(2)}, u32[]{:S(2)}) collective-permute-start(bf16[2,12,64,256]{3,2,1,0:T(8,128)(2,1)S(1)} %pad_maximum_fusion.6), channel_id=1, source_target_pairs={{0,24},{2,26},{4,28},{6,30},{8,16},{10,18},{12,20},{14,22},{16,8},... | collective-permute-start | bytes 2359304 | tf_op jit(solution)/shard_map/ppermute | solution.py:362
  37.6 0.7 collective-permute-start.19
  38.5 0.7 collective-permute-start.22
  39.2 0.7 collective-permute-start.20
  39.9 0.8 collective-permute-done.1
  40.7 1.2 collective-permute-start.14
  41.9 0.2 pad_maximum_fusion.refs_0_
  42.1 10.6 %collective-permute-done.3 = bf16[2,12,64,256]{3,2,1,0:T(8,128)(2,1)S(1)} collective-permute-done((bf16[2,12,64,256]{3,2,1,0:T(8,128)(2,1)S(1)}, bf16[2,12,64,256]{3,2,1,0:T(8,128)(2,1)S(1)}, u32[]{:S(2)}, u32[]{:S(2)}) %collective-permute-start.3) | collective-permute-done | bytes 786464 | tf_op jit(solution)/shard_map/ppermute | solution.py:362
  52.7 0.2 pad_maximum_fusion.1.refs_5_
  52.9 5.6 %collective-permute-start.6 = (bf16[4,12,64,256]{3,2,1,0:T(8,128)(2,1)S(1)}, bf16[4,12,64,256]{3,2,1,0:T(8,128)(2,1)S(1)}, u32[]{:S(2)}, u32[]{:S(2)}) collective-permute-start(bf16[4,12,64,256]{3,2,1,0:T(8,128)(2,1)S(1)} %pad_maximum_fusion.refs_0_), channel_id=1, source_target_pairs={{0,24},{2,26},{4,28},{6,30},{8,0},{10,2},{12,4},{14,6},{16,8},{18,... | collective-permute-start | bytes 4718600 | tf_op jit(solution)/shard_map/ppermute | solution.py:362
  58.6 1.9 collective-permute-start.4
  60.6 2.1 %collective-permute-start.12 = (bf16[2,1024,256]{2,1,0:T(8,128)(2,1)S(1)}, bf16[2,1024,256]{2,1,0:T(8,128)(2,1)S(1)}, u32[]{:S(2)}, u32[]{:S(2)}) collective-permute-start(bf16[2,1024,256]{2,1,0:T(8,128)(2,1)S(1)} %pad_maximum_fusion.2.refs_10_.refs_18_), channel_id=1, source_target_pairs={{0,2},{1,3},{2,4},{3,5},{4,6},{5,7},{6,0},{7,1},{8,10},{9,11},{10,... | collective-permute-start | bytes 3145736 | tf_op jit(solution)/shard_map/ppermute | solution.py:362
  62.6 2.8 %collective-permute-done.14.refs_13_.refs_21_ = bf16[2,1024,256]{2,1,0:T(8,128)(2,1)S(1)} collective-permute-done((bf16[2,1024,256]{2,1,0:T(8,128)(2,1)S(1)}, bf16[2,1024,256]{2,1,0:T(8,128)(2,1)S(1)}, u32[]{:S(2)}, u32[]{:S(2)}) %collective-permute-start.14) | collective-permute-done | bytes 1048608 | tf_op jit(solution)/shard_map/ppermute | solution.py:362
  65.4 4.7 %collective-permute-start.10 = (bf16[4,12,64,256]{3,2,1,0:T(8,128)(2,1)S(1)}, bf16[4,12,64,256]{3,2,1,0:T(8,128)(2,1)S(1)}, u32[]{:S(2)}, u32[]{:S(2)}) collective-permute-start(bf16[4,12,64,256]{3,2,1,0:T(8,128)(2,1)S(1)} %pad_maximum_fusion.1.refs_5_), channel_id=1, source_target_pairs={{0,96},{2,98},{4,100},{6,102},{8,104},{10,106},{12,108},{14,110},{... | collective-permute-start | bytes 4718600 | tf_op jit(solution)/shard_map/ppermute | solution.py:362
  70.0 16.1 %collective-permute-done.13.refs_12_.refs_20_ = bf16[2,1024,256]{2,1,0:T(8,128)(2,1)S(1)} collective-permute-done((bf16[2,1024,256]{2,1,0:T(8,128)(2,1)S(1)}, bf16[2,1024,256]{2,1,0:T(8,128)(2,1)S(1)}, u32[]{:S(2)}, u32[]{:S(2)}) %collective-permute-start.13) | collective-permute-done | bytes 1048608 | tf_op jit(solution)/shard_map/ppermute | solution.py:362
  86.1 2.1 %collective-permute-start.8 = (bf16[4,12,64,256]{3,2,1,0:T(8,128)(2,1)S(1)}, bf16[4,12,64,256]{3,2,1,0:T(8,128)(2,1)S(1)}, u32[]{:S(2)}, u32[]{:S(2)}) collective-permute-start(bf16[4,12,64,256]{3,2,1,0:T(8,128)(2,1)S(1)} %pad_maximum_fusion.1.refs_5_), channel_id=1, source_target_pairs={{0,32},{2,34},{4,36},{6,38},{8,40},{10,42},{12,44},{14,46},{16,48}... | collective-permute-start | bytes 4718600 | tf_op jit(solution)/shard_map/ppermute | solution.py:362
  88.2 13.8 %collective-permute-done.12.refs_11_.refs_19_ = bf16[2,1024,256]{2,1,0:T(8,128)(2,1)S(1)} collective-permute-done((bf16[2,1024,256]{2,1,0:T(8,128)(2,1)S(1)}, bf16[2,1024,256]{2,1,0:T(8,128)(2,1)S(1)}, u32[]{:S(2)}, u32[]{:S(2)}) %collective-permute-start.12) | collective-permute-done | bytes 1048608 | tf_op jit(solution)/shard_map/ppermute | solution.py:362
  102.1 0.5 collective-permute-start.17
  102.9 0.7 collective-permute-start.25
  103.9 0.8 collective-permute-done.18.refs_17_.refs_25_
  104.7 5.2 %collective-permute-start.7 = (bf16[2,12,64,256]{3,2,1,0:T(8,128)(2,1)S(1)}, bf16[2,12,64,256]{3,2,1,0:T(8,128)(2,1)S(1)}, u32[]{:S(2)}, u32[]{:S(2)}) collective-permute-start(bf16[2,12,64,256]{3,2,1,0:T(8,128)(2,1)S(1)} %slice.33), channel_id=1, source_target_pairs={{0,24},{2,26},{4,28},{6,30},{8,0},{10,2},{12,4},{14,6},{16,8},{18,... | collective-permute-start | bytes 2359304 | tf_op jit(solution)/shard_map/ppermute | solution.py:362
  109.9 1.9 collective-permute-start.5
  111.9 2.4 %collective-permute-start.11 = (bf16[2,12,64,256]{3,2,1,0:T(8,128)(2,1)S(1)}, bf16[2,12,64,256]{3,2,1,0:T(8,128)(2,1)S(1)}, u32[]{:S(2)}, u32[]{:S(2)}) collective-permute-start(bf16[2,12,64,256]{3,2,1,0:T(8,128)(2,1)S(1)} %slice.35), channel_id=1, source_target_pairs={{0,96},{2,98},{4,100},{6,102},{8,104},{10,106},{12,108},{14,110},{... | collective-permute-start | bytes 2359304 | tf_op jit(solution)/shard_map/ppermute | solution.py:362
  114.4 3.5 %collective-permute-start.9 = (bf16[2,12,64,256]{3,2,1,0:T(8,128)(2,1)S(1)}, bf16[2,12,64,256]{3,2,1,0:T(8,128)(2,1)S(1)}, u32[]{:S(2)}, u32[]{:S(2)}) collective-permute-start(bf16[2,12,64,256]{3,2,1,0:T(8,128)(2,1)S(1)} %slice.34), channel_id=1, source_target_pairs={{0,32},{2,34},{4,36},{6,38},{8,40},{10,42},{12,44},{14,46},{16,48}... | collective-permute-start | bytes 2359304 | tf_op jit(solution)/shard_map/ppermute | solution.py:362
  117.8 21.0 %collective-permute-done.7.refs_3_ = bf16[2,12,64,256]{3,2,1,0:T(8,128)(2,1)S(1)} collective-permute-done((bf16[2,12,64,256]{3,2,1,0:T(8,128)(2,1)S(1)}, bf16[2,12,64,256]{3,2,1,0:T(8,128)(2,1)S(1)}, u32[]{:S(2)}, u32[]{:S(2)}) %collective-permute-start.7) | collective-permute-done | bytes 786464 | tf_op jit(solution)/shard_map/ppermute | solution.py:362
  138.9 0.7 collective-permute-start.24
  139.6 2.9 %collective-permute-done.5.refs_2_ = bf16[2,12,64,256]{3,2,1,0:T(8,128)(2,1)S(1)} collective-permute-done((bf16[2,12,64,256]{3,2,1,0:T(8,128)(2,1)S(1)}, bf16[2,12,64,256]{3,2,1,0:T(8,128)(2,1)S(1)}, u32[]{:S(2)}, u32[]{:S(2)}) %collective-permute-start.5) | collective-permute-done | bytes 786464 | tf_op jit(solution)/shard_map/ppermute | solution.py:362
  142.5 0.7 collective-permute-start.23
  143.2 0.7 collective-permute-start.28
  144.0 0.7 collective-permute-start.27
  144.8 0.7 collective-permute-start.26
  145.5 0.2 copy-done.22
  145.7 54.4 %column.1 = (f32[1024,1024]{1,0:T(8,128)}, f32[64,1024]{1,0:T(8,128)}) custom-call(s32[12]{0:T(128)S(1)} %concatenate.37.meta, bf16[4,12,64,256]{3,2,1,0:T(8,128)(2,1)} %copy-done.10, bf16[4,12,64,256]{3,2,1,0:T(8,128)(2,1)} %copy-done.15, bf16[2,12,64,256]{3,2,1,0:T(8,128)(2,1)S(1)} %collective-permute-done.5.refs_2_, ...), custom_call_target="tpu_custom_call" | custom-call | flops 60000002048 | bytes 20000000 | tf_op jit(solution)/shard_map/column/pallas_call | solution.py:444
  200.3 1.0 copy-done.23
  201.3 0.4 copy-done.24
  201.7 0.3 copy-done.25
  202.0 0.4 copy-done.26
  202.4 0.2 copy-done.27
  202.6 2.0 tile.1
  (97 shorter events, 1.8 us)
Async XLA Ops:
  0.7 15.0 %all-to-all-start = ((bf16[8,1,2,64,256]{4,3,2,1,0:T(8,128)(2,1)}), bf16[8,1,2,64,256]{4,3,2,1,0:T(8,128)(2,1)S(1)}, u32[]{:S(2)}, u32[]{:S(2)}) async-start(bf16[8,1,2,64,256]{4,3,2,1,0:T(8,128)(2,1)} %param.10), calls=%async_computation | async-start | bytes 1048576 | tf_op jit(solution)/shard_map/all_to_all | solution.py:422
  7.7 138.1 %copy-start.9 = (s32[12]{0:T(128)}, s32[12]{0:T(128)S(1)}, u32[]{:S(2)}) copy-start(s32[12]{0:T(128)S(1)} %concatenate.37.meta) | copy-start | bytes 148
  7.8 138.0 %copy-start.1 = (bf16[2,1024,256]{2,1,0:T(8,128)(2,1)}, bf16[2,1024,256]{2,1,0:T(8,128)(2,1)S(1)}, u32[]{:S(2)}) copy-start(bf16[2,1024,256]{2,1,0:T(8,128)(2,1)S(1)} %pad_maximum_fusion.2.refs_10_.refs_18_) | copy-start | bytes 3145732
  15.9 9.7 %collective-permute-start = (bf16[1,12,64,256]{3,2,1,0:T(8,128)(2,1)S(1)}, bf16[1,12,64,256]{3,2,1,0:T(8,128)(2,1)S(1)}, u32[]{:S(2)}, u32[]{:S(2)}) collective-permute-start(bf16[1,12,64,256]{3,2,1,0:T(8,128)(2,1)S(1)} %maximum_bitcast_fusion), channel_id=1, source_target_pairs={{0,32},{2,34},{4,36},{6,38},{8,40},{10,42},{12,44},{14,46},{16,48}... | collective-permute-start | bytes 1179656 | tf_op jit(solution)/shard_map/ppermute | solution.py:362
  19.4 11.7 %collective-permute-start.2 = (bf16[1,12,64,256]{3,2,1,0:T(8,128)(2,1)S(1)}, bf16[1,12,64,256]{3,2,1,0:T(8,128)(2,1)S(1)}, u32[]{:S(2)}, u32[]{:S(2)}) collective-permute-start(bf16[1,12,64,256]{3,2,1,0:T(8,128)(2,1)S(1)} %maximum_bitcast_fusion.1), channel_id=1, source_target_pairs={{0,8},{2,10},{4,12},{6,14},{8,0},{10,2},{12,4},{14,6},{16,24},{18,... | collective-permute-start | bytes 1179656 | tf_op jit(solution)/shard_map/ppermute | solution.py:362
  25.7 15.1 %collective-permute-start.1 = (bf16[2,12,64,256]{3,2,1,0:T(8,128)(2,1)S(1)}, bf16[2,12,64,256]{3,2,1,0:T(8,128)(2,1)S(1)}, u32[]{:S(2)}, u32[]{:S(2)}) collective-permute-start(bf16[2,12,64,256]{3,2,1,0:T(8,128)(2,1)S(1)} %pad_maximum_fusion.5), channel_id=1, source_target_pairs={{0,96},{2,98},{4,100},{6,102},{8,104},{10,106},{12,108},{14,110},{... | collective-permute-start | bytes 2359304 | tf_op jit(solution)/shard_map/ppermute | solution.py:362
  30.3 8.1 %collective-permute-start.21 = (bf16[1,8,64,256]{3,2,1,0:T(8,128)(2,1)S(1)}, bf16[1,8,64,256]{3,2,1,0:T(8,128)(2,1)S(1)}, u32[]{:S(2)}, u32[]{:S(2)}) collective-permute-start(bf16[1,8,64,256]{3,2,1,0:T(8,128)(2,1)S(1)} %get-tuple-element.70), channel_id=1, source_target_pairs={{1,9},{3,11},{5,13},{7,15},{9,1},{11,3},{13,5},{15,7},{17,25},{19,... | collective-permute-start | bytes 786440 | tf_op jit(solution)/shard_map/ppermute | solution.py:362
  31.1 21.6 %collective-permute-start.3 = (bf16[2,12,64,256]{3,2,1,0:T(8,128)(2,1)S(1)}, bf16[2,12,64,256]{3,2,1,0:T(8,128)(2,1)S(1)}, u32[]{:S(2)}, u32[]{:S(2)}) collective-permute-start(bf16[2,12,64,256]{3,2,1,0:T(8,128)(2,1)S(1)} %pad_maximum_fusion.6), channel_id=1, source_target_pairs={{0,24},{2,26},{4,28},{6,30},{8,16},{10,18},{12,20},{14,22},{16,8},... | collective-permute-start | bytes 2359304 | tf_op jit(solution)/shard_map/ppermute | solution.py:362
  37.6 1.6 collective-permute-start.19
  38.3 22.2 %collective-permute-start.15 = (bf16[2,1024,256]{2,1,0:T(8,128)(2,1)S(1)}, bf16[2,1024,256]{2,1,0:T(8,128)(2,1)S(1)}, u32[]{:S(2)}, u32[]{:S(2)}) collective-permute-start(bf16[2,1024,256]{2,1,0:T(8,128)(2,1)S(1)} %pad_maximum_fusion.2.refs_10_.refs_18_), channel_id=1, source_target_pairs={{0,1},{1,0},{2,3},{3,2},{4,5},{5,4},{6,7},{7,6},{8,9},{9,8},{10,11... | collective-permute-start | bytes 3145736 | tf_op jit(solution)/shard_map/ppermute | solution.py:362
  38.5 20.0 %collective-permute-start.22 = (bf16[2,8,64,256]{3,2,1,0:T(8,128)(2,1)S(1)}, bf16[2,8,64,256]{3,2,1,0:T(8,128)(2,1)S(1)}, u32[]{:S(2)}, u32[]{:S(2)}) collective-permute-start(bf16[2,8,64,256]{3,2,1,0:T(8,128)(2,1)S(1)} %pad_maximum_fusion.8), channel_id=1, source_target_pairs={{1,25},{3,27},{5,29},{7,31},{9,17},{11,19},{13,21},{15,23},{17,9},... | collective-permute-start | bytes 1572872 | tf_op jit(solution)/shard_map/ppermute | solution.py:362
  39.2 19.4 %collective-permute-start.20 = (bf16[2,8,64,256]{3,2,1,0:T(8,128)(2,1)S(1)}, bf16[2,8,64,256]{3,2,1,0:T(8,128)(2,1)S(1)}, u32[]{:S(2)}, u32[]{:S(2)}) collective-permute-start(bf16[2,8,64,256]{3,2,1,0:T(8,128)(2,1)S(1)} %pad_maximum_fusion.7), channel_id=1, source_target_pairs={{1,97},{3,99},{5,101},{7,103},{9,105},{11,107},{13,109},{15,111},{... | collective-permute-start | bytes 1572872 | tf_op jit(solution)/shard_map/ppermute | solution.py:362
  40.7 24.6 %collective-permute-start.14 = (bf16[2,1024,256]{2,1,0:T(8,128)(2,1)S(1)}, bf16[2,1024,256]{2,1,0:T(8,128)(2,1)S(1)}, u32[]{:S(2)}, u32[]{:S(2)}) collective-permute-start(bf16[2,1024,256]{2,1,0:T(8,128)(2,1)S(1)} %pad_maximum_fusion.2.refs_10_.refs_18_), channel_id=1, source_target_pairs={{0,6},{1,7},{2,0},{3,1},{4,2},{5,3},{6,4},{7,5},{8,14},{9,15},{10,... | collective-permute-start | bytes 3145736 | tf_op jit(solution)/shard_map/ppermute | solution.py:362
  42.1 16.5 %copy-start.10 = (bf16[4,12,64,256]{3,2,1,0:T(8,128)(2,1)}, bf16[4,12,64,256]{3,2,1,0:T(8,128)(2,1)S(1)}, u32[]{:S(2)}) copy-start(bf16[4,12,64,256]{3,2,1,0:T(8,128)(2,1)S(1)} %pad_maximum_fusion.refs_0_) | copy-start | bytes 4718596
  52.9 50.0 %copy-start.11 = (bf16[4,12,64,256]{3,2,1,0:T(8,128)(2,1)}, bf16[4,12,64,256]{3,2,1,0:T(8,128)(2,1)S(1)}, u32[]{:S(2)}) copy-start(bf16[4,12,64,256]{3,2,1,0:T(8,128)(2,1)S(1)} %pad_maximum_fusion.1.refs_5_) | copy-start | bytes 4718596
  52.9 49.2 %collective-permute-start.6 = (bf16[4,12,64,256]{3,2,1,0:T(8,128)(2,1)S(1)}, bf16[4,12,64,256]{3,2,1,0:T(8,128)(2,1)S(1)}, u32[]{:S(2)}, u32[]{:S(2)}) collective-permute-start(bf16[4,12,64,256]{3,2,1,0:T(8,128)(2,1)S(1)} %pad_maximum_fusion.refs_0_), channel_id=1, source_target_pairs={{0,24},{2,26},{4,28},{6,30},{8,0},{10,2},{12,4},{14,6},{16,8},{18,... | collective-permute-start | bytes 4718600 | tf_op jit(solution)/shard_map/ppermute | solution.py:362
  58.5 27.6 %collective-permute-start.13 = (bf16[2,1024,256]{2,1,0:T(8,128)(2,1)S(1)}, bf16[2,1024,256]{2,1,0:T(8,128)(2,1)S(1)}, u32[]{:S(2)}, u32[]{:S(2)}) collective-permute-start(bf16[2,1024,256]{2,1,0:T(8,128)(2,1)S(1)} %pad_maximum_fusion.2.refs_10_.refs_18_), channel_id=1, source_target_pairs={{0,4},{1,5},{2,6},{3,7},{4,0},{5,1},{6,2},{7,3},{8,12},{9,13},{10,... | collective-permute-start | bytes 3145736 | tf_op jit(solution)/shard_map/ppermute | solution.py:362
  58.6 43.9 %collective-permute-start.4 = (bf16[4,12,64,256]{3,2,1,0:T(8,128)(2,1)S(1)}, bf16[4,12,64,256]{3,2,1,0:T(8,128)(2,1)S(1)}, u32[]{:S(2)}, u32[]{:S(2)}) collective-permute-start(bf16[4,12,64,256]{3,2,1,0:T(8,128)(2,1)S(1)} %pad_maximum_fusion.refs_0_), channel_id=1, source_target_pairs={{0,8},{2,10},{4,12},{6,14},{8,16},{10,18},{12,20},{14,22},{16,24},... | collective-permute-start | bytes 4718600 | tf_op jit(solution)/shard_map/ppermute | solution.py:362
  60.5 53.8 %copy-start.18 = (bf16[2,1024,256]{2,1,0:T(8,128)(2,1)}, bf16[2,1024,256]{2,1,0:T(8,128)(2,1)S(1)}, u32[]{:S(2)}) copy-start(bf16[2,1024,256]{2,1,0:T(8,128)(2,1)S(1)} %collective-permute-done.15.refs_14_.refs_22_) | copy-start | bytes 3145732
  60.6 41.5 %collective-permute-start.12 = (bf16[2,1024,256]{2,1,0:T(8,128)(2,1)S(1)}, bf16[2,1024,256]{2,1,0:T(8,128)(2,1)S(1)}, u32[]{:S(2)}, u32[]{:S(2)}) collective-permute-start(bf16[2,1024,256]{2,1,0:T(8,128)(2,1)S(1)} %pad_maximum_fusion.2.refs_10_.refs_18_), channel_id=1, source_target_pairs={{0,2},{1,3},{2,4},{3,5},{4,6},{5,7},{6,0},{7,1},{8,10},{9,11},{10,... | collective-permute-start | bytes 3145736 | tf_op jit(solution)/shard_map/ppermute | solution.py:362
  65.4 80.3 %copy-start.2 = (bf16[2,1024,256]{2,1,0:T(8,128)(2,1)}, bf16[2,1024,256]{2,1,0:T(8,128)(2,1)S(1)}, u32[]{:S(2)}) copy-start(bf16[2,1024,256]{2,1,0:T(8,128)(2,1)S(1)} %collective-permute-done.14.refs_13_.refs_21_) | copy-start | bytes 3145732
  65.4 37.5 %collective-permute-start.10 = (bf16[4,12,64,256]{3,2,1,0:T(8,128)(2,1)S(1)}, bf16[4,12,64,256]{3,2,1,0:T(8,128)(2,1)S(1)}, u32[]{:S(2)}, u32[]{:S(2)}) collective-permute-start(bf16[4,12,64,256]{3,2,1,0:T(8,128)(2,1)S(1)} %pad_maximum_fusion.1.refs_5_), channel_id=1, source_target_pairs={{0,96},{2,98},{4,100},{6,102},{8,104},{10,106},{12,108},{14,110},{... | collective-permute-start | bytes 4718600 | tf_op jit(solution)/shard_map/ppermute | solution.py:362
  86.1 59.6 %copy-start.3 = (bf16[2,1024,256]{2,1,0:T(8,128)(2,1)}, bf16[2,1024,256]{2,1,0:T(8,128)(2,1)S(1)}, u32[]{:S(2)}) copy-start(bf16[2,1024,256]{2,1,0:T(8,128)(2,1)S(1)} %collective-permute-done.13.refs_12_.refs_20_) | copy-start | bytes 3145732
  86.1 25.7 %collective-permute-start.8 = (bf16[4,12,64,256]{3,2,1,0:T(8,128)(2,1)S(1)}, bf16[4,12,64,256]{3,2,1,0:T(8,128)(2,1)S(1)}, u32[]{:S(2)}, u32[]{:S(2)}) collective-permute-start(bf16[4,12,64,256]{3,2,1,0:T(8,128)(2,1)S(1)} %pad_maximum_fusion.1.refs_5_), channel_id=1, source_target_pairs={{0,32},{2,34},{4,36},{6,38},{8,40},{10,42},{12,44},{14,46},{16,48}... | collective-permute-start | bytes 4718600 | tf_op jit(solution)/shard_map/ppermute | solution.py:362
  102.0 43.7 %copy-start.4 = (bf16[2,1024,256]{2,1,0:T(8,128)(2,1)}, bf16[2,1024,256]{2,1,0:T(8,128)(2,1)S(1)}, u32[]{:S(2)}) copy-start(bf16[2,1024,256]{2,1,0:T(8,128)(2,1)S(1)} %collective-permute-done.12.refs_11_.refs_19_) | copy-start | bytes 3145732
  102.0 2.7 %collective-permute-start.18 = (bf16[2,1024,256]{2,1,0:T(8,128)(2,1)S(1)}, bf16[2,1024,256]{2,1,0:T(8,128)(2,1)S(1)}, u32[]{:S(2)}, u32[]{:S(2)}) collective-permute-start(bf16[2,1024,256]{2,1,0:T(8,128)(2,1)S(1)} %collective-permute-done.14.refs_13_.refs_21_), channel_id=1, source_target_pairs={{0,1},{1,0},{2,3},{3,2},{4,5},{5,4},{6,7},{7,6},{8,9},{9,8},{10,11... | collective-permute-start | bytes 3145736 | tf_op jit(solution)/shard_map/ppermute | solution.py:362
  102.1 7.8 %collective-permute-start.17 = (bf16[2,1024,256]{2,1,0:T(8,128)(2,1)S(1)}, bf16[2,1024,256]{2,1,0:T(8,128)(2,1)S(1)}, u32[]{:S(2)}, u32[]{:S(2)}) collective-permute-start(bf16[2,1024,256]{2,1,0:T(8,128)(2,1)S(1)} %collective-permute-done.13.refs_12_.refs_20_), channel_id=1, source_target_pairs={{0,1},{1,0},{2,3},{3,2},{4,5},{5,4},{6,7},{7,6},{8,9},{9,8},{10,11... | collective-permute-start | bytes 3145736 | tf_op jit(solution)/shard_map/ppermute | solution.py:362
  102.6 11.8 %collective-permute-start.16 = (bf16[2,1024,256]{2,1,0:T(8,128)(2,1)S(1)}, bf16[2,1024,256]{2,1,0:T(8,128)(2,1)S(1)}, u32[]{:S(2)}, u32[]{:S(2)}) collective-permute-start(bf16[2,1024,256]{2,1,0:T(8,128)(2,1)S(1)} %collective-permute-done.12.refs_11_.refs_19_), channel_id=1, source_target_pairs={{0,1},{1,0},{2,3},{3,2},{4,5},{5,4},{6,7},{7,6},{8,9},{9,8},{10,11... | collective-permute-start | bytes 3145736 | tf_op jit(solution)/shard_map/ppermute | solution.py:362
  102.8 42.0 %copy-start.12 = (bf16[4,8,64,256]{3,2,1,0:T(8,128)(2,1)}, bf16[4,8,64,256]{3,2,1,0:T(8,128)(2,1)S(1)}, u32[]{:S(2)}) copy-start(bf16[4,8,64,256]{3,2,1,0:T(8,128)(2,1)S(1)} %pad_maximum_fusion.4.refs_14_) | copy-start | bytes 3145732
  102.9 39.6 %copy-start.13 = (bf16[4,8,64,256]{3,2,1,0:T(8,128)(2,1)}, bf16[4,8,64,256]{3,2,1,0:T(8,128)(2,1)S(1)}, u32[]{:S(2)}) copy-start(bf16[4,8,64,256]{3,2,1,0:T(8,128)(2,1)S(1)} %pad_maximum_fusion.3.refs_10_) | copy-start | bytes 3145732
  102.9 42.8 %copy-start.16 = (bf16[4,12,64,256]{3,2,1,0:T(8,128)(2,1)}, bf16[4,12,64,256]{3,2,1,0:T(8,128)(2,1)S(1)}, u32[]{:S(2)}) copy-start(bf16[4,12,64,256]{3,2,1,0:T(8,128)(2,1)S(1)} %collective-permute-done.10.refs_9_) | copy-start | bytes 4718596
  102.9 41.8 %collective-permute-start.25 = (bf16[4,8,64,256]{3,2,1,0:T(8,128)(2,1)S(1)}, bf16[4,8,64,256]{3,2,1,0:T(8,128)(2,1)S(1)}, u32[]{:S(2)}, u32[]{:S(2)}) collective-permute-start(bf16[4,8,64,256]{3,2,1,0:T(8,128)(2,1)S(1)} %pad_maximum_fusion.3.refs_10_), channel_id=1, source_target_pairs={{1,25},{3,27},{5,29},{7,31},{9,1},{11,3},{13,5},{15,7},{17,9},{19,... | collective-permute-start | bytes 3145736 | tf_op jit(solution)/shard_map/ppermute | solution.py:362
  104.7 40.8 %copy-start.19 = (bf16[2,1024,256]{2,1,0:T(8,128)(2,1)}, bf16[2,1024,256]{2,1,0:T(8,128)(2,1)S(1)}, u32[]{:S(2)}) copy-start(bf16[2,1024,256]{2,1,0:T(8,128)(2,1)S(1)} %collective-permute-done.18.refs_17_.refs_25_) | copy-start | bytes 3145732
  104.7 34.2 %collective-permute-start.7 = (bf16[2,12,64,256]{3,2,1,0:T(8,128)(2,1)S(1)}, bf16[2,12,64,256]{3,2,1,0:T(8,128)(2,1)S(1)}, u32[]{:S(2)}, u32[]{:S(2)}) collective-permute-start(bf16[2,12,64,256]{3,2,1,0:T(8,128)(2,1)S(1)} %slice.33), channel_id=1, source_target_pairs={{0,24},{2,26},{4,28},{6,30},{8,0},{10,2},{12,4},{14,6},{16,8},{18,... | collective-permute-start | bytes 2359304 | tf_op jit(solution)/shard_map/ppermute | solution.py:362
  109.9 35.6 %copy-start.20 = (bf16[2,1024,256]{2,1,0:T(8,128)(2,1)}, bf16[2,1024,256]{2,1,0:T(8,128)(2,1)S(1)}, u32[]{:S(2)}) copy-start(bf16[2,1024,256]{2,1,0:T(8,128)(2,1)S(1)} %collective-permute-done.17.refs_16_.refs_24_) | copy-start | bytes 3145732
  109.9 32.6 %collective-permute-start.5 = (bf16[2,12,64,256]{3,2,1,0:T(8,128)(2,1)S(1)}, bf16[2,12,64,256]{3,2,1,0:T(8,128)(2,1)S(1)}, u32[]{:S(2)}, u32[]{:S(2)}) collective-permute-start(bf16[2,12,64,256]{3,2,1,0:T(8,128)(2,1)S(1)} %slice.32), channel_id=1, source_target_pairs={{0,8},{2,10},{4,12},{6,14},{8,16},{10,18},{12,20},{14,22},{16,24},... | collective-permute-start | bytes 2359304 | tf_op jit(solution)/shard_map/ppermute | solution.py:362
  111.9 31.4 %collective-permute-start.11 = (bf16[2,12,64,256]{3,2,1,0:T(8,128)(2,1)S(1)}, bf16[2,12,64,256]{3,2,1,0:T(8,128)(2,1)S(1)}, u32[]{:S(2)}, u32[]{:S(2)}) collective-permute-start(bf16[2,12,64,256]{3,2,1,0:T(8,128)(2,1)S(1)} %slice.35), channel_id=1, source_target_pairs={{0,96},{2,98},{4,100},{6,102},{8,104},{10,106},{12,108},{14,110},{... | collective-permute-start | bytes 2359304 | tf_op jit(solution)/shard_map/ppermute | solution.py:362
  114.4 31.1 %copy-start.21 = (bf16[2,1024,256]{2,1,0:T(8,128)(2,1)}, bf16[2,1024,256]{2,1,0:T(8,128)(2,1)S(1)}, u32[]{:S(2)}) copy-start(bf16[2,1024,256]{2,1,0:T(8,128)(2,1)S(1)} %collective-permute-done.16.refs_15_.refs_23_) | copy-start | bytes 3145732
  114.4 29.6 %collective-permute-start.9 = (bf16[2,12,64,256]{3,2,1,0:T(8,128)(2,1)S(1)}, bf16[2,12,64,256]{3,2,1,0:T(8,128)(2,1)S(1)}, u32[]{:S(2)}, u32[]{:S(2)}) collective-permute-start(bf16[2,12,64,256]{3,2,1,0:T(8,128)(2,1)S(1)} %slice.34), channel_id=1, source_target_pairs={{0,32},{2,34},{4,36},{6,38},{8,40},{10,42},{12,44},{14,46},{16,48}... | collective-permute-start | bytes 2359304 | tf_op jit(solution)/shard_map/ppermute | solution.py:362
  138.9 61.3 %copy-start.5 = (bf16[2,12,64,256]{3,2,1,0:T(8,128)(2,1)}, bf16[2,12,64,256]{3,2,1,0:T(8,128)(2,1)S(1)}, u32[]{:S(2)}) copy-start(bf16[2,12,64,256]{3,2,1,0:T(8,128)(2,1)S(1)} %collective-permute-done.7.refs_3_) | copy-start | bytes 2359300
  138.9 61.4 %collective-permute-start.24 = (bf16[4,8,64,256]{3,2,1,0:T(8,128)(2,1)S(1)}, bf16[4,8,64,256]{3,2,1,0:T(8,128)(2,1)S(1)}, u32[]{:S(2)}, u32[]{:S(2)}) collective-permute-start(bf16[4,8,64,256]{3,2,1,0:T(8,128)(2,1)S(1)} %pad_maximum_fusion.3.refs_10_), channel_id=1, source_target_pairs={{1,17},{3,19},{5,21},{7,23},{9,25},{11,27},{13,29},{15,31},{17,1},... | collective-permute-start | bytes 3145736 | tf_op jit(solution)/shard_map/ppermute | solution.py:362
  142.5 57.7 %copy-start.6 = (bf16[2,12,64,256]{3,2,1,0:T(8,128)(2,1)}, bf16[2,12,64,256]{3,2,1,0:T(8,128)(2,1)S(1)}, u32[]{:S(2)}) copy-start(bf16[2,12,64,256]{3,2,1,0:T(8,128)(2,1)S(1)} %collective-permute-done.5.refs_2_) | copy-start | bytes 2359300
  142.5 57.8 %collective-permute-start.23 = (bf16[4,8,64,256]{3,2,1,0:T(8,128)(2,1)S(1)}, bf16[4,8,64,256]{3,2,1,0:T(8,128)(2,1)S(1)}, u32[]{:S(2)}, u32[]{:S(2)}) collective-permute-start(bf16[4,8,64,256]{3,2,1,0:T(8,128)(2,1)S(1)} %pad_maximum_fusion.3.refs_10_), channel_id=1, source_target_pairs={{1,9},{3,11},{5,13},{7,15},{9,17},{11,19},{13,21},{15,23},{17,25},... | collective-permute-start | bytes 3145736 | tf_op jit(solution)/shard_map/ppermute | solution.py:362
  143.2 57.0 %copy-start.7 = (bf16[2,12,64,256]{3,2,1,0:T(8,128)(2,1)}, bf16[2,12,64,256]{3,2,1,0:T(8,128)(2,1)S(1)}, u32[]{:S(2)}) copy-start(bf16[2,12,64,256]{3,2,1,0:T(8,128)(2,1)S(1)} %collective-permute-done.11.refs_8_) | copy-start | bytes 2359300
  143.2 57.1 %collective-permute-start.28 = (bf16[4,8,64,256]{3,2,1,0:T(8,128)(2,1)S(1)}, bf16[4,8,64,256]{3,2,1,0:T(8,128)(2,1)S(1)}, u32[]{:S(2)}, u32[]{:S(2)}) collective-permute-start(bf16[4,8,64,256]{3,2,1,0:T(8,128)(2,1)S(1)} %pad_maximum_fusion.4.refs_14_), channel_id=1, source_target_pairs={{1,97},{3,99},{5,101},{7,103},{9,105},{11,107},{13,109},{15,111},{... | collective-permute-start | bytes 3145736 | tf_op jit(solution)/shard_map/ppermute | solution.py:362
  144.0 56.3 %copy-start.8 = (bf16[2,12,64,256]{3,2,1,0:T(8,128)(2,1)}, bf16[2,12,64,256]{3,2,1,0:T(8,128)(2,1)S(1)}, u32[]{:S(2)}) copy-start(bf16[2,12,64,256]{3,2,1,0:T(8,128)(2,1)S(1)} %collective-permute-done.9.refs_7_) | copy-start | bytes 2359300
  144.0 56.3 %collective-permute-start.27 = (bf16[4,8,64,256]{3,2,1,0:T(8,128)(2,1)S(1)}, bf16[4,8,64,256]{3,2,1,0:T(8,128)(2,1)S(1)}, u32[]{:S(2)}, u32[]{:S(2)}) collective-permute-start(bf16[4,8,64,256]{3,2,1,0:T(8,128)(2,1)S(1)} %pad_maximum_fusion.4.refs_14_), channel_id=1, source_target_pairs={{1,65},{3,67},{5,69},{7,71},{9,73},{11,75},{13,77},{15,79},{17,81}... | collective-permute-start | bytes 3145736 | tf_op jit(solution)/shard_map/ppermute | solution.py:362
  144.8 55.6 %collective-permute-start.26 = (bf16[4,8,64,256]{3,2,1,0:T(8,128)(2,1)S(1)}, bf16[4,8,64,256]{3,2,1,0:T(8,128)(2,1)S(1)}, u32[]{:S(2)}, u32[]{:S(2)}) collective-permute-start(bf16[4,8,64,256]{3,2,1,0:T(8,128)(2,1)S(1)} %pad_maximum_fusion.4.refs_14_), channel_id=1, source_target_pairs={{1,33},{3,35},{5,37},{7,39},{9,41},{11,43},{13,45},{15,47},{17,49}... | collective-permute-start | bytes 3145736 | tf_op jit(solution)/shard_map/ppermute | solution.py:362
  (11 other events, 48.5 us)

commit v3 on v1

--- a/solution.py
+++ b/solution.py
@@ -413,7 +413,12 @@
     a, b = lax.optimization_barrier(first_leg(jnp.concatenate([sides, high]), jnp.concatenate([bases, low]), 0))
     fs, gs = second_leg(a, b, 0)
     far = [moved(p, across(lambda c: c ^ 1)) for p in near]
-    odd_a, odd_b = lax.optimization_barrier(first_leg(sides, bases, 1))
+    odd_a, odd_b = first_leg(sides, bases, 1)
+    seen = jnp.stack([fs[2][0, 0, :8, :128], gs[2][0, 0, :8, :128]])
+    seen = lax.ppermute(seen, AXES, [(row * 8 + col, row * 8 + col + 1) for row in range(16) for col in range(0, 8, 2)])
+    held = jnp.any(seen != seen)
+    odd_a, odd_b, held = lax.optimization_barrier((odd_a, odd_b, held))
+    odd_a, odd_b = [jnp.where(held, jnp.zeros((), p.dtype), p) for p in (odd_a, odd_b)]
     odd_fs, odd_gs = second_leg(odd_a, odd_b, 1)
     fs, gs, near, far, own_a, own_b = lax.optimization_barrier((fs, gs, near, far, odd_fs[0], odd_gs[0]))
     odd_fs, odd_gs = [own_a] + odd_fs[1:], [own_b] + odd_gs[1:]

time: 224 us -> 220 us (0.982)
  the two profiles are of different devices: /device:TPU:32 before, /device:TPU:0 now
where the time goes in v3:
time: 220 us
  waiting for transfers between devices  86.4 us (39%)
  starting transfers between devices  67.1 us (30%)
  Pallas kernels  56.9 us (26%)
  local copies, waits for them, and re-layouts  3.8 us (2%)
  other arithmetic  3.18 us (1%)
  between operations  2.23 us (1%)
    ppermute x27, waiting for transfers between devices, moved(): return lax.ppermute(value, AXES, pairs)  78.5 us
    pallas_call x1, Pallas kernels, shards(): pl.pallas_call(column_kernel, out_shape=outs, in_specs=[smem] + [hbm] * 1...  54.9 us
    ppermute x27, starting transfers between devices, moved(): return lax.ppermute(value, AXES, pairs)  53.8 us
    ppermute x1, starting transfers between devices, shards(): lax.ppermute(seen, AXES, [(row * 8 + col, row * 8 + col + 1) for row in r...  8.56 us
    all_to_all x1, waiting for transfers between devices, shards(): lax.all_to_all(col_factors, 'cols', split_axis=0, concat_axis=1, tiled=True)  7.86 us
    all_to_all x1, starting transfers between devices, shards(): lax.all_to_all(col_factors, 'cols', split_axis=0, concat_axis=1, tiled=True)  4.73 us
  transfers between devices with their start and end apart: 29, of which 11 were waited for; matrix products, arithmetic and copies ran while one was open for 2% of the time, Pallas kernels for 25%

profile of v3, /device:TPU:0, one launch (start us, length us, event | category | flops | bytes accessed | tf_op | source)
XLA Modules:
  0.0 219.6 jit_solution(5408979045968670937)
XLA Ops:
  0.7 4.7 %all-to-all-start = ((bf16[8,1,2,64,256]{4,3,2,1,0:T(8,128)(2,1)}), bf16[8,1,2,64,256]{4,3,2,1,0:T(8,128)(2,1)S(1)}, u32[]{:S(2)}, u32[]{:S(2)}) async-start(bf16[8,1,2,64,256]{4,3,2,1,0:T(8,128)(2,1)} %param.10), calls=%async_computation | async-start | bytes 1048576 | tf_op jit(solution)/shard_map/all_to_all | solution.py:403
  6.0 1.1 reshape_squeeze.7
  7.2 0.2 copy.16
  7.8 7.9 %all-to-all-done = bf16[8,1,2,64,256]{4,3,2,1,0:T(8,128)(2,1)S(1)} async-done(((bf16[8,1,2,64,256]{4,3,2,1,0:T(8,128)(2,1)}), bf16[8,1,2,64,256]{4,3,2,1,0:T(8,128)(2,1)S(1)}, u32[]{:S(2)}, u32[]{:S(2)}) %all-to-all-start) | async-done | bytes 524320 | tf_op jit(solution)/shard_map/all_to_all | solution.py:403
  15.9 3.4 %collective-permute-start = (bf16[1,12,64,256]{3,2,1,0:T(8,128)(2,1)S(1)}, bf16[1,12,64,256]{3,2,1,0:T(8,128)(2,1)S(1)}, u32[]{:S(2)}, u32[]{:S(2)}) collective-permute-start(bf16[1,12,64,256]{3,2,1,0:T(8,128)(2,1)S(1)} %maximum_bitcast_fusion), channel_id=1, source_target_pairs={{0,32},{2,34},{4,36},{6,38},{8,40},{10,42},{12,44},{14,46},{16,48}... | collective-permute-start | bytes 1179656 | tf_op jit(solution)/shard_map/ppermute | solution.py:356
  19.4 3.8 %collective-permute-start.2 = (bf16[1,12,64,256]{3,2,1,0:T(8,128)(2,1)S(1)}, bf16[1,12,64,256]{3,2,1,0:T(8,128)(2,1)S(1)}, u32[]{:S(2)}, u32[]{:S(2)}) collective-permute-start(bf16[1,12,64,256]{3,2,1,0:T(8,128)(2,1)S(1)} %maximum_bitcast_fusion.1), channel_id=1, source_target_pairs={{0,8},{2,10},{4,12},{6,14},{8,0},{10,2},{12,4},{14,6},{16,24},{18,... | collective-permute-start | bytes 1179656 | tf_op jit(solution)/shard_map/ppermute | solution.py:356
  23.2 2.4 %collective-permute-done = bf16[1,12,64,256]{3,2,1,0:T(8,128)(2,1)S(1)} collective-permute-done((bf16[1,12,64,256]{3,2,1,0:T(8,128)(2,1)S(1)}, bf16[1,12,64,256]{3,2,1,0:T(8,128)(2,1)S(1)}, u32[]{:S(2)}, u32[]{:S(2)}) %collective-permute-start) | collective-permute-done | bytes 393248 | tf_op jit(solution)/shard_map/ppermute | solution.py:356
  25.7 4.7 %collective-permute-start.1 = (bf16[2,12,64,256]{3,2,1,0:T(8,128)(2,1)S(1)}, bf16[2,12,64,256]{3,2,1,0:T(8,128)(2,1)S(1)}, u32[]{:S(2)}, u32[]{:S(2)}) collective-permute-start(bf16[2,12,64,256]{3,2,1,0:T(8,128)(2,1)S(1)} %pad_maximum_fusion.5), channel_id=1, source_target_pairs={{0,96},{2,98},{4,100},{6,102},{8,104},{10,106},{12,108},{14,110},{... | collective-permute-start | bytes 2359304 | tf_op jit(solution)/shard_map/ppermute | solution.py:356
  30.4 5.9 %collective-permute-start.3 = (bf16[2,12,64,256]{3,2,1,0:T(8,128)(2,1)S(1)}, bf16[2,12,64,256]{3,2,1,0:T(8,128)(2,1)S(1)}, u32[]{:S(2)}, u32[]{:S(2)}) collective-permute-start(bf16[2,12,64,256]{3,2,1,0:T(8,128)(2,1)S(1)} %pad_maximum_fusion.6), channel_id=1, source_target_pairs={{0,24},{2,26},{4,28},{6,30},{8,16},{10,18},{12,20},{14,22},{16,8},... | collective-permute-start | bytes 2359304 | tf_op jit(solution)/shard_map/ppermute | solution.py:356
  36.4 0.7 collective-permute-start.19
  37.1 0.7 collective-permute-start.20
  37.8 0.7 collective-permute-start.17
  38.5 2.2 %collective-permute-done.1 = bf16[2,12,64,256]{3,2,1,0:T(8,128)(2,1)S(1)} collective-permute-done((bf16[2,12,64,256]{3,2,1,0:T(8,128)(2,1)S(1)}, bf16[2,12,64,256]{3,2,1,0:T(8,128)(2,1)S(1)}, u32[]{:S(2)}, u32[]{:S(2)}) %collective-permute-start.1) | collective-permute-done | bytes 786464 | tf_op jit(solution)/shard_map/ppermute | solution.py:356
  40.9 6.9 %collective-permute-done.3 = bf16[2,12,64,256]{3,2,1,0:T(8,128)(2,1)S(1)} collective-permute-done((bf16[2,12,64,256]{3,2,1,0:T(8,128)(2,1)S(1)}, bf16[2,12,64,256]{3,2,1,0:T(8,128)(2,1)S(1)}, u32[]{:S(2)}, u32[]{:S(2)}) %collective-permute-start.3) | collective-permute-done | bytes 786464 | tf_op jit(solution)/shard_map/ppermute | solution.py:356
  48.0 3.5 %collective-permute-start.5 = (bf16[4,12,64,256]{3,2,1,0:T(8,128)(2,1)S(1)}, bf16[4,12,64,256]{3,2,1,0:T(8,128)(2,1)S(1)}, u32[]{:S(2)}, u32[]{:S(2)}) collective-permute-start(bf16[4,12,64,256]{3,2,1,0:T(8,128)(2,1)S(1)} %pad_maximum_fusion.refs_0_), channel_id=1, source_target_pairs={{0,16},{2,18},{4,20},{6,22},{8,24},{10,26},{12,28},{14,30},{16,0},... | collective-permute-start | bytes 4718600 | tf_op jit(solution)/shard_map/ppermute | solution.py:356
  51.4 5.2 %collective-permute-start.8 = (bf16[4,12,64,256]{3,2,1,0:T(8,128)(2,1)S(1)}, bf16[4,12,64,256]{3,2,1,0:T(8,128)(2,1)S(1)}, u32[]{:S(2)}, u32[]{:S(2)}) collective-permute-start(bf16[4,12,64,256]{3,2,1,0:T(8,128)(2,1)S(1)} %pad_maximum_fusion.1.refs_4_), channel_id=1, source_target_pairs={{0,64},{2,66},{4,68},{6,70},{8,72},{10,74},{12,76},{14,78},{16,80}... | collective-permute-start | bytes 4718600 | tf_op jit(solution)/shard_map/ppermute | solution.py:356
  56.7 1.2 collective-permute-start.12
  57.9 1.5 collective-permute-start.11
  59.4 15.6 %collective-permute-done.12.refs_11_.refs_19_ = bf16[2,1024,256]{2,1,0:T(8,128)(2,1)S(1)} collective-permute-done((bf16[2,1024,256]{2,1,0:T(8,128)(2,1)S(1)}, bf16[2,1024,256]{2,1,0:T(8,128)(2,1)S(1)}, u32[]{:S(2)}, u32[]{:S(2)}) %collective-permute-start.12) | collective-permute-done | bytes 1048608 | tf_op jit(solution)/shard_map/ppermute | solution.py:356
  75.0 3.7 %collective-permute-done.11.refs_10_.refs_18_ = bf16[2,1024,256]{2,1,0:T(8,128)(2,1)S(1)} collective-permute-done((bf16[2,1024,256]{2,1,0:T(8,128)(2,1)S(1)}, bf16[2,1024,256]{2,1,0:T(8,128)(2,1)S(1)}, u32[]{:S(2)}, u32[]{:S(2)}) %collective-permute-start.11) | collective-permute-done | bytes 1048608 | tf_op jit(solution)/shard_map/ppermute | solution.py:356
  78.7 11.1 %collective-permute-done.10.refs_9_.refs_17_ = bf16[2,1024,256]{2,1,0:T(8,128)(2,1)S(1)} collective-permute-done((bf16[2,1024,256]{2,1,0:T(8,128)(2,1)S(1)}, bf16[2,1024,256]{2,1,0:T(8,128)(2,1)S(1)}, u32[]{:S(2)}, u32[]{:S(2)}) %collective-permute-start.10) | collective-permute-done | bytes 1048608 | tf_op jit(solution)/shard_map/ppermute | solution.py:356
  89.9 0.7 collective-permute-start.18
  90.6 4.2 %collective-permute-start.14 = (bf16[2,1024,256]{2,1,0:T(8,128)(2,1)S(1)}, bf16[2,1024,256]{2,1,0:T(8,128)(2,1)S(1)}, u32[]{:S(2)}, u32[]{:S(2)}) collective-permute-start(bf16[2,1024,256]{2,1,0:T(8,128)(2,1)S(1)} %collective-permute-done.10.refs_9_.refs_17_), channel_id=1, source_target_pairs={{0,1},{1,0},{2,3},{3,2},{4,5},{5,4},{6,7},{7,6},{8,9},{9,8},{10,11... | collective-permute-start | bytes 3145736 | tf_op jit(solution)/shard_map/ppermute | solution.py:356
  94.8 8.6 %collective-permute-start.21 = (bf16[2,8,128]{2,1,0:T(8,128)(2,1)S(1)}, bf16[2,8,128]{2,1,0:T(8,128)(2,1)S(1)}, u32[]{:S(2)}, u32[]{:S(2)}) collective-permute-start(bf16[2,8,128]{2,1,0:T(8,128)(2,1)S(1)} %pad_maximum_fusion.9), channel_id=1, source_target_pairs={{0,1},{2,3},{4,5},{6,7},{8,9},{10,11},{12,13},{14,15},{16,17},{18,... | collective-permute-start | bytes 12296 | tf_op jit(solution)/shard_map/ppermute | solution.py:418
  103.5 2.2 %collective-permute-start.6 = (bf16[4,12,64,256]{3,2,1,0:T(8,128)(2,1)S(1)}, bf16[4,12,64,256]{3,2,1,0:T(8,128)(2,1)S(1)}, u32[]{:S(2)}, u32[]{:S(2)}) collective-permute-start(bf16[4,12,64,256]{3,2,1,0:T(8,128)(2,1)S(1)} %pad_maximum_fusion.refs_0_), channel_id=1, source_target_pairs={{0,24},{2,26},{4,28},{6,30},{8,0},{10,2},{12,4},{14,6},{16,8},{18,... | collective-permute-start | bytes 4718600 | tf_op jit(solution)/shard_map/ppermute | solution.py:356
  105.8 3.6 %collective-permute-start.4 = (bf16[4,12,64,256]{3,2,1,0:T(8,128)(2,1)S(1)}, bf16[4,12,64,256]{3,2,1,0:T(8,128)(2,1)S(1)}, u32[]{:S(2)}, u32[]{:S(2)}) collective-permute-start(bf16[4,12,64,256]{3,2,1,0:T(8,128)(2,1)S(1)} %pad_maximum_fusion.refs_0_), channel_id=1, source_target_pairs={{0,8},{2,10},{4,12},{6,14},{8,16},{10,18},{12,20},{14,22},{16,24},... | collective-permute-start | bytes 4718600 | tf_op jit(solution)/shard_map/ppermute | solution.py:356
  109.5 4.6 %collective-permute-start.9 = (bf16[4,12,64,256]{3,2,1,0:T(8,128)(2,1)S(1)}, bf16[4,12,64,256]{3,2,1,0:T(8,128)(2,1)S(1)}, u32[]{:S(2)}, u32[]{:S(2)}) collective-permute-start(bf16[4,12,64,256]{3,2,1,0:T(8,128)(2,1)S(1)} %pad_maximum_fusion.1.refs_4_), channel_id=1, source_target_pairs={{0,96},{2,98},{4,100},{6,102},{8,104},{10,106},{12,108},{14,110},{... | collective-permute-start | bytes 4718600 | tf_op jit(solution)/shard_map/ppermute | solution.py:356
  114.1 1.9 collective-permute-start.7
  116.2 0.6 compare_reduce_fusion
  116.8 0.7 broadcast_select_fusion.refs_12_
  117.5 0.7 collective-permute-start.27
  118.3 0.7 broadcast_select_fusion.1.refs_8_
  119.0 11.0 %collective-permute-done.6.refs_3_ = bf16[4,12,64,256]{3,2,1,0:T(8,128)(2,1)S(1)} collective-permute-done((bf16[4,12,64,256]{3,2,1,0:T(8,128)(2,1)S(1)}, bf16[4,12,64,256]{3,2,1,0:T(8,128)(2,1)S(1)}, u32[]{:S(2)}, u32[]{:S(2)}) %collective-permute-start.6) | collective-permute-done | bytes 1572896 | tf_op jit(solution)/shard_map/ppermute | solution.py:356
  130.1 0.7 collective-permute-start.26
  130.8 11.0 %collective-permute-done.4.refs_1_ = bf16[4,12,64,256]{3,2,1,0:T(8,128)(2,1)S(1)} collective-permute-done((bf16[4,12,64,256]{3,2,1,0:T(8,128)(2,1)S(1)}, bf16[4,12,64,256]{3,2,1,0:T(8,128)(2,1)S(1)}, u32[]{:S(2)}, u32[]{:S(2)}) %collective-permute-start.4) | collective-permute-done | bytes 1572896 | tf_op jit(solution)/shard_map/ppermute | solution.py:356
  141.8 0.7 collective-permute-start.25
  142.5 9.1 %collective-permute-done.9.refs_7_ = bf16[4,12,64,256]{3,2,1,0:T(8,128)(2,1)S(1)} collective-permute-done((bf16[4,12,64,256]{3,2,1,0:T(8,128)(2,1)S(1)}, bf16[4,12,64,256]{3,2,1,0:T(8,128)(2,1)S(1)}, u32[]{:S(2)}, u32[]{:S(2)}) %collective-permute-start.9) | collective-permute-done | bytes 1572896 | tf_op jit(solution)/shard_map/ppermute | solution.py:356
  151.7 1.6 collective-permute-start.24
  153.3 5.4 %collective-permute-done.7.refs_5_ = bf16[4,12,64,256]{3,2,1,0:T(8,128)(2,1)S(1)} collective-permute-done((bf16[4,12,64,256]{3,2,1,0:T(8,128)(2,1)S(1)}, bf16[4,12,64,256]{3,2,1,0:T(8,128)(2,1)S(1)}, u32[]{:S(2)}, u32[]{:S(2)}) %collective-permute-start.7) | collective-permute-done | bytes 1572896 | tf_op jit(solution)/shard_map/ppermute | solution.py:356
  158.7 0.7 collective-permute-start.23
  159.4 0.7 collective-permute-start.22
  160.2 0.2 copy-done.20
  160.5 54.9 %column.1 = (f32[1024,1024]{1,0:T(8,128)}, f32[64,1024]{1,0:T(8,128)}) custom-call(s32[12]{0:T(128)S(1)} %concatenate.37.meta, bf16[4,12,64,256]{3,2,1,0:T(8,128)(2,1)} %copy-done.9, bf16[4,12,64,256]{3,2,1,0:T(8,128)(2,1)} %copy-done.16, bf16[4,12,64,256]{3,2,1,0:T(8,128)(2,1)} %copy-done.13, bf16[4,12,64,256]{3,2,1,0:T(8,128)(2,1)} %copy-done.15, ...), custom_call_target="tpu_custom_call" | custom-call | flops 60000002048 | bytes 20000000 | tf_op jit(solution)/shard_map/column/pallas_call | solution.py:430
  215.5 0.9 copy-done.21
  216.4 0.3 copy-done.22
  216.7 0.4 copy-done.23
  217.1 0.3 copy-done.24
  217.4 2.0 tile.1
  (91 shorter events, 1.6 us)
Async XLA Ops:
  0.6 6.9 %copy-start = (s32[8,8]{1,0:T(8,128)S(1)}, s32[8,8]{1,0:T(8,128)}, u32[]{:S(2)}) copy-start(s32[8,8]{1,0:T(8,128)} %param.11) | copy-start | bytes 772
  0.7 15.0 %all-to-all-start = ((bf16[8,1,2,64,256]{4,3,2,1,0:T(8,128)(2,1)}), bf16[8,1,2,64,256]{4,3,2,1,0:T(8,128)(2,1)S(1)}, u32[]{:S(2)}, u32[]{:S(2)}) async-start(bf16[8,1,2,64,256]{4,3,2,1,0:T(8,128)(2,1)} %param.10), calls=%async_computation | async-start | bytes 1048576 | tf_op jit(solution)/shard_map/all_to_all | solution.py:403
  7.7 152.8 %copy-start.8 = (s32[12]{0:T(128)}, s32[12]{0:T(128)S(1)}, u32[]{:S(2)}) copy-start(s32[12]{0:T(128)S(1)} %concatenate.37.meta) | copy-start | bytes 148
  7.8 152.7 %copy-start.1 = (bf16[2,1024,256]{2,1,0:T(8,128)(2,1)}, bf16[2,1024,256]{2,1,0:T(8,128)(2,1)S(1)}, u32[]{:S(2)}) copy-start(bf16[2,1024,256]{2,1,0:T(8,128)(2,1)S(1)} %pad_maximum_fusion.2.refs_8_.refs_16_) | copy-start | bytes 3145732
  15.9 9.7 %collective-permute-start = (bf16[1,12,64,256]{3,2,1,0:T(8,128)(2,1)S(1)}, bf16[1,12,64,256]{3,2,1,0:T(8,128)(2,1)S(1)}, u32[]{:S(2)}, u32[]{:S(2)}) collective-permute-start(bf16[1,12,64,256]{3,2,1,0:T(8,128)(2,1)S(1)} %maximum_bitcast_fusion), channel_id=1, source_target_pairs={{0,32},{2,34},{4,36},{6,38},{8,40},{10,42},{12,44},{14,46},{16,48}... | collective-permute-start | bytes 1179656 | tf_op jit(solution)/shard_map/ppermute | solution.py:356
  19.4 11.0 %collective-permute-start.2 = (bf16[1,12,64,256]{3,2,1,0:T(8,128)(2,1)S(1)}, bf16[1,12,64,256]{3,2,1,0:T(8,128)(2,1)S(1)}, u32[]{:S(2)}, u32[]{:S(2)}) collective-permute-start(bf16[1,12,64,256]{3,2,1,0:T(8,128)(2,1)S(1)} %maximum_bitcast_fusion.1), channel_id=1, source_target_pairs={{0,8},{2,10},{4,12},{6,14},{8,0},{10,2},{12,4},{14,6},{16,24},{18,... | collective-permute-start | bytes 1179656 | tf_op jit(solution)/shard_map/ppermute | solution.py:356
  25.7 15.1 %collective-permute-start.1 = (bf16[2,12,64,256]{3,2,1,0:T(8,128)(2,1)S(1)}, bf16[2,12,64,256]{3,2,1,0:T(8,128)(2,1)S(1)}, u32[]{:S(2)}, u32[]{:S(2)}) collective-permute-start(bf16[2,12,64,256]{3,2,1,0:T(8,128)(2,1)S(1)} %pad_maximum_fusion.5), channel_id=1, source_target_pairs={{0,96},{2,98},{4,100},{6,102},{8,104},{10,106},{12,108},{14,110},{... | collective-permute-start | bytes 2359304 | tf_op jit(solution)/shard_map/ppermute | solution.py:356
  30.4 17.4 %collective-permute-start.3 = (bf16[2,12,64,256]{3,2,1,0:T(8,128)(2,1)S(1)}, bf16[2,12,64,256]{3,2,1,0:T(8,128)(2,1)S(1)}, u32[]{:S(2)}, u32[]{:S(2)}) collective-permute-start(bf16[2,12,64,256]{3,2,1,0:T(8,128)(2,1)S(1)} %pad_maximum_fusion.6), channel_id=1, source_target_pairs={{0,24},{2,26},{4,28},{6,30},{8,16},{10,18},{12,20},{14,22},{16,8},... | collective-permute-start | bytes 2359304 | tf_op jit(solution)/shard_map/ppermute | solution.py:356
  36.4 0.7 collective-permute-start.19
  37.1 22.3 %collective-permute-start.20 = (bf16[2,8,64,256]{3,2,1,0:T(8,128)(2,1)S(1)}, bf16[2,8,64,256]{3,2,1,0:T(8,128)(2,1)S(1)}, u32[]{:S(2)}, u32[]{:S(2)}) collective-permute-start(bf16[2,8,64,256]{3,2,1,0:T(8,128)(2,1)S(1)} %pad_maximum_fusion.8), channel_id=1, source_target_pairs={{1,25},{3,27},{5,29},{7,31},{9,17},{11,19},{13,21},{15,23},{17,9},... | collective-permute-start | bytes 1572872 | tf_op jit(solution)/shard_map/ppermute | solution.py:356
  37.8 20.1 %collective-permute-start.17 = (bf16[1,8,64,256]{3,2,1,0:T(8,128)(2,1)S(1)}, bf16[1,8,64,256]{3,2,1,0:T(8,128)(2,1)S(1)}, u32[]{:S(2)}, u32[]{:S(2)}) collective-permute-start(bf16[1,8,64,256]{3,2,1,0:T(8,128)(2,1)S(1)} %get-tuple-element.69), channel_id=1, source_target_pairs={{1,33},{3,35},{5,37},{7,39},{9,41},{11,43},{13,45},{15,47},{17,49}... | collective-permute-start | bytes 786440 | tf_op jit(solution)/shard_map/ppermute | solution.py:356
  40.9 64.9 %copy-start.9 = (bf16[4,12,64,256]{3,2,1,0:T(8,128)(2,1)}, bf16[4,12,64,256]{3,2,1,0:T(8,128)(2,1)S(1)}, u32[]{:S(2)}) copy-start(bf16[4,12,64,256]{3,2,1,0:T(8,128)(2,1)S(1)} %pad_maximum_fusion.refs_0_) | copy-start | bytes 4718596
  47.9 66.1 %copy-start.10 = (bf16[4,12,64,256]{3,2,1,0:T(8,128)(2,1)}, bf16[4,12,64,256]{3,2,1,0:T(8,128)(2,1)S(1)}, u32[]{:S(2)}) copy-start(bf16[4,12,64,256]{3,2,1,0:T(8,128)(2,1)S(1)} %pad_maximum_fusion.1.refs_4_) | copy-start | bytes 4718596
  48.0 41.9 %collective-permute-start.5 = (bf16[4,12,64,256]{3,2,1,0:T(8,128)(2,1)S(1)}, bf16[4,12,64,256]{3,2,1,0:T(8,128)(2,1)S(1)}, u32[]{:S(2)}, u32[]{:S(2)}) collective-permute-start(bf16[4,12,64,256]{3,2,1,0:T(8,128)(2,1)S(1)} %pad_maximum_fusion.refs_0_), channel_id=1, source_target_pairs={{0,16},{2,18},{4,20},{6,22},{8,24},{10,26},{12,28},{14,30},{16,0},... | collective-permute-start | bytes 4718600 | tf_op jit(solution)/shard_map/ppermute | solution.py:356
  51.4 39.1 %collective-permute-start.8 = (bf16[4,12,64,256]{3,2,1,0:T(8,128)(2,1)S(1)}, bf16[4,12,64,256]{3,2,1,0:T(8,128)(2,1)S(1)}, u32[]{:S(2)}, u32[]{:S(2)}) collective-permute-start(bf16[4,12,64,256]{3,2,1,0:T(8,128)(2,1)S(1)} %pad_maximum_fusion.1.refs_4_), channel_id=1, source_target_pairs={{0,64},{2,66},{4,68},{6,70},{8,72},{10,74},{12,76},{14,78},{16,80}... | collective-permute-start | bytes 4718600 | tf_op jit(solution)/shard_map/ppermute | solution.py:356
  56.7 18.3 %collective-permute-start.12 = (bf16[2,1024,256]{2,1,0:T(8,128)(2,1)S(1)}, bf16[2,1024,256]{2,1,0:T(8,128)(2,1)S(1)}, u32[]{:S(2)}, u32[]{:S(2)}) collective-permute-start(bf16[2,1024,256]{2,1,0:T(8,128)(2,1)S(1)} %pad_maximum_fusion.2.refs_8_.refs_16_), channel_id=1, source_target_pairs={{0,6},{1,7},{2,0},{3,1},{4,2},{5,3},{6,4},{7,5},{8,14},{9,15},{10,... | collective-permute-start | bytes 3145736 | tf_op jit(solution)/shard_map/ppermute | solution.py:356
  57.9 20.8 %collective-permute-start.11 = (bf16[2,1024,256]{2,1,0:T(8,128)(2,1)S(1)}, bf16[2,1024,256]{2,1,0:T(8,128)(2,1)S(1)}, u32[]{:S(2)}, u32[]{:S(2)}) collective-permute-start(bf16[2,1024,256]{2,1,0:T(8,128)(2,1)S(1)} %pad_maximum_fusion.2.refs_8_.refs_16_), channel_id=1, source_target_pairs={{0,4},{1,5},{2,6},{3,7},{4,0},{5,1},{6,2},{7,3},{8,12},{9,13},{10,... | collective-permute-start | bytes 3145736 | tf_op jit(solution)/shard_map/ppermute | solution.py:356
  59.4 30.4 %collective-permute-start.10 = (bf16[2,1024,256]{2,1,0:T(8,128)(2,1)S(1)}, bf16[2,1024,256]{2,1,0:T(8,128)(2,1)S(1)}, u32[]{:S(2)}, u32[]{:S(2)}) collective-permute-start(bf16[2,1024,256]{2,1,0:T(8,128)(2,1)S(1)} %pad_maximum_fusion.2.refs_8_.refs_16_), channel_id=1, source_target_pairs={{0,2},{1,3},{2,4},{3,5},{4,6},{5,7},{6,0},{7,1},{8,10},{9,11},{10,... | collective-permute-start | bytes 3145736 | tf_op jit(solution)/shard_map/ppermute | solution.py:356
  75.0 85.4 %copy-start.2 = (bf16[2,1024,256]{2,1,0:T(8,128)(2,1)}, bf16[2,1024,256]{2,1,0:T(8,128)(2,1)S(1)}, u32[]{:S(2)}) copy-start(bf16[2,1024,256]{2,1,0:T(8,128)(2,1)S(1)} %collective-permute-done.12.refs_11_.refs_19_) | copy-start | bytes 3145732
  75.0 28.5 %collective-permute-start.13 = (bf16[2,1024,256]{2,1,0:T(8,128)(2,1)S(1)}, bf16[2,1024,256]{2,1,0:T(8,128)(2,1)S(1)}, u32[]{:S(2)}, u32[]{:S(2)}) collective-permute-start(bf16[2,1024,256]{2,1,0:T(8,128)(2,1)S(1)} %pad_maximum_fusion.2.refs_8_.refs_16_), channel_id=1, source_target_pairs={{0,1},{1,0},{2,3},{3,2},{4,5},{5,4},{6,7},{7,6},{8,9},{9,8},{10,11... | collective-permute-start | bytes 3145736 | tf_op jit(solution)/shard_map/ppermute | solution.py:356
  78.7 81.7 %copy-start.3 = (bf16[2,1024,256]{2,1,0:T(8,128)(2,1)}, bf16[2,1024,256]{2,1,0:T(8,128)(2,1)S(1)}, u32[]{:S(2)}) copy-start(bf16[2,1024,256]{2,1,0:T(8,128)(2,1)S(1)} %collective-permute-done.11.refs_10_.refs_18_) | copy-start | bytes 3145732
  78.7 27.1 %collective-permute-start.16 = (bf16[2,1024,256]{2,1,0:T(8,128)(2,1)S(1)}, bf16[2,1024,256]{2,1,0:T(8,128)(2,1)S(1)}, u32[]{:S(2)}, u32[]{:S(2)}) collective-permute-start(bf16[2,1024,256]{2,1,0:T(8,128)(2,1)S(1)} %collective-permute-done.12.refs_11_.refs_19_), channel_id=1, source_target_pairs={{0,1},{1,0},{2,3},{3,2},{4,5},{5,4},{6,7},{7,6},{8,9},{9,8},{10,11... | collective-permute-start | bytes 3145736 | tf_op jit(solution)/shard_map/ppermute | solution.py:356
  89.8 70.6 %copy-start.4 = (bf16[2,1024,256]{2,1,0:T(8,128)(2,1)}, bf16[2,1024,256]{2,1,0:T(8,128)(2,1)S(1)}, u32[]{:S(2)}) copy-start(bf16[2,1024,256]{2,1,0:T(8,128)(2,1)S(1)} %collective-permute-done.10.refs_9_.refs_17_) | copy-start | bytes 3145732
  89.8 19.6 %collective-permute-start.15 = (bf16[2,1024,256]{2,1,0:T(8,128)(2,1)S(1)}, bf16[2,1024,256]{2,1,0:T(8,128)(2,1)S(1)}, u32[]{:S(2)}, u32[]{:S(2)}) collective-permute-start(bf16[2,1024,256]{2,1,0:T(8,128)(2,1)S(1)} %collective-permute-done.11.refs_10_.refs_18_), channel_id=1, source_target_pairs={{0,1},{1,0},{2,3},{3,2},{4,5},{5,4},{6,7},{7,6},{8,9},{9,8},{10,11... | collective-permute-start | bytes 3145736 | tf_op jit(solution)/shard_map/ppermute | solution.py:356
  89.9 70.6 %copy-start.13 = (bf16[4,12,64,256]{3,2,1,0:T(8,128)(2,1)}, bf16[4,12,64,256]{3,2,1,0:T(8,128)(2,1)S(1)}, u32[]{:S(2)}) copy-start(bf16[4,12,64,256]{3,2,1,0:T(8,128)(2,1)S(1)} %collective-permute-done.5.refs_2_) | copy-start | bytes 4718596
  89.9 5.0 %collective-permute-start.18 = (bf16[2,8,64,256]{3,2,1,0:T(8,128)(2,1)S(1)}, bf16[2,8,64,256]{3,2,1,0:T(8,128)(2,1)S(1)}, u32[]{:S(2)}, u32[]{:S(2)}) collective-permute-start(bf16[2,8,64,256]{3,2,1,0:T(8,128)(2,1)S(1)} %pad_maximum_fusion.7), channel_id=1, source_target_pairs={{1,97},{3,99},{5,101},{7,103},{9,105},{11,107},{13,109},{15,111},{... | collective-permute-start | bytes 1572872 | tf_op jit(solution)/shard_map/ppermute | solution.py:356
  90.6 69.9 %copy-start.14 = (bf16[4,12,64,256]{3,2,1,0:T(8,128)(2,1)}, bf16[4,12,64,256]{3,2,1,0:T(8,128)(2,1)S(1)}, u32[]{:S(2)}) copy-start(bf16[4,12,64,256]{3,2,1,0:T(8,128)(2,1)S(1)} %collective-permute-done.8.refs_6_) | copy-start | bytes 4718596
  90.6 26.9 %collective-permute-start.14 = (bf16[2,1024,256]{2,1,0:T(8,128)(2,1)S(1)}, bf16[2,1024,256]{2,1,0:T(8,128)(2,1)S(1)}, u32[]{:S(2)}, u32[]{:S(2)}) collective-permute-start(bf16[2,1024,256]{2,1,0:T(8,128)(2,1)S(1)} %collective-permute-done.10.refs_9_.refs_17_), channel_id=1, source_target_pairs={{0,1},{1,0},{2,3},{3,2},{4,5},{5,4},{6,7},{7,6},{8,9},{9,8},{10,11... | collective-permute-start | bytes 3145736 | tf_op jit(solution)/shard_map/ppermute | solution.py:356
  94.8 19.2 %collective-permute-start.21 = (bf16[2,8,128]{2,1,0:T(8,128)(2,1)S(1)}, bf16[2,8,128]{2,1,0:T(8,128)(2,1)S(1)}, u32[]{:S(2)}, u32[]{:S(2)}) collective-permute-start(bf16[2,8,128]{2,1,0:T(8,128)(2,1)S(1)} %pad_maximum_fusion.9), channel_id=1, source_target_pairs={{0,1},{2,3},{4,5},{6,7},{8,9},{10,11},{12,13},{14,15},{16,17},{18,... | collective-permute-start | bytes 12296 | tf_op jit(solution)/shard_map/ppermute | solution.py:418
  103.5 56.9 %copy-start.5 = (bf16[2,1024,256]{2,1,0:T(8,128)(2,1)}, bf16[2,1024,256]{2,1,0:T(8,128)(2,1)S(1)}, u32[]{:S(2)}) copy-start(bf16[2,1024,256]{2,1,0:T(8,128)(2,1)S(1)} %collective-permute-done.13.refs_12_.refs_20_) | copy-start | bytes 3145732
  103.5 26.5 %collective-permute-start.6 = (bf16[4,12,64,256]{3,2,1,0:T(8,128)(2,1)S(1)}, bf16[4,12,64,256]{3,2,1,0:T(8,128)(2,1)S(1)}, u32[]{:S(2)}, u32[]{:S(2)}) collective-permute-start(bf16[4,12,64,256]{3,2,1,0:T(8,128)(2,1)S(1)} %pad_maximum_fusion.refs_0_), channel_id=1, source_target_pairs={{0,24},{2,26},{4,28},{6,30},{8,0},{10,2},{12,4},{14,6},{16,8},{18,... | collective-permute-start | bytes 4718600 | tf_op jit(solution)/shard_map/ppermute | solution.py:356
  105.8 8.3 %copy-start.19 = (bf16[2,1024,256]{2,1,0:T(8,128)(2,1)}, bf16[2,1024,256]{2,1,0:T(8,128)(2,1)S(1)}, u32[]{:S(2)}) copy-start(bf16[2,1024,256]{2,1,0:T(8,128)(2,1)S(1)} %collective-permute-done.16.refs_15_.refs_23_) | copy-start | bytes 3145732
  105.8 36.0 %collective-permute-start.4 = (bf16[4,12,64,256]{3,2,1,0:T(8,128)(2,1)S(1)}, bf16[4,12,64,256]{3,2,1,0:T(8,128)(2,1)S(1)}, u32[]{:S(2)}, u32[]{:S(2)}) collective-permute-start(bf16[4,12,64,256]{3,2,1,0:T(8,128)(2,1)S(1)} %pad_maximum_fusion.refs_0_), channel_id=1, source_target_pairs={{0,8},{2,10},{4,12},{6,14},{8,16},{10,18},{12,20},{14,22},{16,24},... | collective-permute-start | bytes 4718600 | tf_op jit(solution)/shard_map/ppermute | solution.py:356
  109.4 51.0 %copy-start.6 = (bf16[2,1024,256]{2,1,0:T(8,128)(2,1)}, bf16[2,1024,256]{2,1,0:T(8,128)(2,1)S(1)}, u32[]{:S(2)}) copy-start(bf16[2,1024,256]{2,1,0:T(8,128)(2,1)S(1)} %collective-permute-done.15.refs_14_.refs_22_) | copy-start | bytes 3145732
  109.5 42.2 %collective-permute-start.9 = (bf16[4,12,64,256]{3,2,1,0:T(8,128)(2,1)S(1)}, bf16[4,12,64,256]{3,2,1,0:T(8,128)(2,1)S(1)}, u32[]{:S(2)}, u32[]{:S(2)}) collective-permute-start(bf16[4,12,64,256]{3,2,1,0:T(8,128)(2,1)S(1)} %pad_maximum_fusion.1.refs_4_), channel_id=1, source_target_pairs={{0,96},{2,98},{4,100},{6,102},{8,104},{10,106},{12,108},{14,110},{... | collective-permute-start | bytes 4718600 | tf_op jit(solution)/shard_map/ppermute | solution.py:356
  114.1 44.6 %collective-permute-start.7 = (bf16[4,12,64,256]{3,2,1,0:T(8,128)(2,1)S(1)}, bf16[4,12,64,256]{3,2,1,0:T(8,128)(2,1)S(1)}, u32[]{:S(2)}, u32[]{:S(2)}) collective-permute-start(bf16[4,12,64,256]{3,2,1,0:T(8,128)(2,1)S(1)} %pad_maximum_fusion.1.refs_4_), channel_id=1, source_target_pairs={{0,32},{2,34},{4,36},{6,38},{8,40},{10,42},{12,44},{14,46},{16,48}... | collective-permute-start | bytes 4718600 | tf_op jit(solution)/shard_map/ppermute | solution.py:356
  117.5 97.9 %copy-start.11 = (bf16[4,8,64,256]{3,2,1,0:T(8,128)(2,1)}, bf16[4,8,64,256]{3,2,1,0:T(8,128)(2,1)S(1)}, u32[]{:S(2)}) copy-start(bf16[4,8,64,256]{3,2,1,0:T(8,128)(2,1)S(1)} %broadcast_select_fusion.refs_12_) | copy-start | bytes 3145732
  117.5 97.9 %copy-start.7 = (bf16[2,1024,256]{2,1,0:T(8,128)(2,1)}, bf16[2,1024,256]{2,1,0:T(8,128)(2,1)S(1)}, u32[]{:S(2)}) copy-start(bf16[2,1024,256]{2,1,0:T(8,128)(2,1)S(1)} %collective-permute-done.14.refs_13_.refs_21_) | copy-start | bytes 3145732
  117.5 41.9 %collective-permute-start.27 = (bf16[4,8,64,256]{3,2,1,0:T(8,128)(2,1)S(1)}, bf16[4,8,64,256]{3,2,1,0:T(8,128)(2,1)S(1)}, u32[]{:S(2)}, u32[]{:S(2)}) collective-permute-start(bf16[4,8,64,256]{3,2,1,0:T(8,128)(2,1)S(1)} %broadcast_select_fusion.refs_12_), channel_id=1, source_target_pairs={{1,97},{3,99},{5,101},{7,103},{9,105},{11,107},{13,109},{15,111},{... | collective-permute-start | bytes 3145736 | tf_op jit(solution)/shard_map/ppermute | solution.py:356
  119.0 96.4 %copy-start.12 = (bf16[4,8,64,256]{3,2,1,0:T(8,128)(2,1)}, bf16[4,8,64,256]{3,2,1,0:T(8,128)(2,1)S(1)}, u32[]{:S(2)}) copy-start(bf16[4,8,64,256]{3,2,1,0:T(8,128)(2,1)S(1)} %broadcast_select_fusion.1.refs_8_) | copy-start | bytes 3145732
  130.1 30.4 %copy-start.15 = (bf16[4,12,64,256]{3,2,1,0:T(8,128)(2,1)}, bf16[4,12,64,256]{3,2,1,0:T(8,128)(2,1)S(1)}, u32[]{:S(2)}) copy-start(bf16[4,12,64,256]{3,2,1,0:T(8,128)(2,1)S(1)} %collective-permute-done.6.refs_3_) | copy-start | bytes 4718596
  130.1 85.3 %collective-permute-start.26 = (bf16[4,8,64,256]{3,2,1,0:T(8,128)(2,1)S(1)}, bf16[4,8,64,256]{3,2,1,0:T(8,128)(2,1)S(1)}, u32[]{:S(2)}, u32[]{:S(2)}) collective-permute-start(bf16[4,8,64,256]{3,2,1,0:T(8,128)(2,1)S(1)} %broadcast_select_fusion.refs_12_), channel_id=1, source_target_pairs={{1,65},{3,67},{5,69},{7,71},{9,73},{11,75},{13,77},{15,79},{17,81}... | collective-permute-start | bytes 3145736 | tf_op jit(solution)/shard_map/ppermute | solution.py:356
  141.8 17.6 %copy-start.16 = (bf16[4,12,64,256]{3,2,1,0:T(8,128)(2,1)}, bf16[4,12,64,256]{3,2,1,0:T(8,128)(2,1)S(1)}, u32[]{:S(2)}) copy-start(bf16[4,12,64,256]{3,2,1,0:T(8,128)(2,1)S(1)} %collective-permute-done.4.refs_1_) | copy-start | bytes 4718596
  141.8 73.6 %collective-permute-start.25 = (bf16[4,8,64,256]{3,2,1,0:T(8,128)(2,1)S(1)}, bf16[4,8,64,256]{3,2,1,0:T(8,128)(2,1)S(1)}, u32[]{:S(2)}, u32[]{:S(2)}) collective-permute-start(bf16[4,8,64,256]{3,2,1,0:T(8,128)(2,1)S(1)} %broadcast_select_fusion.refs_12_), channel_id=1, source_target_pairs={{1,33},{3,35},{5,37},{7,39},{9,41},{11,43},{13,45},{15,47},{17,49}... | collective-permute-start | bytes 3145736 | tf_op jit(solution)/shard_map/ppermute | solution.py:356
  151.7 8.5 %copy-start.17 = (bf16[4,12,64,256]{3,2,1,0:T(8,128)(2,1)}, bf16[4,12,64,256]{3,2,1,0:T(8,128)(2,1)S(1)}, u32[]{:S(2)}) copy-start(bf16[4,12,64,256]{3,2,1,0:T(8,128)(2,1)S(1)} %collective-permute-done.9.refs_7_) | copy-start | bytes 4718596
  151.7 63.8 %collective-permute-start.24 = (bf16[4,8,64,256]{3,2,1,0:T(8,128)(2,1)S(1)}, bf16[4,8,64,256]{3,2,1,0:T(8,128)(2,1)}, u32[]{:S(2)}, u32[]{:S(2)}) collective-permute-start(bf16[4,8,64,256]{3,2,1,0:T(8,128)(2,1)S(1)} %broadcast_select_fusion.1.refs_8_), channel_id=1, source_target_pairs={{1,25},{3,27},{5,29},{7,31},{9,1},{11,3},{13,5},{15,7},{17,9},{19,... | collective-permute-start | bytes 3145736 | tf_op jit(solution)/shard_map/ppermute | solution.py:356
  158.7 56.8 %collective-permute-start.23 = (bf16[4,8,64,256]{3,2,1,0:T(8,128)(2,1)S(1)}, bf16[4,8,64,256]{3,2,1,0:T(8,128)(2,1)S(1)}, u32[]{:S(2)}, u32[]{:S(2)}) collective-permute-start(bf16[4,8,64,256]{3,2,1,0:T(8,128)(2,1)S(1)} %broadcast_select_fusion.1.refs_8_), channel_id=1, source_target_pairs={{1,17},{3,19},{5,21},{7,23},{9,25},{11,27},{13,29},{15,31},{17,1},... | collective-permute-start | bytes 3145736 | tf_op jit(solution)/shard_map/ppermute | solution.py:356
  159.4 56.0 %collective-permute-start.22 = (bf16[4,8,64,256]{3,2,1,0:T(8,128)(2,1)S(1)}, bf16[4,8,64,256]{3,2,1,0:T(8,128)(2,1)S(1)}, u32[]{:S(2)}, u32[]{:S(2)}) collective-permute-start(bf16[4,8,64,256]{3,2,1,0:T(8,128)(2,1)S(1)} %broadcast_select_fusion.1.refs_8_), channel_id=1, source_target_pairs={{1,9},{3,11},{5,13},{7,15},{9,17},{11,19},{13,21},{15,23},{17,25},... | collective-permute-start | bytes 3145736 | tf_op jit(solution)/shard_map/ppermute | solution.py:356
  (7 other events, 13.9 us)
